TPU v7x, 32 devices: a whole 2x2x4 slice. The times are simulated.
32 devices in a mesh: dp: 4 (over z), row: 4 (over x, core), col: 2 (over y).
Axes of the slice: x: 2, y: 2, z: 4, core: 2. Of those that a mesh axis runs over, the one named last changes fastest.
Arguments:
- inputs: float32 [768, 16384], P('row', ('dp', 'col')), may hold values from -6 to 6
- teacher: float32 [768, 16384], P('row', ('dp', 'col')), may hold values from -6 to 6
- lengths: int32 [8], P('dp'), may hold values from 1024 to 2048, as said below
- omega: bfloat16 [12, 64, 256], P('col'), may hold values from -4 to 4
- w_query: float32 [768, 768], P('row', 'col'), may hold values from -0.21875 to 0.21875
- b_query: float32 [768], P('col'), may hold values from -1.5 to 1.5
- w_key: float32 [768, 768], P('row', 'col'), may hold values from -0.21875 to 0.21875
- b_key: float32 [768], P('col'), may hold values from -1.5 to 1.5
- w_value: float32 [768, 768], P('row', 'col'), may hold values from -0.21875 to 0.21875
- b_value: float32 [768], P('col'), may hold values from -1.5 to 1.5
- w_out: float32 [768, 768], P('row', 'col'), may hold values from -0.875 to 0.875
- b_out: float32 [768], P('row'), may hold values from -1.5 to 1.5
- norm1_gain: float32 [768], P('row'), may hold values from 0.5 to 1.5
- norm1_bias: float32 [768], P('row'), may hold values from -1.5 to 1.5
- w_up: float32 [768, 3072], P('row', 'col'), may hold values from -0.21875 to 0.21875
- up_bias: float32 [3072], P('col'), may hold values from -1.5 to 1.5
- w_down: float32 [768, 3072], P('row', 'col'), may hold values from -0.109375 to 0.109375
- b_down: float32 [768], P('row'), may hold values from -1.5 to 1.5
- norm2_gain: float32 [768], P('row'), may hold values from 0.5 to 1.5
- norm2_bias: float32 [768], P('row'), may hold values from -1.5 to 1.5
Outputs:
- output: float32 [768, 16384], P('row', ('dp', 'col'))
- loss: float32 [], replicated
- grad_input: float32 [768, 16384], P('row', ('dp', 'col'))
- grad_w_query: float32 [768, 768], P('row', 'col')
- grad_b_query: float32 [768], P('col')
- grad_w_key: float32 [768, 768], P('row', 'col')
- grad_b_key: float32 [768], P('col')
- grad_w_value: float32 [768, 768], P('row', 'col')
- grad_b_value: float32 [768], P('col')
- grad_w_out: float32 [768, 768], P('row', 'col')
- grad_b_out: float32 [768], P('row')
- grad_norm1_gain: float32 [768], P('row')
- grad_norm1_bias: float32 [768], P('row')
- grad_w_up: float32 [768, 3072], P('row', 'col')
- grad_b_up: float32 [3072], P('col')
- grad_w_down: float32 [768, 3072], P('row', 'col')
- grad_b_down: float32 [768], P('row')
- grad_norm2_gain: float32 [768], P('row')
- grad_norm2_bias: float32 [768], P('row')
Inputs may be any that keep to these rules, and one draw needn't show every extreme that they name: `lengths`: every draw has a sequence with all 2048 tokens valid and one with 1024.
All inputs are finite; a program needn't handle non-finite values.
Results may differ from a plain program's by a relative error of at most 0.025.
Values may be sent and summed in bfloat16 or wider, within the bound.
No kernel may reach another device: no remote copies, remote signals or barrier semaphores. Data moves between devices by JAX's collectives and lax.ppermute only.
A program may use at most 256 MiB of HBM per device.

v0:
```python
import jax
import jax.numpy as jnp
from jax import lax
from jax.experimental import pallas as pl
from jax.experimental.pallas import tpu as pltpu
from jax.sharding import PartitionSpec as P

LOSS_SCALE = 16777216
stabilizer = 2.0
norm_eps = 1e-12
root_half = 0.7071067811865476
inv_root_two_pi = 0.3989422804014327
f32 = jnp.float32
bf16 = jnp.bfloat16
PAD = 8
EXTRA = 16
CUT = 48
ASIDE = 256


def dot(a, b, dims):
    return lax.dot_general(a, b, (dims, ((), ())), preferred_element_type=f32)


def nn(a, b):
    return dot(a, b, ((1,), (0,)))


def nt(a, b):
    return dot(a, b, ((1,), (1,)))


def tn(a, b):
    return dot(a, b, ((0,), (0,)))


def ones_rows(tokens):
    return jnp.ones((8, tokens), bf16)


def call(body, outs, args, name, grid=None, in_specs=None, out_specs=None, scratch=(), limit=40, pinned=False):
    if grid is None:
        grid = (1,)
        in_specs = [single(a.shape) for a in args] if in_specs is None else in_specs
        out_specs = [single(s) for s, _ in outs]
    extra = dict(grid=grid, in_specs=in_specs, out_specs=out_specs)
    if pinned:
        args = [a if p is SMEM else pltpu.with_memory_space_constraint(a, pltpu.HBM) for a, p in zip(args, in_specs)]
    make = pltpu.HBM if pinned else jax.ShapeDtypeStruct
    return pl.pallas_call(
        body,
        out_shape=[make(s, d) for s, d in outs],
        scratch_shapes=list(scratch),
        compiler_params=pltpu.CompilerParams(vmem_limit_bytes=limit * 1024 * 1024),
        cost_estimate=pl.CostEstimate(flops=1000, bytes_accessed=1000, transcendentals=0),
        name=name,
        **extra,
    )(*args)


def single(shape):
    zeros = (0,) * len(shape)
    return pl.BlockSpec(shape, lambda s: zeros, pipeline_mode=pl.Buffered(1))


def whole(a):
    zeros = (0,) * a.ndim
    return pl.BlockSpec(a.shape, lambda s: zeros)


def whole_out(shape):
    zeros = (0,) * len(shape)
    return pl.BlockSpec(shape, lambda s: zeros)


SMEM = pl.BlockSpec(memory_space=pltpu.SMEM)


def split_positions(shard, row, row_parts):
    k, length = shard.shape
    n = length // row_parts

    def body(row_ref, in_ref, *out_refs):
        r = row_ref[0]
        for j, o_ref in enumerate(out_refs):
            at = pl.multiple_of(jnp.bitwise_xor(r, j) * n, n)
            o_ref[...] = in_ref[:, pl.ds(at, n)].astype(bf16)

    return call(body, [((k, n), bf16)] * row_parts, (row, shard), "split_positions", in_specs=[SMEM, single(shard.shape)], pinned=True)


def join_positions(blocks, row):
    k, n = blocks[0].shape
    parts = len(blocks)

    def body(row_ref, *refs):
        r = row_ref[0]
        o_ref = refs[parts]
        for j in range(parts):
            at = pl.multiple_of(jnp.bitwise_xor(r, j) * n, n)
            o_ref[:, pl.ds(at, n)] = refs[j][...].astype(f32)

    return call(body, [((k, n * parts), f32)], (row, *blocks), "join_positions", in_specs=[SMEM] + [single(b.shape) for b in blocks])[0]


def narrow(parts, steps, name):
    n = parts[0].shape[0]
    widths = [p.shape[1] for p in parts]

    def body(*refs):
        at = 0
        for ref, w in zip(refs, widths):
            refs[-1][:, at : at + w] = ref[...].astype(bf16)
            at += w

    return call(
        body, [((n, sum(widths)), bf16)], parts, name, (steps,),
        [pl.BlockSpec((n // steps, w), lambda s: (s, 0)) for w in widths],
        [pl.BlockSpec((n // steps, sum(widths)), lambda s: (s, 0))],
        pinned=True,
    )[0]


def narrow_small(parts, vecs, biases, up_bias, name):
    n, hb = parts[0].shape
    width = hb * len(parts)
    nv = len(vecs)
    rest = up_bias.shape[0] - width
    small = [v.reshape(1, v.shape[0]) for v in vecs] + [jnp.concatenate((*biases, up_bias)).reshape(-1, hb)]

    def body(*refs):
        p_refs = refs[: len(parts)]
        v_refs = refs[len(parts) : len(parts) + nv]
        b_ref, o_ref, small_ref = refs[len(parts) + nv :]
        small_ref[...] = jnp.zeros(small_ref.shape, f32)
        for m, ref in enumerate(v_refs):
            small_ref[m : m + 1, :n] = ref[...]
        for m, ref in enumerate(p_refs):
            o_ref[:n, m * hb : (m + 1) * hb] = ref[...].astype(bf16)
            small_ref[nv : nv + 1, m * hb : (m + 1) * hb] = b_ref[m : m + 1]
            small_ref[nv + 1 : nv + 2, m * hb : (m + 1) * hb] = b_ref[len(parts) + m : len(parts) + m + 1]
        small_ref[0:1, ASIDE : ASIDE + rest] = b_ref[2 * len(parts) : 2 * len(parts) + 1]
        value = small_ref[...]
        high = value.astype(bf16).astype(f32)
        o_ref[n:] = jnp.concatenate((high, value - high), axis=0).astype(bf16)

    scratch = [pltpu.VMEM((8, width), f32)]
    return call(body, [((n + EXTRA, width), bf16)], (*parts, *small), name, scratch=scratch, pinned=True)[0]


def small_rows(ref, k):
    v = ref[k : k + EXTRA].astype(f32)
    return v[0:8] + v[8:16]


def attention_in(xs, near, other, omegas, keep, head_local, head_width, hid_local):
    k, tokens = xs[0].shape
    feats = omegas[0].shape[2]
    heads = 2 * head_local
    hb = head_local * head_width
    rows = head_width + PAD
    factor = head_width ** (-0.25)
    n_near, n_other = len(near), len(other)

    def body(*refs):
        x_in = refs[:4]
        near_refs = refs[4 : 4 + n_near]
        other_refs = refs[4 + n_near : 4 + n_near + n_other]
        (om0_ref, om1_ref, keep_ref, x_ref, fq_ref, fk_ref, uq_ref, uk_ref, v_ref, kv_ref, vec_ref, up_ref) = refs[
            4 + n_near + n_other :
        ]
        for p in range(4):
            vec_ref[:, p * k : (p + 1) * k] = small_rows(near_refs[p], k)[:, :k]
        up_ref[...] = jnp.zeros(up_ref.shape, f32)
        for p in range(4):
            x_ref[p * k : (p + 1) * k] = x_in[p][...]
        xv = x_ref[...]
        ones = jnp.ones((PAD, tokens), bf16)
        for i, pieces in enumerate((near_refs, other_refs)):
            omega_ref = (om0_ref, om1_ref)[i]
            small = small_rows(pieces[0], k)
            up_ref[i : i + 1, : 3 * hb] = small[7:8]
            up_ref[i : i + 1, 3 * hb :] = small[0:1, ASIDE : ASIDE + hid_local - 3 * hb]
            triple = tn(jnp.concatenate([p[:k] for p in pieces], axis=0), xv) + jnp.transpose(small)[:, 6:7]
            for hl in range(head_local):
                h = i * head_local + hl
                at = h * head_width
                lo = hl * head_width
                value = triple[2 * hb + lo : 2 * hb + lo + head_width].astype(bf16)
                v_ref[at : at + head_width] = value
                for base, u_ref, f_ref, mask in ((0, uq_ref, fq_ref, False), (hb, uk_ref, fk_ref, True)):
                    u = triple[base + lo : base + lo + head_width] * factor
                    ub = u.astype(bf16)
                    u_ref[at : at + head_width] = ub
                    z = tn(omega_ref[hl], ub)
                    feat = jnp.exp(z - (0.5 * jnp.sum(u * u, axis=0, keepdims=True) + stabilizer))
                    if mask:
                        feat = feat * keep_ref[0:1]
                    feat = feat.astype(bf16)
                    f_ref[h * feats : (h + 1) * feats] = feat
                kv_ref[h * rows : (h + 1) * rows] = nt(jnp.concatenate((value, ones), axis=0), feat).astype(bf16)

    n = heads * head_width
    outs = [((4 * k, tokens), bf16)] + [((heads * feats, tokens), bf16)] * 2 + [((n, tokens), bf16)] * 3
    outs += [((heads * rows, feats), bf16), ((8, 4 * k), f32), ((8, hid_local), f32)]
    return call(body, outs, (*xs, *near, *other, *omegas, keep), "attention_in", pinned=True)


def weight_specs(pieces, block, first):
    return [pl.BlockSpec((p.shape[0], block), lambda s, f=first: (0, f + s)) for p in pieces]


def fixed_specs(pieces, block, at):
    return [pl.BlockSpec((p.shape[0], block), lambda s: (0, at)) for p in pieces]


def rows_of(refs):
    return jnp.concatenate([r[...] for r in refs], axis=0)


def middle(kv0, kv1, fq, x, near, other, vecs, up_bias, target, keep, scale, heads, head_width, hid_local):
    width, tokens = x.shape
    feats = kv0.shape[1]
    rows = head_width + PAD
    hb = heads * head_width // 2
    steps = hid_local // hb
    k = width // 4
    nn_, no = len(near), len(other)
    np_ = nn_ + no

    def body(*refs):
        kv0_ref, kv1_ref, fq_ref, x_ref = refs[:4]
        out_w = refs[4 : 4 + np_]
        up_w = refs[4 + np_ : 4 + 2 * np_]
        down_w = refs[4 + 2 * np_ : 4 + 3 * np_]
        (vec_ref, upb_ref, t0, t1, t2, t3, keep_ref, scale_ref,
         kv_ref, att_ref, inv_ref, xh1_ref, r1_ref, x1_ref, hid_ref, slope_ref, gf_ref, sum_ref,
         o0, o1, o2, o3, acc_ref, vec_s) = refs[4 + 3 * np_ :]
        step = pl.program_id(0)

        @pl.when(step == 0)
        def _():
            vec = jnp.transpose(vec_ref[...])
            vec_s[...] = vec
            kv_ref[...] = (kv0_ref[...].astype(f32) + kv1_ref[...].astype(f32)).astype(bf16)
            for h in range(heads):
                both = nn(kv_ref[h * rows : (h + 1) * rows], fq_ref[h * feats : (h + 1) * feats])
                inverse = 1.0 / both[head_width : head_width + 1]
                inv_ref[h : h + 1] = inverse
                att_ref[h * head_width : (h + 1) * head_width] = (both[:head_width] * inverse).astype(bf16)
            w = jnp.concatenate((rows_of(out_w[:nn_]), rows_of(out_w[nn_:])), axis=1)
            h1 = nn(w, att_ref[...]) + x_ref[...].astype(f32) + vec[:, 0:1]
            mean = jnp.sum(h1, axis=0, keepdims=True) * (1.0 / width)
            h1 = h1 - mean
            r1 = lax.rsqrt(jnp.sum(h1 * h1, axis=0, keepdims=True) * (1.0 / width) + norm_eps)
            h1 = h1 * r1
            r1_ref[...] = jnp.broadcast_to(r1, (8, tokens))
            xh1_ref[...] = h1.astype(bf16)
            x1 = h1 * vec[:, 1:2] + vec[:, 2:3]
            x1_ref[...] = x1.astype(bf16)
            acc_ref[...] = x1 + vec[:, 3:4]

        x1b = x1_ref[...]
        bias = jnp.transpose(upb_ref[...])
        total = acc_ref[...]
        for i, (a, b) in enumerate(((0, nn_), (nn_, np_))):
            up = tn(rows_of(up_w[a:b]), x1b) + bias[:, i : i + 1]
            gate = 0.5 * (1.0 + lax.erf(up * root_half))
            slope_ref[i] = (gate + up * inv_root_two_pi * jnp.exp(-0.5 * up * up)).astype(bf16)
            hid = (up * gate).astype(bf16)
            hid_ref[i] = hid
            total = total + nn(rows_of(down_w[a:b]), hid)
        acc_ref[...] = total

        @pl.when(step == steps - 1)
        def _():
            vec = vec_s[...]
            h2 = acc_ref[...]
            mean = jnp.sum(h2, axis=0, keepdims=True) * (1.0 / width)
            h2 = h2 - mean
            r2 = lax.rsqrt(jnp.sum(h2 * h2, axis=0, keepdims=True) * (1.0 / width) + norm_eps)
            h2 = h2 * r2
            out = h2 * vec[:, 4:5] + vec[:, 5:6]
            for p, o_ref in enumerate((o0, o1, o2, o3)):
                o_ref[...] = out[p * k : (p + 1) * k].astype(bf16)
            target = jnp.concatenate((t0[...], t1[...], t2[...], t3[...]), axis=0).astype(f32)
            diff = (out - target) * keep_ref[0:1]
            g = diff * scale_ref[0:1, 0:1]
            ones = ones_rows(tokens)
            sum_ref[0:8] = nt(ones, (g * h2).astype(bf16))
            sum_ref[8:16] = nt(ones, g.astype(bf16))
            sum_ref[16:24] = jnp.full((8, width), jnp.sum(diff * diff), f32)
            a = g * vec[:, 4:5]
            first = jnp.sum(a, axis=0, keepdims=True) * (1.0 / width)
            second = jnp.sum(a * h2, axis=0, keepdims=True) * (1.0 / width)
            gf_ref[...] = (r2 * (a - first - h2 * second)).astype(bf16)

    outs = [
        ((heads * rows, feats), bf16), ((width, tokens), bf16), ((16, tokens), f32), ((width, tokens), bf16),
        ((8, tokens), f32), ((width, tokens), bf16), ((2, hid_local, tokens), bf16), ((2, hid_local, tokens), bf16),
        ((width, tokens), bf16), ((24, width), f32),
    ] + [((k, tokens), bf16)] * 4
    pieces = (*near, *other)
    args = (kv0, kv1, fq, x, *pieces, *pieces, *pieces, vecs, up_bias, *target, keep, scale)
    in_specs = [whole(a) for a in (kv0, kv1, fq, x)]
    in_specs += fixed_specs(pieces, hb, 0) + weight_specs(pieces, hb, 1) + weight_specs(pieces, hb, 1 + steps)
    in_specs += [whole(vecs), pl.BlockSpec((8, hb), lambda s: (0, s))] + [whole(t) for t in target] + [whole(keep), whole(scale)]
    out_specs = [whole_out(s) for s, _ in outs]
    out_specs[6] = out_specs[7] = pl.BlockSpec((2, hb, tokens), lambda s: (0, s, 0))
    scratch = [pltpu.VMEM((width, tokens), f32), pltpu.VMEM((width, 8), f32)]
    return call(body, outs, args, "middle", (steps,), in_specs, out_specs, scratch, limit=56, pinned=True)


def grad_theirs(left, right, block, name):
    n, tokens = left.shape
    k = right.shape[1]
    half = n // 2

    def body(l_ref, r_ref, o_ref):
        for i in range(2):
            o_ref[i] = nt(l_ref[...], r_ref[i]).astype(bf16)

    return call(
        body, [((2, half, k), bf16)], (left, right), name, (k // block,),
        [pl.BlockSpec((half, tokens), lambda s: (1, 0)), pl.BlockSpec((2, block, tokens), lambda s: (0, s, 0))],
        [pl.BlockSpec((2, half, block), lambda s: (0, 0, s))],
    )[0]


def grad_mine(left, right, got, block, name):
    n, tokens = left.shape
    k = right.shape[1]
    half = n // 2
    share = k // block // 2

    def body(l_ref, r_ref, got_ref, keep0, keep1, send0, send1):
        step = pl.program_id(0)

        def part(keep_ref, send_ref):
            for i, o_ref in enumerate((keep_ref, send_ref)):
                o_ref[...] = (nt(l_ref[...], r_ref[i]) + got_ref[i].astype(f32)).astype(bf16)

        pl.when(step < share)(lambda: part(keep0, send0))
        pl.when(step >= share)(lambda: part(keep1, send1))

    first = pl.BlockSpec((half, block), lambda s: (0, jnp.minimum(s, share - 1)))
    second = pl.BlockSpec((half, block), lambda s: (0, jnp.maximum(s - share, 0)))
    return call(
        body, [((half, k // 2), bf16)] * 4, (left, right, got), name, (2 * share,),
        [
            pl.BlockSpec((half, tokens), lambda s: (0, 0)),
            pl.BlockSpec((2, block, tokens), lambda s: (0, s, 0)),
            pl.BlockSpec((2, half, block), lambda s: (0, 0, s)),
        ],
        [first, second, first, second],
    )


def pair_theirs(x, gq, go, att, name):
    n, tokens = x.shape
    half = n // 2
    k = gq.shape[1]

    def body(x_ref, gq_ref, go_ref, att_ref, o_ref):
        for i in range(2):
            o_ref[i, :, :k] = nt(x_ref[half:], gq_ref[i]).astype(bf16)
            o_ref[i, :, k:] = nt(go_ref[half:], att_ref[i]).astype(bf16)

    return call(body, [((2, half, 2 * k), bf16)], (x, gq, go, att), name)[0]


def pair_mine(x, gq, go, att, got, name):
    n, tokens = x.shape
    half = n // 2
    k = gq.shape[1]

    def body(x_ref, gq_ref, go_ref, att_ref, got_ref, keep_ref, send_ref):
        for i, o_ref in enumerate((keep_ref, send_ref)):
            o_ref[:, :k] = (nt(x_ref[:half], gq_ref[i]) + got_ref[i, :, :k].astype(f32)).astype(bf16)
            o_ref[:, k:] = (nt(go_ref[:half], att_ref[i]) + got_ref[i, :, k:].astype(f32)).astype(bf16)

    return call(body, [((half, 2 * k), bf16)] * 2, (x, gq, go, att, got), name)


def down_back(gf, slope, near, other, hb, hid_local):
    width, tokens = gf.shape
    steps = hid_local // hb
    nn_, no = len(near), len(other)
    pieces = (*near, *other)

    def body(gf_ref, slope_ref, *refs):
        gu_ref, sum_ref, bd_ref = refs[nn_ + no :]
        g = gf_ref[...]
        ones = ones_rows(tokens)

        @pl.when(pl.program_id(0) == 0)
        def _():
            bd_ref[...] = nt(ones, g)

        for i, w in enumerate((refs[:nn_], refs[nn_ : nn_ + no])):
            v = (tn(rows_of(w), g) * slope_ref[i].astype(f32)).astype(bf16)
            gu_ref[i] = v
            sum_ref[i] = nt(ones, v)

    spec = pl.BlockSpec((2, hb, tokens), lambda s: (0, s, 0))
    return call(
        body, [((2, hid_local, tokens), bf16), ((2, 8, hid_local), f32), ((8, width), f32)], (gf, slope, *pieces), "down_back",
        (steps,), [whole(gf), spec] + weight_specs(pieces, hb, 1 + steps),
        [spec, pl.BlockSpec((2, 8, hb), lambda s: (0, 0, s)), whole_out((8, width))],
    )


def up_back(gu, gf, xh1, r1, vecs, near, other, hb):
    width, tokens = gf.shape
    steps = gu.shape[1] // hb
    nn_, no = len(near), len(other)
    pieces = (*near, *other)

    def body(gu_ref, gf_ref, xh_ref, r1_ref, vec_ref, *refs):
        go_ref, sum_ref, acc_ref = refs[nn_ + no :]
        step = pl.program_id(0)

        @pl.when(step == 0)
        def _():
            acc_ref[...] = gf_ref[...].astype(f32)

        acc_ref[...] += nn(rows_of(refs[:nn_]), gu_ref[0]) + nn(rows_of(refs[nn_ : nn_ + no]), gu_ref[1])

        @pl.when(step == steps - 1)
        def _():
            vec = jnp.transpose(vec_ref[...])
            g = acc_ref[...]
            xh = xh_ref[...].astype(f32)
            ones = ones_rows(tokens)
            sum_ref[0:8] = nt(ones, (g * xh).astype(bf16))
            sum_ref[8:16] = nt(ones, g.astype(bf16))
            a = g * vec[:, 1:2]
            first = jnp.sum(a, axis=0, keepdims=True) * (1.0 / width)
            second = jnp.sum(a * xh, axis=0, keepdims=True) * (1.0 / width)
            go = (r1_ref[0:1] * (a - first - xh * second)).astype(bf16)
            go_ref[...] = go
            sum_ref[16:24] = nt(ones, go)

    return call(
        body, [((width, tokens), bf16), ((24, width), f32)], (gu, gf, xh1, r1, vecs, *pieces), "up_back", (steps,),
        [pl.BlockSpec((2, hb, tokens), lambda s: (0, s, 0))] + [whole(a) for a in (gf, xh1, r1, vecs)] + weight_specs(pieces, hb, 1),
        [whole_out((width, tokens)), whole_out((24, width))], [pltpu.VMEM((width, tokens), f32)],
    )


def attention_mid(go, att, inv, fq, near, other, heads, head_width):
    width, tokens = go.shape
    feats = fq.shape[0] // heads
    hb = heads * head_width // 2
    rows = head_width + PAD
    nn_, no = len(near), len(other)
    pieces = (*near, *other)

    def body(go_ref, att_ref, inv_ref, fq_ref, *refs):
        gn_ref, kv_ref = refs[nn_ + no :]
        g = go_ref[...]
        zeros = jnp.zeros((PAD - 1, tokens), f32)
        for i, w in enumerate((refs[:nn_], refs[nn_ : nn_ + no])):
            ga = tn(rows_of(w), g)
            for hl in range(heads // 2):
                h = i * (heads // 2) + hl
                gh = ga[hl * head_width : (hl + 1) * head_width]
                inverse = inv_ref[h : h + 1]
                a = att_ref[h * head_width : (h + 1) * head_width].astype(f32)
                gd = -jnp.sum(gh * a, axis=0, keepdims=True) * inverse
                both = jnp.concatenate((gh * inverse, gd, zeros), axis=0).astype(bf16)
                gn_ref[h * rows : (h + 1) * rows] = both
                kv_ref[h * rows : (h + 1) * rows] = nt(both, fq_ref[h * feats : (h + 1) * feats]).astype(bf16)

    outs = [((heads * rows, tokens), bf16), ((heads * rows, feats), bf16)]
    args = (go, att, inv, fq, *pieces)
    return call(
        body, outs, args, "attention_mid", (1,), [whole(a) for a in args[:4]] + fixed_specs(pieces, hb, 0),
        [whole_out(s) for s, _ in outs],
    )


def query_back(gn, kv, fq, uq, omegas, heads, head_width):
    n, tokens = uq.shape
    feats = fq.shape[0] // heads
    rows = head_width + PAD
    factor = head_width ** (-0.25)

    def body(gn_ref, kv_ref, fq_ref, uq_ref, om0_ref, om1_ref, gq_ref, sum_ref):
        for h in range(heads):
            om_ref = (om0_ref, om1_ref)[h // (heads // 2)]
            e = tn(kv_ref[h * rows : (h + 1) * rows], gn_ref[h * rows : (h + 1) * rows])
            e = e * fq_ref[h * feats : (h + 1) * feats].astype(f32)
            s = jnp.sum(e, axis=0, keepdims=True)
            u = uq_ref[h * head_width : (h + 1) * head_width].astype(f32)
            gq_ref[h * head_width : (h + 1) * head_width] = (
                factor * (nn(om_ref[h % (heads // 2)], e.astype(bf16)) - s * u)
            ).astype(bf16)
        sum_ref[...] = nt(ones_rows(tokens), gq_ref[...])

    return call(body, [((n, tokens), bf16), ((8, n), f32)], (gn, kv, fq, uq, *omegas), "query_back")


def key_back(gkv0, gkv1, fk, uk, v, omegas, heads, head_width):
    n, tokens = uk.shape
    feats = fk.shape[0] // heads
    rows = head_width + PAD
    factor = head_width ** (-0.25)
    hl_n = heads // 2
    hb = hl_n * head_width

    def body(gkv0_ref, gkv1_ref, fk_ref, uk_ref, v_ref, om0_ref, om1_ref, g_ref, sum_ref):
        ones = jnp.ones((PAD, tokens), bf16)
        for h in range(heads):
            i, hl = divmod(h, hl_n)
            base = i * 2 * hb + hl * head_width
            kv = (gkv0_ref[h * rows : (h + 1) * rows].astype(f32) + gkv1_ref[h * rows : (h + 1) * rows].astype(f32)).astype(bf16)
            f = fk_ref[h * feats : (h + 1) * feats]
            at = h * head_width
            value = jnp.concatenate((v_ref[at : at + head_width], ones), axis=0)
            e = tn(kv, value) * f.astype(f32)
            s = jnp.sum(e, axis=0, keepdims=True)
            u = uk_ref[at : at + head_width].astype(f32)
            g_ref[base : base + head_width] = (
                factor * (nn((om0_ref, om1_ref)[i][hl], e.astype(bf16)) - s * u)
            ).astype(bf16)
            g_ref[base + hb : base + hb + head_width] = nn(kv[:head_width], f).astype(bf16)
        sum_ref[...] = nt(ones_rows(tokens), g_ref[...])

    return call(body, [((2 * n, tokens), bf16), ((8, 2 * n), f32)], (gkv0, gkv1, fk, uk, v, *omegas), "key_back")


def last_parts(x, g, sums, got, name):
    sum1, sum2, bd, bu, sum_q, sum_kv = sums
    n, tokens = x.shape
    q = n // 4
    k = g.shape[1]
    hb = k // 2
    hid_local = bu.shape[2]
    ups = hid_local // hb
    rows = q + EXTRA
    which = 0 if got is not None else 1

    def body(x_ref, g_ref, s1_ref, s2_ref, bd_ref, bu_ref, sq_ref, skv_ref, *refs):
        if got is None:
            o_ref, row_s, col_s = refs
        else:
            got_ref, keep_ref, send_ref, row_s, col_s = refs
        for m, v in enumerate((s1_ref[16:17], s1_ref[0:1], s1_ref[8:9], bd_ref[0:1], s2_ref[0:1], s2_ref[8:9], s2_ref[16:17])):
            row_s[m : m + 1] = v
        row_s[7:8] = jnp.zeros((1, n), f32)
        col_s[...] = jnp.zeros(col_s.shape, f32)
        for i in range(2):
            col_s[i, 0:1] = sq_ref[0:1, i * hb : (i + 1) * hb]
            col_s[i, 1:2] = skv_ref[0:1, i * k : i * k + hb]
            col_s[i, 2:3] = skv_ref[0:1, i * k + hb : (i + 1) * k]
            for u in range(ups):
                col_s[i, 3 + u : 4 + u] = bu_ref[i, 0:1, u * hb : (u + 1) * hb]
        for i in range(2):
            for jx in range(2):
                p = 2 * which + jx
                main = nt(x_ref[p * q : (p + 1) * q], g_ref[i])
                small = row_s[:, p * q : (p + 1) * q]
                small = jnp.concatenate((small, jnp.zeros((8, hb - q), f32), col_s[i]), axis=1)
                small = jnp.concatenate((small, jnp.zeros((EXTRA - 8, k), f32)), axis=0)
                if got is None:
                    o_ref[i, jx, :q] = main.astype(bf16)
                    o_ref[i, jx, q:] = small.astype(bf16)
                else:
                    o = send_ref if jx else keep_ref
                    o[i * rows : i * rows + q] = (main + got_ref[i, jx, :q].astype(f32)).astype(bf16)
                    o[i * rows + q : (i + 1) * rows] = (small + got_ref[i, jx, q:].astype(f32)).astype(bf16)

    outs = [((2, 2, rows, k), bf16)] if got is None else [((2 * rows, k), bf16)] * 2
    args = (x, g, *sums) if got is None else (x, g, *sums, got)
    return call(body, outs, args, name, scratch=[pltpu.VMEM((8, n), f32), pltpu.VMEM((2, 8, hb), f32)])


def input_grad(gq, g, go, near, other):
    width, tokens = go.shape
    hb = gq.shape[1]
    k = width // 4
    nn_, no = len(near), len(other)

    def body(gq_ref, g_ref, go_ref, *refs):
        total = go_ref[...].astype(f32)
        for i, w in enumerate((refs[:nn_], refs[nn_ : nn_ + no])):
            w = jnp.concatenate([r[:k] for r in w], axis=0)
            total = total + nn(w[:, :hb], gq_ref[i]) + nn(w[:, hb:], g_ref[i])
        for p, o_ref in enumerate(refs[nn_ + no :]):
            o_ref[...] = total[p * k : (p + 1) * k].astype(bf16)

    return call(body, [((k, tokens), bf16)] * 4, (gq, g, go, *near, *other), "input_grad")


def swap(value, axis, mask):
    size = lax.axis_size(axis)
    return lax.ppermute(value, axis, [(s, s ^ mask) for s in range(size)])


def after(value, *others):
    return lax.optimization_barrier((value, *others))[0]


class Fold:
    def __init__(self, value):
        self.value = value
        self.four = lax.axis_size("dp") == 4
        if not self.four:
            self.value = lax.psum(value, "dp")
            return
        self.odd = lax.axis_index("dp") % 2 == 1
        n = value.shape[1] // 2
        low, high = value[:, :n], value[:, n:]
        self.value = jnp.where(self.odd, high, low)
        self.got = swap(jnp.where(self.odd, low, high), "dp", 1)

    def step(self, order, mask):
        if not self.four:
            return order
        self.value = after(self.value, order) + self.got
        self.got = swap(self.value, "dp", mask)
        return self.value

    def middle(self, order):
        return self.step(order, 2)

    def back(self, order):
        return self.step(order, 1)

    def result(self):
        if not self.four:
            return self.value.astype(f32)
        a, b = self.value.astype(f32), self.got.astype(f32)
        return jnp.concatenate((jnp.where(self.odd, b, a), jnp.where(self.odd, a, b)), axis=1)


def total(keep, got, last):
    n = keep.shape[0] // 2
    return keep[:n] + got[:n] + last


def far_half(keep, got):
    n = keep.shape[0] // 2
    return keep[n:] + got[n:]


def exchange(blocks):
    return [blocks[0]] + [swap(blocks[j], "row", j) for j in (1, 2, 3)]


def reduce_small(value, axis):
    step = 1
    while step < lax.axis_size(axis):
        value = value + swap(value, axis, step)
        step *= 2
    return value


def shards(
    inputs, teacher, lengths, omega,
    w_query, b_query, w_key, b_key, w_value, b_value, w_out, b_out,
    norm1_gain, norm1_bias, w_up, up_bias, w_down, b_down, norm2_gain, norm2_bias,
):
    row_parts = lax.axis_size("row")
    feat_local, seq_length = inputs.shape
    width = feat_local * row_parts
    head_local, head_width, feats = omega.shape
    heads = head_local * lax.axis_size("col")
    tokens = seq_length // row_parts
    hb = head_local * head_width
    hid_local = w_up.shape[1]
    row = lax.axis_index("row")
    col = lax.axis_index("col")
    row_ref = row.astype(jnp.int32).reshape(1)

    omegas = (omega, swap(omega, "col", 1))
    vecs = (b_out, norm1_gain, norm1_bias, b_down, norm2_gain, norm2_bias)
    ins = split_positions(inputs, row_ref, row_parts)
    ins_got = exchange(ins)
    xs = [ins_got[j] for j in (0, 2, 1, 3)]
    own_a = narrow_small((after(w_query, *ins), w_key, w_value), vecs, (b_query, b_key, b_value), up_bias, "narrow_a")
    a_y = swap(own_a, "col", 1)
    a_x = swap(own_a, "row", 2)
    a_far = swap(after(a_x, a_y, omegas[1]), "col", 1)
    near_a = (own_a, a_x, swap(own_a, "row", 1), swap(a_x, "row", 1))
    other_a = (a_y, a_far, swap(a_y, "row", 1), swap(a_far, "row", 1))
    count = reduce_small(jnp.sum(lengths).astype(f32).reshape(1, 1) + jnp.zeros((8, 128), f32), "dp")
    own_b = narrow((after(w_out, own_a, count), w_up, w_down), 3, "narrow_b")
    b_x = swap(after(own_b, a_x, ins_got[2], ins_got[3]), "row", 2)
    b_y = swap(after(own_b, a_far), "col", 1)
    length = lax.dynamic_index_in_dim(lengths, col, 0, False)
    keep = ((row * tokens + jnp.arange(tokens, dtype=jnp.int32)) < length).astype(f32)
    keep = jnp.broadcast_to(keep[None, :], (8, tokens))
    scale = (2.0 * LOSS_SCALE) / (count * width)

    x, fq, fk, uq, uk, v, kv, vecs, up_bias_all = attention_in(
        xs, near_a, other_a, omegas, keep, head_local, head_width, hid_local
    )
    kv0 = kv + swap(kv, "row", 1)
    kv1 = swap(kv0, "row", 2)
    theirs = split_positions(after(teacher, kv0), row_ref, row_parts)
    teach = exchange(theirs)
    target = [teach[j] for j in (0, 2, 1, 3)]
    b_x = after(b_x, kv0, theirs[0])
    b_y = after(b_y, kv0, theirs[0])
    b_far_y = swap(b_x[CUT:], "col", 1)
    b_far_x = swap(b_y[:CUT], "row", 2)
    near_b = (own_b, b_x)
    near_b = near_b + tuple(swap(p, "row", 1) for p in near_b)
    other_b = (b_y, b_far_x, after(b_far_y, kv1, b_far_x, teach[2], teach[3]))
    other_b = other_b + tuple(swap(p, "row", 1) for p in other_b)
    kv, att, inv, xh1, r1, x1, hid, slope, gf, sum2, *out = middle(
        kv0, kv1, fq, x, near_b, other_b, vecs, up_bias_all, target, keep, scale, heads, head_width, hid_local
    )
    out = exchange([out[j] for j in (0, 2, 1, 3)])

    theirs = grad_theirs(gf, hid, hb, "down_theirs")
    got1 = swap(theirs, "row", 1)
    gu, bu, bd = down_back(after(gf, theirs), slope, near_b, other_b, hb, hid_local)
    kept0, kept1, send0, send1 = grad_mine(after(gf, gu), hid, got1, hb, "down_mine")
    down = ((kept0, swap(send0, "col", 1)), (kept1, swap(send1, "col", 1)))
    go, sum1 = up_back(after(gu, send0), gf, xh1, r1, vecs, near_b, other_b, hb)
    gn, gkv = attention_mid(go, att, inv, fq, near_b, other_b, heads, head_width)
    gkv0 = gkv + swap(gkv, "row", 1)
    gkv1 = swap(gkv0, "row", 2)
    far = far_half(after(down[0][0], gn, *out), down[0][1])
    r_down0 = swap(far, "row", 2)
    theirs = grad_theirs(after(x1, far), gu, hb, "up_theirs")
    got2 = swap(theirs, "row", 1)
    gq, sum_q = query_back(after(gn, theirs), kv, fq, uq, omegas, heads, head_width)
    kept0, kept1, send0, send1 = grad_mine(after(x1, gq, gkv0), gu, got2, hb, "up_mine")
    up = ((kept0, swap(send0, "col", 1)), (kept1, swap(send1, "col", 1)))
    far = far_half(after(down[1][0], send0), down[1][1])
    r_down1 = swap(far, "row", 2)
    gq = gq.reshape(2, hb, tokens)
    att2 = att.reshape(2, hb, tokens)
    theirs = pair_theirs(after(x, far), gq, go, att2, "pair_theirs")
    got3 = swap(theirs, "row", 1)
    down0 = total(after(down[0][0], theirs), down[0][1], r_down0)
    z_down0 = Fold(down0)
    g, sum_kv = key_back(after(gkv0, down0), gkv1, fk, uk, v, omegas, heads, head_width)
    g = g.reshape(2, 2 * hb, tokens)
    sums = (sum1, sum2, bd, bu, sum_q, sum_kv)
    far = far_half(after(up[0][0], g), up[0][1])
    r_up0 = swap(far, "row", 2)
    theirs = last_parts(after(x, far), g, sums, None, "last_theirs")[0]
    got4 = swap(theirs, "row", 1)
    keep3, send3 = pair_mine(after(x, theirs), gq, go, att2, got3, "pair_mine")
    r_y3 = swap(send3, "col", 1)
    keep4, send4 = last_parts(after(x, send3), g, sums, got4, "last_mine")
    r_x4 = swap(send4, "row", 2)
    down1 = total(after(down[1][0], send4), down[1][1], r_down1)
    z_down1 = Fold(down1)
    order = z_down0.middle(down1)
    far = far_half(after(up[1][0], order), up[1][1])
    r_up1 = swap(far, "row", 2)
    gin = input_grad(gq, g, after(go, far), near_a, other_a)
    far = far_half(after(keep4, gin[0]), r_x4)
    r_y4 = swap(far, "col", 1)
    up0 = total(after(up[0][0], far), up[0][1], r_up0)
    z_up0 = Fold(up0)
    order = z_down1.middle(up0)
    order = z_down0.back(order)
    far = far_half(after(keep3, order), r_y3)
    r_x3 = swap(far, "row", 2)
    gin = exchange([after(gin[j], far) for j in (0, 2, 1, 3)])
    order = z_up0.middle(far)
    up1 = total(after(up[1][0], order), up[1][1], r_up1)
    z_up1 = Fold(up1)
    order = z_down1.back(up1)
    last = total(after(keep4, order), r_x4, r_y4)
    last = jnp.concatenate((last, total(keep3, r_y3, r_x3)), axis=0)
    z_last = Fold(last)
    order = z_up1.middle(last)
    order = z_up0.back(order)
    order = z_last.middle(order)
    order = z_up1.back(order)
    order = z_last.back(order)
    out[0] = after(out[0], order)
    out = join_positions(out, row_ref)
    grad_in = join_positions([after(gin[0], out), *gin[1:]], row_ref)
    grad_down = jnp.concatenate((z_down0.result(), z_down1.result()), axis=1)
    grad_up = jnp.concatenate((z_up0.result(), z_up1.result()), axis=1)
    last = z_last.result()
    grad_pair = last[keep4.shape[0] // 2 :]

    extra = last[feat_local : keep4.shape[0] // 2]
    rows = extra[:7, :feat_local]
    cols = extra[:7, hb:]
    loss = rows[6, 0] / (count[0, 0] * width)
    return (
        out,
        loss,
        grad_in,
        grad_pair[:, :hb],
        cols[0],
        last[:feat_local, :hb],
        cols[1],
        last[:feat_local, hb:],
        cols[2],
        grad_pair[:, hb:],
        rows[0],
        rows[1],
        rows[2],
        grad_up,
        cols[3:].reshape(hid_local),
        grad_down,
        rows[3],
        rows[4],
        rows[5],
    )


def solution(mesh):
    both = P("row", ("dp", "col"))
    in_specs = (
        both, both, P("dp"), P("col", None, None),
        P("row", "col"), P("col"), P("row", "col"), P("col"), P("row", "col"), P("col"),
        P("row", "col"), P("row"), P("row"), P("row"),
        P("row", "col"), P("col"), P("row", "col"), P("row"), P("row"), P("row"),
    )
    out_specs = (
        both, P(), both,
        P("row", "col"), P("col"), P("row", "col"), P("col"), P("row", "col"), P("col"),
        P("row", "col"), P("row"), P("row"), P("row"),
        P("row", "col"), P("col"), P("row", "col"), P("row"), P("row"), P("row"),
    )
    return jax.shard_map(shards, mesh=mesh, in_specs=in_specs, out_specs=out_specs, check_vma=False)
```

profile of v0, /device:TPU:0, one launch (start us, length us, event | category | flops | bytes accessed | tf_op | source)
XLA Modules:
  0.0 313.9 jit_solution(9079052028659054494)
XLA Ops:
  2.0 2.4 split_positions.2
  4.4 2.1 narrow_a.1.refs_4_.refs_0_
  6.5 3.0 collective-permute-start.6
  16.0 2.6 collective-permute-start.14
  19.1 5.8 %collective-permute-done.7.refs_13_.om1_ref = bf16[6,64,256]{2,1,0:T(8,128)(2,1)S(1)} collective-permute-done((bf16[6,64,256]{2,1,0:T(8,128)(2,1)S(1)}, bf16[6,64,256]{2,1,0:T(8,128)(2,1)S(1)}, u32[]{:S(2)}, u32[]{:S(2)}) %collective-permute-start.7) | collective-permute-done | bytes 196640 | tf_op jit(solution)/shard_map/ppermute | solution.py:598
  28.9 3.6 %narrow_b.1.refs_4_.refs_14_.refs_24_.refs_0_ = bf16[192,3456]{1,0:T(8,128)(2,1)} custom-call(f32[192,384]{1,0:T(8,128)} %refs_0_.1, f32[192,1536]{1,0:T(8,128)} %refs_1_.3, f32[192,1536]{1,0:T(8,128)} %refs_2_.3), custom_call_target="tpu_custom_call" | custom-call | flops 1000 | bytes 1000 | tf_op jit(solution)/shard_map/narrow_b/pallas_call | solution.py:50
  34.7 5.3 %collective-permute-done.8.refs_9_.refs_5_ = bf16[208,1152]{1,0:T(8,128)(2,1)} collective-permute-done((bf16[208,1152]{1,0:T(8,128)(2,1)}, bf16[208,1152]{1,0:T(8,128)(2,1)}, u32[]{:S(2)}, u32[]{:S(2)}) %collective-permute-start.8) | collective-permute-done | bytes 479264 | tf_op jit(solution)/shard_map/ppermute | solution.py:598
  43.4 11.2 %attention_in.1 = (bf16[768,512]{1,0:T(8,128)(2,1)}, bf16[3072,512]{1,0:T(8,128)(2,1)}, bf16[3072,512]{1,0:T(8,128)(2,1)}, bf16[768,512]{1,0:T(8,128)(2,1)}, bf1...) custom-call(bf16[192,512]{1,0:T(8,128)(2,1)} %get-tuple-element.125., ...), custom_call_target="tpu_custom_call" | custom-call | flops 1000 | bytes 1000 | tf_op jit(solution)/shard_map/attention_in/pallas_call | solution.py:50
  54.8 1.8 collective-permute-done.11
  57.8 2.5 split_positions.3
  60.3 3.3 %collective-permute-done.15.refs_5_.refs_15_.refs_25_.refs_1_ = bf16[192,3456]{1,0:T(8,128)(2,1)S(1)} collective-permute-done((bf16[192,3456]{1,0:T(8,128)(2,1)}, bf16[192,3456]{1,0:T(8,128)(2,1)S(1)}, u32[]{:S(2)}, u32[]{:S(2)}) %collective-permute-start.15) | collective-permute-done | bytes 1327136 | tf_op jit(solution)/shard_map/ppermute | solution.py:598
  65.7 1.8 collective-permute-start.21
  67.5 4.7 %collective-permute-done.18.refs_8_.refs_18_.refs_28_.refs_4_ = bf16[192,3456]{1,0:T(8,128)(2,1)S(1)} collective-permute-done((bf16[192,3456]{1,0:T(8,128)(2,1)}, bf16[192,3456]{1,0:T(8,128)(2,1)S(1)}, u32[]{:S(2)}, u32[]{:S(2)}) %collective-permute-start.18) | collective-permute-done | bytes 1327136 | tf_op jit(solution)/shard_map/ppermute | solution.py:598
  72.3 10.4 %collective-permute-done.21.refs_37_ = bf16[192,512]{1,0:T(8,128)(2,1)S(1)} collective-permute-done((bf16[192,512]{1,0:T(8,128)(2,1)S(1)}, bf16[192,512]{1,0:T(8,128)(2,1)S(1)}, u32[]{:S(2)}, u32[]{:S(2)}) %collective-permute-start.21) | collective-permute-done | bytes 196640 | tf_op jit(solution)/shard_map/ppermute | solution.py:598
  84.7 2.3 collective-permute-start.17
  87.1 5.1 %collective-permute-done.19.refs_9_.refs_19_.refs_29_.refs_5_ = bf16[48,3456]{1,0:T(8,128)(2,1)S(1)} collective-permute-done((bf16[48,3456]{1,0:T(8,128)(2,1)S(1)}, bf16[48,3456]{1,0:T(8,128)(2,1)S(1)}, u32[]{:S(2)}, u32[]{:S(2)}) %collective-permute-start.19) | collective-permute-done | bytes 331808 | tf_op jit(solution)/shard_map/ppermute | solution.py:598
  93.7 2.7 collective-permute-done.26.refs_38_
  98.6 21.2 %middle.1 = (bf16[864,256]{1,0:T(8,128)(2,1)}, bf16[768,512]{1,0:T(8,128)(2,1)}, f32[16,512]{1,0:T(8,128)}, bf16[768,512]{1,0:T(8,128)(2,1)}, f32[8,512]{1,0:T(8...) custom-call(bf16[864,256]{1,0:T(8,128)(2,1)} %copy-done.72, ...), custom_call_target="tpu_custom_call" | custom-call | flops 1000 | bytes 1000 | tf_op jit(solution)/shard_map/middle/pallas_call | solution.py:50
  121.0 1.9 copy-done.24
  122.9 2.8 down_theirs.1
  129.6 7.6 %down_back.1 = (bf16[2,1536,512]{2,1,0:T(8,128)(2,1)}, f32[2,8,1536]{2,1,0:T(8,128)S(1)}, f32[8,768]{1,0:T(8,128)S(1)}) custom-call(bf16[768,512]{1,0:T(8,128)(2,1)S(1)} %copy-done.23, bf16[2,1536,512]{2,1,0:T(8,128)(2,1)} %get-tuple-element.152.slope_ref, bf16[192,3456]{1,0:T(8,128)(2,1)S(1)} %copy-done.1, bf16[192,3456]{1,0:T(8,128)(2,1)S(1)} %copy-done.3, ...), custom_call_target="tpu_custom_call" | custom-call | flops 1000 | bytes 1000 | tf_op jit(solution)/shard_map/down_back/pallas_call | solution.py:50
  137.3 3.2 %down_mine.1 = (bf16[384,768]{1,0:T(8,128)(2,1)S(1)}, bf16[384,768]{1,0:T(8,128)(2,1)S(1)}, bf16[384,768]{1,0:T(8,128)(2,1)S(1)}, bf16[384,768]{1,0:T(8,128)(2,1)S(1)}) custom-call(bf16[768,512]{1,0:T(8,128)(2,1)S(1)} %copy-done.23, bf16[2,1536,512]{2,1,0:T(8,128)(2,1)S(1)} %copy-done.24, bf16[2,384,1536]{2,1,0:T(8,128)(2,1)S(1)} %collective-permute-done.27.got_ref), custom_call_target="tpu_custom_call" | custom-call | flops 1000 | bytes 1000 | tf_op jit(solution)/shard_map/down_mine/pallas_call | solution.py:50
  144.0 18.3 %up_back.1 = (bf16[768,512]{1,0:T(8,128)(2,1)S(1)}, f32[24,768]{1,0:T(8,128)S(1)}) custom-call(bf16[2,1536,512]{2,1,0:T(8,128)(2,1)} %get-tuple-element.156.gu_ref.r_ref, bf16[768,512]{1,0:T(8,128)(2,1)S(1)} %copy-done.23, bf16[768,512]{1,0:T(8,128)(2,1)S(1)} %copy-done.44, f32[8,512]{1,0:T(8,128)S(1)} %copy-done.69, f32[8,768]{1,0:T(8,128)S(1)} %copy-done.65, ...), custom_call_target="tpu_custom_call" | custom-call | flops 1000 | bytes 1000 | tf_op jit(solution)/shard_map/up_back/pallas_call | solution.py:50
  163.0 3.7 %attention_mid.1 = (bf16[864,512]{1,0:T(8,128)(2,1)S(1)}, bf16[864,256]{1,0:T(8,128)(2,1)S(1)}) custom-call(bf16[768,512]{1,0:T(8,128)(2,1)S(1)} %get-tuple-element.205.go_ref, bf16[768,512]{1,0:T(8,128)(2,1)S(1)} %copy-done.32, f32[16,512]{1,0:T(8,128)S(1)} %copy-done.68, bf16[3072,512]{1,0:T(8,128)(2,1)} %get-tuple-element.132.refs_2_.fq_ref, ...), custom_call_target="tpu_custom_call" | custom-call | flops 1000 | bytes 1000 | tf_op jit(solution)/shard_map/attention_mid/pallas_call | solution.py:50
  168.0 2.8 up_theirs.1
  171.8 4.3 %collective-permute-done.32 = bf16[864,256]{1,0:T(8,128)(2,1)S(1)} collective-permute-done((bf16[864,256]{1,0:T(8,128)(2,1)S(1)}, bf16[864,256]{1,0:T(8,128)(2,1)S(1)}, u32[]{:S(2)}, u32[]{:S(2)}) %collective-permute-start.32) | collective-permute-done | bytes 442400 | tf_op jit(solution)/shard_map/ppermute | solution.py:598
  176.3 2.9 query_back.1
  179.2 3.9 %up_mine.1 = (bf16[384,768]{1,0:T(8,128)(2,1)S(1)}, bf16[384,768]{1,0:T(8,128)(2,1)S(1)}, bf16[384,768]{1,0:T(8,128)(2,1)S(1)}, bf16[384,768]{1,0:T(8,128)(2,1)}) custom-call(bf16[768,512]{1,0:T(8,128)(2,1)S(1)} %copy-done.36, bf16[2,1536,512]{2,1,0:T(8,128)(2,1)S(1)} %copy-done.20, bf16[2,384,1536]{2,1,0:T(8,128)(2,1)S(1)} %collective-permute-done.33.got_ref), custom_call_target="tpu_custom_call" | custom-call | flops 1000 | bytes 1000 | tf_op jit(solution)/shard_map/up_mine/pallas_call | solution.py:50
  188.1 2.0 pair_theirs.1
  190.1 3.3 %collective-permute-done.35 = bf16[192,768]{1,0:T(8,128)(2,1)S(1)} collective-permute-done((bf16[192,768]{1,0:T(8,128)(2,1)S(1)}, bf16[192,768]{1,0:T(8,128)(2,1)S(1)}, u32[]{:S(2)}, u32[]{:S(2)}) %collective-permute-start.35) | collective-permute-done | bytes 294944 | tf_op jit(solution)/shard_map/ppermute | solution.py:598
  194.2 7.8 %collective-permute-done.36.gkv1_ref = bf16[864,256]{1,0:T(8,128)(2,1)S(1)} collective-permute-done((bf16[864,256]{1,0:T(8,128)(2,1)S(1)}, bf16[864,256]{1,0:T(8,128)(2,1)S(1)}, u32[]{:S(2)}, u32[]{:S(2)}) %collective-permute-start.36) | collective-permute-done | bytes 442400 | tf_op jit(solution)/shard_map/ppermute | solution.py:598
  202.1 3.7 %key_back.1 = (bf16[1536,512]{1,0:T(8,128)(2,1)S(1)}, f32[8,1536]{1,0:T(8,128)S(1)}) custom-call(bf16[864,256]{1,0:T(8,128)(2,1)S(1)} %add.132.gkv0_ref, bf16[864,256]{1,0:T(8,128)(2,1)S(1)} %collective-permute-done.36.gkv1_ref, bf16[3072,512]{1,0:T(8,128)(2,1)S(1)} %copy-done.37, bf16[768,512]{1,0:T(8,128)(2,1)S(1)} %copy-done.45, ...), custom_call_target="tpu_custom_call" | custom-call | flops 1000 | bytes 1000 | tf_op jit(solution)/shard_map/key_back/pallas_call | solution.py:50
  206.6 2.2 last_theirs.1
  219.0 2.3 pair_mine.1
  221.8 2.5 last_mine.1
  226.1 2.6 collective-permute-start.46
  231.4 3.9 %input_grad.1 = (bf16[192,512]{1,0:T(8,128)(2,1)S(1)}, bf16[192,512]{1,0:T(8,128)(2,1)S(1)}, bf16[192,512]{1,0:T(8,128)(2,1)S(1)}, bf16[192,512]{1,0:T(8,128)(2,1)S(1)}) custom-call(bf16[2,384,512]{2,1,0:T(8,128)(2,1)S(1)} %bitcast.23, bf16[2,768,512]{2,1,0:T(8,128)(2,1)S(1)} %bitcast.20, bf16[768,512]{1,0:T(8,128)(2,1)S(1)} %get-tuple-element.205.go_ref, ...), custom_call_target="tpu_custom_call" | custom-call | flops 1000 | bytes 1000 | tf_op jit(solution)/shard_map/input_grad/pallas_call | solution.py:50
  235.3 6.4 %collective-permute-done.43 = bf16[416,768]{1,0:T(8,128)(2,1)S(1)} collective-permute-done((bf16[416,768]{1,0:T(8,128)(2,1)S(1)}, bf16[416,768]{1,0:T(8,128)(2,1)S(1)}, u32[]{:S(2)}, u32[]{:S(2)}) %collective-permute-start.43) | collective-permute-done | bytes 639008 | tf_op jit(solution)/shard_map/ppermute | solution.py:598
  242.3 5.8 %collective-permute-done.45 = bf16[192,384]{1,0:T(8,128)(2,1)S(1)} collective-permute-done((bf16[192,384]{1,0:T(8,128)(2,1)S(1)}, bf16[192,384]{1,0:T(8,128)(2,1)S(1)}, u32[]{:S(2)}, u32[]{:S(2)}) %collective-permute-start.45) | collective-permute-done | bytes 147488 | tf_op jit(solution)/shard_map/ppermute | solution.py:598
  248.2 2.4 collective-permute-start.50
  250.7 2.0 collective-permute-start.48
  253.7 4.6 %collective-permute-done.48 = bf16[192,384]{1,0:T(8,128)(2,1)S(1)} collective-permute-done((bf16[192,384]{1,0:T(8,128)(2,1)S(1)}, bf16[192,384]{1,0:T(8,128)(2,1)S(1)}, u32[]{:S(2)}, u32[]{:S(2)}) %collective-permute-start.48) | collective-permute-done | bytes 147488 | tf_op jit(solution)/shard_map/ppermute | solution.py:598
  258.2 2.3 collective-permute-start.51
  267.9 7.0 %collective-permute-done.53 = bf16[192,384]{1,0:T(8,128)(2,1)S(1)} collective-permute-done((bf16[192,384]{1,0:T(8,128)(2,1)S(1)}, bf16[192,384]{1,0:T(8,128)(2,1)S(1)}, u32[]{:S(2)}, u32[]{:S(2)}) %collective-permute-start.53) | collective-permute-done | bytes 147488 | tf_op jit(solution)/shard_map/ppermute | solution.py:598
  277.8 6.3 %collective-permute-done.55 = bf16[400,384]{1,0:T(8,128)(2,1)S(1)} collective-permute-done((bf16[400,384]{1,0:T(8,128)(2,1)S(1)}, bf16[400,384]{1,0:T(8,128)(2,1)S(1)}, u32[]{:S(2)}, u32[]{:S(2)}) %collective-permute-start.55) | collective-permute-done | bytes 307232 | tf_op jit(solution)/shard_map/ppermute | solution.py:598
  286.1 2.2 collective-permute-done.62
  288.9 11.2 %collective-permute-done.57 = bf16[400,384]{1,0:T(8,128)(2,1)S(1)} collective-permute-done((bf16[400,384]{1,0:T(8,128)(2,1)S(1)}, bf16[400,384]{1,0:T(8,128)(2,1)S(1)}, u32[]{:S(2)}, u32[]{:S(2)}) %collective-permute-start.57) | collective-permute-done | bytes 307232 | tf_op jit(solution)/shard_map/ppermute | solution.py:598
  304.3 4.2 %collective-permute-done.58 = bf16[400,384]{1,0:T(8,128)(2,1)S(1)} collective-permute-done((bf16[400,384]{1,0:T(8,128)(2,1)S(1)}, bf16[400,384]{1,0:T(8,128)(2,1)S(1)}, u32[]{:S(2)}, u32[]{:S(2)}) %collective-permute-start.58) | collective-permute-done | bytes 307232 | tf_op jit(solution)/shard_map/ppermute | solution.py:598
  (348 shorter events, 81.1 us)
Async XLA Ops:
  6.5 18.7 %collective-permute-start.6 = (bf16[208,1152]{1,0:T(8,128)(2,1)}, bf16[208,1152]{1,0:T(8,128)(2,1)S(1)}, u32[]{:S(2)}, u32[]{:S(2)}) collective-permute-start(bf16[208,1152]{1,0:T(8,128)(2,1)} %narrow_a.1.refs_4_.refs_0_), channel_id=1, source_target_pairs={{0,1},{1,0},{2,3},{3,2},{4,5},{5,4},{6,7},{7,6},{8,9},{9,8},{10,11... | collective-permute-start | bytes 1437704 | tf_op jit(solution)/shard_map/ppermute | solution.py:598
  9.5 17.2 %collective-permute-start.3 = (bf16[208,1152]{1,0:T(8,128)(2,1)}, bf16[208,1152]{1,0:T(8,128)(2,1)}, u32[]{:S(2)}, u32[]{:S(2)}) collective-permute-start(bf16[208,1152]{1,0:T(8,128)(2,1)} %narrow_a.1.refs_4_.refs_0_), channel_id=1, source_target_pairs={{0,4},{2,6},{4,0},{6,2},{1,5},{3,7},{5,1},{7,3},{8,12},{10,14},{12... | collective-permute-start | bytes 1437704 | tf_op jit(solution)/shard_map/ppermute | solution.py:598
  13.9 10.9 %collective-permute-start.7 = (bf16[6,64,256]{2,1,0:T(8,128)(2,1)S(1)}, bf16[6,64,256]{2,1,0:T(8,128)(2,1)S(1)}, u32[]{:S(2)}, u32[]{:S(2)}) collective-permute-start(bf16[6,64,256]{2,1,0:T(8,128)(2,1)S(1)} %copy-done.40), channel_id=1, source_target_pairs={{0,1},{1,0},{2,3},{3,2},{4,5},{5,4},{6,7},{7,6},{8,9},{9,8},{10,11... | collective-permute-start | bytes 589832 | tf_op jit(solution)/shard_map/ppermute | solution.py:598
  16.0 12.3 %collective-permute-start.14 = (f32[8,128]{1,0:T(8,128)S(1)}, f32[8,128]{1,0:T(8,128)S(1)}, u32[]{:S(2)}, u32[]{:S(2)}) collective-permute-start(f32[8,128]{1,0:T(8,128)S(1)} %broadcast_add_fusion), channel_id=1, source_target_pairs={{0,16},{8,24},{16,0},{24,8},{1,17},{9,25},{17,1},{25,9},{2,18},{10... | collective-permute-start | bytes 12296 | tf_op jit(solution)/shard_map/ppermute | solution.py:598
  18.6 13.9 %collective-permute-start = (bf16[192,512]{1,0:T(8,128)(2,1)S(1)}, bf16[192,512]{1,0:T(8,128)(2,1)S(1)}, u32[]{:S(2)}, u32[]{:S(2)}) collective-permute-start(bf16[192,512]{1,0:T(8,128)(2,1)S(1)} %copy-done.90), channel_id=1, source_target_pairs={{0,4},{2,6},{4,0},{6,2},{1,5},{3,7},{5,1},{7,3},{8,12},{10,14},{12... | collective-permute-start | bytes 589832 | tf_op jit(solution)/shard_map/ppermute | solution.py:598
  25.2 14.8 %collective-permute-start.4 = (bf16[208,1152]{1,0:T(8,128)(2,1)}, bf16[208,1152]{1,0:T(8,128)(2,1)}, u32[]{:S(2)}, u32[]{:S(2)}) collective-permute-start(bf16[208,1152]{1,0:T(8,128)(2,1)} %narrow_a.1.refs_4_.refs_0_), channel_id=1, source_target_pairs={{0,2},{2,0},{4,6},{6,4},{1,3},{3,1},{5,7},{7,5},{8,10},{10,8},{12,... | collective-permute-start | bytes 1437704 | tf_op jit(solution)/shard_map/ppermute | solution.py:598
  26.7 13.3 %collective-permute-start.8 = (bf16[208,1152]{1,0:T(8,128)(2,1)}, bf16[208,1152]{1,0:T(8,128)(2,1)}, u32[]{:S(2)}, u32[]{:S(2)}) collective-permute-start(bf16[208,1152]{1,0:T(8,128)(2,1)} %collective-permute-done.3.refs_5_.refs_1_), channel_id=1, source_target_pairs={{0,1},{1,0},{2,3},{3,2},{4,5},{5,4},{6,7},{7,6},{8,9},{9,8},{10,11... | collective-permute-start | bytes 1437704 | tf_op jit(solution)/shard_map/ppermute | solution.py:598
  32.5 31.1 %collective-permute-start.15 = (bf16[192,3456]{1,0:T(8,128)(2,1)}, bf16[192,3456]{1,0:T(8,128)(2,1)S(1)}, u32[]{:S(2)}, u32[]{:S(2)}) collective-permute-start(bf16[192,3456]{1,0:T(8,128)(2,1)} %narrow_b.1.refs_4_.refs_14_.refs_24_.refs_0_), channel_id=1, source_target_pairs={{0,4},{2,6},{4,0},{6,2},{1,5},{3,7},{5,1},{7,3},{8,12},{10,14},{12... | collective-permute-start | bytes 3981320 | tf_op jit(solution)/shard_map/ppermute | solution.py:598
  33.1 9.7 %collective-permute-start.9 = (bf16[208,1152]{1,0:T(8,128)(2,1)S(1)}, bf16[208,1152]{1,0:T(8,128)(2,1)}, u32[]{:S(2)}, u32[]{:S(2)}) collective-permute-start(bf16[208,1152]{1,0:T(8,128)(2,1)S(1)} %collective-permute-done.6.refs_8_.refs_4_), channel_id=1, source_target_pairs={{0,2},{2,0},{4,6},{6,4},{1,3},{3,1},{5,7},{7,5},{8,10},{10,8},{12,... | collective-permute-start | bytes 1437704 | tf_op jit(solution)/shard_map/ppermute | solution.py:598
  40.0 32.3 %collective-permute-start.18 = (bf16[192,3456]{1,0:T(8,128)(2,1)}, bf16[192,3456]{1,0:T(8,128)(2,1)S(1)}, u32[]{:S(2)}, u32[]{:S(2)}) collective-permute-start(bf16[192,3456]{1,0:T(8,128)(2,1)} %narrow_b.1.refs_4_.refs_14_.refs_24_.refs_0_), channel_id=1, source_target_pairs={{0,1},{1,0},{2,3},{3,2},{4,5},{5,4},{6,7},{7,6},{8,9},{9,8},{10,11... | collective-permute-start | bytes 3981320 | tf_op jit(solution)/shard_map/ppermute | solution.py:598
  63.7 29.4 %collective-permute-start.20 = (bf16[144,3456]{1,0:T(8,128)(2,1)S(1)}, bf16[144,3456]{1,0:T(8,128)(2,1)S(1)}, u32[]{:S(2)}, u32[]{:S(2)}) collective-permute-start(bf16[144,3456]{1,0:T(8,128)(2,1)S(1)} %slice.182), channel_id=1, source_target_pairs={{0,1},{1,0},{2,3},{3,2},{4,5},{5,4},{6,7},{7,6},{8,9},{9,8},{10,11... | collective-permute-start | bytes 2985992 | tf_op jit(solution)/shard_map/ppermute | solution.py:598
  65.4 21.6 %collective-permute-start.12 = (bf16[864,256]{1,0:T(8,128)(2,1)S(1)}, bf16[864,256]{1,0:T(8,128)(2,1)S(1)}, u32[]{:S(2)}, u32[]{:S(2)}) collective-permute-start(bf16[864,256]{1,0:T(8,128)(2,1)S(1)} %add.126.refs_0_), channel_id=1, source_target_pairs={{0,4},{2,6},{4,0},{6,2},{1,5},{3,7},{5,1},{7,3},{8,12},{10,14},{12... | collective-permute-start | bytes 1327112 | tf_op jit(solution)/shard_map/ppermute | solution.py:598
  65.7 27.9 %collective-permute-start.16 = (bf16[192,3456]{1,0:T(8,128)(2,1)S(1)}, bf16[192,3456]{1,0:T(8,128)(2,1)S(1)}, u32[]{:S(2)}, u32[]{:S(2)}) collective-permute-start(bf16[192,3456]{1,0:T(8,128)(2,1)S(1)} %copy-done), channel_id=1, source_target_pairs={{0,2},{2,0},{4,6},{6,4},{1,3},{3,1},{5,7},{7,5},{8,10},{10,8},{12,... | collective-permute-start | bytes 3981320 | tf_op jit(solution)/shard_map/ppermute | solution.py:598
  65.7 17.0 %collective-permute-start.21 = (bf16[192,512]{1,0:T(8,128)(2,1)S(1)}, bf16[192,512]{1,0:T(8,128)(2,1)S(1)}, u32[]{:S(2)}, u32[]{:S(2)}) collective-permute-start(bf16[192,512]{1,0:T(8,128)(2,1)S(1)} %copy-done.92), channel_id=1, source_target_pairs={{0,4},{2,6},{4,0},{6,2},{1,5},{3,7},{5,1},{7,3},{8,12},{10,14},{12... | collective-permute-start | bytes 589832 | tf_op jit(solution)/shard_map/ppermute | solution.py:598
  72.3 12.4 %collective-permute-start.22 = (bf16[192,512]{1,0:T(8,128)(2,1)S(1)}, bf16[192,512]{1,0:T(8,128)(2,1)S(1)}, u32[]{:S(2)}, u32[]{:S(2)}) collective-permute-start(bf16[192,512]{1,0:T(8,128)(2,1)S(1)} %copy-done.91), channel_id=1, source_target_pairs={{0,6},{2,4},{4,2},{6,0},{1,7},{3,5},{5,3},{7,1},{8,14},{10,12},{12... | collective-permute-start | bytes 589832 | tf_op jit(solution)/shard_map/ppermute | solution.py:598
  82.7 9.5 %collective-permute-start.19 = (bf16[48,3456]{1,0:T(8,128)(2,1)S(1)}, bf16[48,3456]{1,0:T(8,128)(2,1)S(1)}, u32[]{:S(2)}, u32[]{:S(2)}) collective-permute-start(bf16[48,3456]{1,0:T(8,128)(2,1)S(1)} %slice.181), channel_id=1, source_target_pairs={{0,4},{2,6},{4,0},{6,2},{1,5},{3,7},{5,1},{7,3},{8,12},{10,14},{12... | collective-permute-start | bytes 995336 | tf_op jit(solution)/shard_map/ppermute | solution.py:598
  84.7 11.7 %collective-permute-start.17 = (bf16[192,3456]{1,0:T(8,128)(2,1)S(1)}, bf16[192,3456]{1,0:T(8,128)(2,1)S(1)}, u32[]{:S(2)}, u32[]{:S(2)}) collective-permute-start(bf16[192,3456]{1,0:T(8,128)(2,1)S(1)} %collective-permute-done.15.refs_5_.refs_15_.refs_25_.refs_1_), channel_id=1, source_target_pairs={{0,2},{2,0},{4,6},{6,4},{1,3},{3,1},{5,7},{7,5},{8,10},{10,8},{12,... | collective-permute-start | bytes 3981320 | tf_op jit(solution)/shard_map/ppermute | solution.py:598
  125.7 11.6 %collective-permute-start.27 = (bf16[2,384,1536]{2,1,0:T(8,128)(2,1)S(1)}, bf16[2,384,1536]{2,1,0:T(8,128)(2,1)S(1)}, u32[]{:S(2)}, u32[]{:S(2)}) collective-permute-start(bf16[2,384,1536]{2,1,0:T(8,128)(2,1)S(1)} %down_theirs.1), channel_id=1, source_target_pairs={{0,2},{2,0},{4,6},{6,4},{1,3},{3,1},{5,7},{7,5},{8,10},{10,8},{12,... | collective-permute-start | bytes 7077896 | tf_op jit(solution)/shard_map/ppermute | solution.py:598
  140.5 26.2 %collective-permute-start.31 = (bf16[384,768]{1,0:T(8,128)(2,1)S(1)}, bf16[384,768]{1,0:T(8,128)(2,1)S(1)}, u32[]{:S(2)}, u32[]{:S(2)}) collective-permute-start(bf16[384,768]{1,0:T(8,128)(2,1)S(1)} %get-tuple-element.155), channel_id=1, source_target_pairs={{0,1},{1,0},{2,3},{3,2},{4,5},{5,4},{6,7},{7,6},{8,9},{9,8},{10,11... | collective-permute-start | bytes 1769480 | tf_op jit(solution)/shard_map/ppermute | solution.py:598
  142.1 24.6 %collective-permute-start.28 = (bf16[192,512]{1,0:T(8,128)(2,1)S(1)}, bf16[192,512]{1,0:T(8,128)(2,1)S(1)}, u32[]{:S(2)}, u32[]{:S(2)}) collective-permute-start(bf16[192,512]{1,0:T(8,128)(2,1)S(1)} %copy-done.88), channel_id=1, source_target_pairs={{0,2},{2,0},{4,6},{6,4},{1,3},{3,1},{5,7},{7,5},{8,10},{10,8},{12,... | collective-permute-start | bytes 589832 | tf_op jit(solution)/shard_map/ppermute | solution.py:598
  142.2 24.5 %collective-permute-start.29 = (bf16[192,512]{1,0:T(8,128)(2,1)S(1)}, bf16[192,512]{1,0:T(8,128)(2,1)S(1)}, u32[]{:S(2)}, u32[]{:S(2)}) collective-permute-start(bf16[192,512]{1,0:T(8,128)(2,1)S(1)} %copy-done.86), channel_id=1, source_target_pairs={{0,4},{2,6},{4,0},{6,2},{1,5},{3,7},{5,1},{7,3},{8,12},{10,14},{12... | collective-permute-start | bytes 589832 | tf_op jit(solution)/shard_map/ppermute | solution.py:598
  142.8 24.0 %collective-permute-start.30 = (bf16[192,512]{1,0:T(8,128)(2,1)S(1)}, bf16[192,512]{1,0:T(8,128)(2,1)S(1)}, u32[]{:S(2)}, u32[]{:S(2)}) collective-permute-start(bf16[192,512]{1,0:T(8,128)(2,1)S(1)} %copy-done.85), channel_id=1, source_target_pairs={{0,6},{2,4},{4,2},{6,0},{1,7},{3,5},{5,3},{7,1},{8,14},{10,12},{12... | collective-permute-start | bytes 589832 | tf_op jit(solution)/shard_map/ppermute | solution.py:598
  171.3 16.0 %collective-permute-start.34 = (bf16[384,768]{1,0:T(8,128)(2,1)S(1)}, bf16[384,768]{1,0:T(8,128)(2,1)S(1)}, u32[]{:S(2)}, u32[]{:S(2)}) collective-permute-start(bf16[384,768]{1,0:T(8,128)(2,1)S(1)} %copy-done.71), channel_id=1, source_target_pairs={{0,1},{1,0},{2,3},{3,2},{4,5},{5,4},{6,7},{7,6},{8,9},{9,8},{10,11... | collective-permute-start | bytes 1769480 | tf_op jit(solution)/shard_map/ppermute | solution.py:598
  183.0 22.7 %collective-permute-start.37 = (bf16[384,768]{1,0:T(8,128)(2,1)S(1)}, bf16[384,768]{1,0:T(8,128)(2,1)S(1)}, u32[]{:S(2)}, u32[]{:S(2)}) collective-permute-start(bf16[384,768]{1,0:T(8,128)(2,1)S(1)} %get-tuple-element.177), channel_id=1, source_target_pairs={{0,1},{1,0},{2,3},{3,2},{4,5},{5,4},{6,7},{7,6},{8,9},{9,8},{10,11... | collective-permute-start | bytes 1769480 | tf_op jit(solution)/shard_map/ppermute | solution.py:598
  183.5 9.9 %collective-permute-start.35 = (bf16[192,768]{1,0:T(8,128)(2,1)S(1)}, bf16[192,768]{1,0:T(8,128)(2,1)S(1)}, u32[]{:S(2)}, u32[]{:S(2)}) collective-permute-start(bf16[192,768]{1,0:T(8,128)(2,1)S(1)} %slice_add_fusion.11), channel_id=1, source_target_pairs={{0,4},{2,6},{4,0},{6,2},{1,5},{3,7},{5,1},{7,3},{8,12},{10,14},{12... | collective-permute-start | bytes 884744 | tf_op jit(solution)/shard_map/ppermute | solution.py:598
  183.9 18.1 %collective-permute-start.36 = (bf16[864,256]{1,0:T(8,128)(2,1)S(1)}, bf16[864,256]{1,0:T(8,128)(2,1)S(1)}, u32[]{:S(2)}, u32[]{:S(2)}) collective-permute-start(bf16[864,256]{1,0:T(8,128)(2,1)S(1)} %add.132.gkv0_ref), channel_id=1, source_target_pairs={{0,4},{2,6},{4,0},{6,2},{1,5},{3,7},{5,1},{7,3},{8,12},{10,14},{12... | collective-permute-start | bytes 1327112 | tf_op jit(solution)/shard_map/ppermute | solution.py:598
  208.8 12.4 %collective-permute-start.39 = (bf16[2,2,208,768]{3,2,1,0:T(8,128)(2,1)}, bf16[2,2,208,768]{3,2,1,0:T(8,128)(2,1)}, u32[]{:S(2)}, u32[]{:S(2)}) collective-permute-start(bf16[2,2,208,768]{3,2,1,0:T(8,128)(2,1)} %last_theirs.1), channel_id=1, source_target_pairs={{0,2},{2,0},{4,6},{6,4},{1,3},{3,1},{5,7},{7,5},{8,10},{10,8},{12,... | collective-permute-start | bytes 3833864 | tf_op jit(solution)/shard_map/ppermute | solution.py:598
  209.3 19.4 %collective-permute-start.42 = (bf16[384,768]{1,0:T(8,128)(2,1)}, bf16[384,768]{1,0:T(8,128)(2,1)}, u32[]{:S(2)}, u32[]{:S(2)}) collective-permute-start(bf16[384,768]{1,0:T(8,128)(2,1)} %get-tuple-element.204), channel_id=1, source_target_pairs={{0,1},{1,0},{2,3},{3,2},{4,5},{5,4},{6,7},{7,6},{8,9},{9,8},{10,11... | collective-permute-start | bytes 1769480 | tf_op jit(solution)/shard_map/ppermute | solution.py:598
  210.8 13.5 %collective-permute-start.40 = (bf16[192,768]{1,0:T(8,128)(2,1)}, bf16[192,768]{1,0:T(8,128)(2,1)}, u32[]{:S(2)}, u32[]{:S(2)}) collective-permute-start(bf16[192,768]{1,0:T(8,128)(2,1)} %slice_add_fusion.10), channel_id=1, source_target_pairs={{0,4},{2,6},{4,0},{6,2},{1,5},{3,7},{5,1},{7,3},{8,12},{10,14},{12... | collective-permute-start | bytes 884744 | tf_op jit(solution)/shard_map/ppermute | solution.py:598
  213.6 12.5 %collective-permute-start.41 = (bf16[192,384]{1,0:T(8,128)(2,1)S(1)}, bf16[192,384]{1,0:T(8,128)(2,1)S(1)}, u32[]{:S(2)}, u32[]{:S(2)}) collective-permute-start(bf16[192,384]{1,0:T(8,128)(2,1)S(1)} %get-tuple-element.264), channel_id=1, source_target_pairs={{0,8},{8,0},{16,24},{24,16},{1,9},{9,1},{17,25},{25,17},{2,10},{10... | collective-permute-start | bytes 442376 | tf_op jit(solution)/shard_map/ppermute | solution.py:598
  215.2 27.0 %collective-permute-start.44 = (bf16[192,768]{1,0:T(8,128)(2,1)}, bf16[192,768]{1,0:T(8,128)(2,1)S(1)}, u32[]{:S(2)}, u32[]{:S(2)}) collective-permute-start(bf16[192,768]{1,0:T(8,128)(2,1)} %slice_add_fusion.8), channel_id=1, source_target_pairs={{0,4},{2,6},{4,0},{6,2},{1,5},{3,7},{5,1},{7,3},{8,12},{10,14},{12... | collective-permute-start | bytes 884744 | tf_op jit(solution)/shard_map/ppermute | solution.py:598
  221.3 31.5 %collective-permute-start.47 = (bf16[384,768]{1,0:T(8,128)(2,1)S(1)}, bf16[384,768]{1,0:T(8,128)(2,1)S(1)}, u32[]{:S(2)}, u32[]{:S(2)}) collective-permute-start(bf16[384,768]{1,0:T(8,128)(2,1)S(1)} %get-tuple-element.196), channel_id=1, source_target_pairs={{0,1},{1,0},{2,3},{3,2},{4,5},{5,4},{6,7},{7,6},{8,9},{9,8},{10,11... | collective-permute-start | bytes 1769480 | tf_op jit(solution)/shard_map/ppermute | solution.py:598
  224.4 17.3 %collective-permute-start.43 = (bf16[416,768]{1,0:T(8,128)(2,1)S(1)}, bf16[416,768]{1,0:T(8,128)(2,1)S(1)}, u32[]{:S(2)}, u32[]{:S(2)}) collective-permute-start(bf16[416,768]{1,0:T(8,128)(2,1)S(1)} %get-tuple-element.199), channel_id=1, source_target_pairs={{0,4},{2,6},{4,0},{6,2},{1,5},{3,7},{5,1},{7,3},{8,12},{10,14},{12... | collective-permute-start | bytes 1916936 | tf_op jit(solution)/shard_map/ppermute | solution.py:598
  226.1 24.5 %collective-permute-start.46 = (bf16[192,384]{1,0:T(8,128)(2,1)S(1)}, bf16[192,384]{1,0:T(8,128)(2,1)S(1)}, u32[]{:S(2)}, u32[]{:S(2)}) collective-permute-start(bf16[192,384]{1,0:T(8,128)(2,1)S(1)} %add.139), channel_id=1, source_target_pairs={{0,16},{8,24},{16,0},{24,8},{1,17},{9,25},{17,1},{25,9},{2,18},{10... | collective-permute-start | bytes 442376 | tf_op jit(solution)/shard_map/ppermute | solution.py:598
  229.8 30.8 %collective-permute-start.49 = (bf16[192,768]{1,0:T(8,128)(2,1)S(1)}, bf16[192,768]{1,0:T(8,128)(2,1)S(1)}, u32[]{:S(2)}, u32[]{:S(2)}) collective-permute-start(bf16[192,768]{1,0:T(8,128)(2,1)S(1)} %slice_add_fusion.6), channel_id=1, source_target_pairs={{0,4},{2,6},{4,0},{6,2},{1,5},{3,7},{5,1},{7,3},{8,12},{10,14},{12... | collective-permute-start | bytes 884744 | tf_op jit(solution)/shard_map/ppermute | solution.py:598
  248.2 13.6 %collective-permute-start.50 = (bf16[192,384]{1,0:T(8,128)(2,1)S(1)}, bf16[192,384]{1,0:T(8,128)(2,1)S(1)}, u32[]{:S(2)}, u32[]{:S(2)}) collective-permute-start(bf16[192,384]{1,0:T(8,128)(2,1)S(1)} %add.144), channel_id=1, source_target_pairs={{0,16},{8,24},{16,0},{24,8},{1,17},{9,25},{17,1},{25,9},{2,18},{10... | collective-permute-start | bytes 442376 | tf_op jit(solution)/shard_map/ppermute | solution.py:598
  250.6 16.0 %collective-permute-start.64 = (bf16[192,384]{1,0:T(8,128)(2,1)S(1)}, bf16[192,384]{1,0:T(8,128)(2,1)S(1)}, u32[]{:S(2)}, u32[]{:S(2)}) collective-permute-start(bf16[192,384]{1,0:T(8,128)(2,1)S(1)} %add.145), channel_id=1, source_target_pairs={{0,8},{8,0},{16,24},{24,16},{1,9},{9,1},{17,25},{25,17},{2,10},{10... | collective-permute-start | bytes 442376 | tf_op jit(solution)/shard_map/ppermute | solution.py:598
  252.8 10.0 %collective-permute-start.52 = (bf16[192,768]{1,0:T(8,128)(2,1)S(1)}, bf16[192,768]{1,0:T(8,128)(2,1)S(1)}, u32[]{:S(2)}, u32[]{:S(2)}) collective-permute-start(bf16[192,768]{1,0:T(8,128)(2,1)S(1)} %slice_add_fusion.4), channel_id=1, source_target_pairs={{0,4},{2,6},{4,0},{6,2},{1,5},{3,7},{5,1},{7,3},{8,12},{10,14},{12... | collective-permute-start | bytes 884744 | tf_op jit(solution)/shard_map/ppermute | solution.py:598
  260.6 42.4 %collective-permute-start.59 = (bf16[192,512]{1,0:T(8,128)(2,1)S(1)}, bf16[192,512]{1,0:T(8,128)(2,1)S(1)}, u32[]{:S(2)}, u32[]{:S(2)}) collective-permute-start(bf16[192,512]{1,0:T(8,128)(2,1)S(1)} %get-tuple-element.226), channel_id=1, source_target_pairs={{0,2},{2,0},{4,6},{6,4},{1,3},{3,1},{5,7},{7,5},{8,10},{10,8},{12,... | collective-permute-start | bytes 589832 | tf_op jit(solution)/shard_map/ppermute | solution.py:598
  261.8 14.4 %collective-permute-start.65 = (bf16[192,384]{1,0:T(8,128)(2,1)S(1)}, bf16[192,384]{1,0:T(8,128)(2,1)S(1)}, u32[]{:S(2)}, u32[]{:S(2)}) collective-permute-start(bf16[192,384]{1,0:T(8,128)(2,1)S(1)} %add.150), channel_id=1, source_target_pairs={{0,8},{8,0},{16,24},{24,16},{1,9},{9,1},{17,25},{25,17},{2,10},{10... | collective-permute-start | bytes 442376 | tf_op jit(solution)/shard_map/ppermute | solution.py:598
  262.8 13.1 %collective-permute-start.54 = (bf16[192,384]{1,0:T(8,128)(2,1)S(1)}, bf16[192,384]{1,0:T(8,128)(2,1)S(1)}, u32[]{:S(2)}, u32[]{:S(2)}) collective-permute-start(bf16[192,384]{1,0:T(8,128)(2,1)S(1)} %add.147), channel_id=1, source_target_pairs={{0,16},{8,24},{16,0},{24,8},{1,17},{9,25},{17,1},{25,9},{2,18},{10... | collective-permute-start | bytes 442376 | tf_op jit(solution)/shard_map/ppermute | solution.py:598
  266.7 17.4 %collective-permute-start.55 = (bf16[400,384]{1,0:T(8,128)(2,1)S(1)}, bf16[400,384]{1,0:T(8,128)(2,1)S(1)}, u32[]{:S(2)}, u32[]{:S(2)}) collective-permute-start(bf16[400,384]{1,0:T(8,128)(2,1)S(1)} %get-tuple-element.248), channel_id=1, source_target_pairs={{0,8},{8,0},{16,24},{24,16},{1,9},{9,1},{17,25},{25,17},{2,10},{10... | collective-permute-start | bytes 921608 | tf_op jit(solution)/shard_map/ppermute | solution.py:598
  274.9 28.1 %collective-permute-start.60 = (bf16[192,512]{1,0:T(8,128)(2,1)S(1)}, bf16[192,512]{1,0:T(8,128)(2,1)S(1)}, u32[]{:S(2)}, u32[]{:S(2)}) collective-permute-start(bf16[192,512]{1,0:T(8,128)(2,1)S(1)} %get-tuple-element.228), channel_id=1, source_target_pairs={{0,4},{2,6},{4,0},{6,2},{1,5},{3,7},{5,1},{7,3},{8,12},{10,14},{12... | collective-permute-start | bytes 589832 | tf_op jit(solution)/shard_map/ppermute | solution.py:598
  275.9 10.1 %collective-permute-start.56 = (bf16[192,384]{1,0:T(8,128)(2,1)S(1)}, bf16[192,384]{1,0:T(8,128)(2,1)S(1)}, u32[]{:S(2)}, u32[]{:S(2)}) collective-permute-start(bf16[192,384]{1,0:T(8,128)(2,1)S(1)} %add.155), channel_id=1, source_target_pairs={{0,16},{8,24},{16,0},{24,8},{1,17},{9,25},{17,1},{25,9},{2,18},{10... | collective-permute-start | bytes 442376 | tf_op jit(solution)/shard_map/ppermute | solution.py:598
  276.2 12.1 %collective-permute-start.62 = (bf16[192,384]{1,0:T(8,128)(2,1)S(1)}, bf16[192,384]{1,0:T(8,128)(2,1)S(1)}, u32[]{:S(2)}, u32[]{:S(2)}) collective-permute-start(bf16[192,384]{1,0:T(8,128)(2,1)S(1)} %add.156), channel_id=1, source_target_pairs={{0,8},{8,0},{16,24},{24,16},{1,9},{9,1},{17,25},{25,17},{2,10},{10... | collective-permute-start | bytes 442376 | tf_op jit(solution)/shard_map/ppermute | solution.py:598
  284.1 15.9 %collective-permute-start.57 = (bf16[400,384]{1,0:T(8,128)(2,1)S(1)}, bf16[400,384]{1,0:T(8,128)(2,1)S(1)}, u32[]{:S(2)}, u32[]{:S(2)}) collective-permute-start(bf16[400,384]{1,0:T(8,128)(2,1)S(1)} %add.157), channel_id=1, source_target_pairs={{0,16},{8,24},{16,0},{24,8},{1,17},{9,25},{17,1},{25,9},{2,18},{10... | collective-permute-start | bytes 921608 | tf_op jit(solution)/shard_map/ppermute | solution.py:598
  286.0 17.0 %collective-permute-start.61 = (bf16[192,512]{1,0:T(8,128)(2,1)S(1)}, bf16[192,512]{1,0:T(8,128)(2,1)S(1)}, u32[]{:S(2)}, u32[]{:S(2)}) collective-permute-start(bf16[192,512]{1,0:T(8,128)(2,1)S(1)} %get-tuple-element.230), channel_id=1, source_target_pairs={{0,6},{2,4},{4,2},{6,0},{1,7},{3,5},{5,3},{7,1},{8,14},{10,12},{12... | collective-permute-start | bytes 589832 | tf_op jit(solution)/shard_map/ppermute | solution.py:598
  288.3 11.9 %collective-permute-start.63 = (bf16[192,384]{1,0:T(8,128)(2,1)S(1)}, bf16[192,384]{1,0:T(8,128)(2,1)S(1)}, u32[]{:S(2)}, u32[]{:S(2)}) collective-permute-start(bf16[192,384]{1,0:T(8,128)(2,1)S(1)} %add.158), channel_id=1, source_target_pairs={{0,8},{8,0},{16,24},{24,16},{1,9},{9,1},{17,25},{25,17},{2,10},{10... | collective-permute-start | bytes 442376 | tf_op jit(solution)/shard_map/ppermute | solution.py:598
  (112 other events, 848.4 us)
where the time goes:
time: 316 us; the launch traced here: 314 us
  waiting for transfers between devices  110 us (35%)
  Pallas kernels  107 us (34%)
  starting transfers between devices  58.4 us (18%)
  local copies, waits for them, and re-layouts  19.4 us (6%)
  other arithmetic  13.9 us (4%)
  between operations  5.06 us (2%)
    ppermute x66, waiting for transfers between devices, swap(): return lax.ppermute(value, axis, [(s, s ^ mask) for s in range(size)])  110 us
    pallas_call x22, Pallas kernels, call(): pl.pallas_call(body, out_shape=[make(s, d) for s, d in outs], scratch_sha...  107 us
    ppermute x66, starting transfers between devices, swap(): return lax.ppermute(value, axis, [(s, s ^ mask) for s in range(size)])  58.4 us
    unnamed x188, local copies, waits for them, and re-layouts  13.6 us
  transfers between devices with their start and end apart: 66, of which 25 were waited for; matrix products, arithmetic and copies ran while one was open for 4% of the time, Pallas kernels for 22%

commit v1 on v0

--- a/solution.py
+++ b/solution.py
@@ -729,17 +729,17 @@
     theirs = grad_theirs(after(x1, far), gu, hb, "up_theirs")
     got2 = swap(theirs, "row", 1)
     gq, sum_q = query_back(after(gn, theirs), kv, fq, uq, omegas, heads, head_width)
-    kept0, kept1, send0, send1 = grad_mine(after(x1, gq, gkv0), gu, got2, hb, "up_mine")
+    down0 = total(after(down[0][0], gq), down[0][1], r_down0)
+    z_down0 = Fold(down0)
+    kept0, kept1, send0, send1 = grad_mine(after(x1, down0, gkv0), gu, got2, hb, "up_mine")
     up = ((kept0, swap(send0, "col", 1)), (kept1, swap(send1, "col", 1)))
     far = far_half(after(down[1][0], send0), down[1][1])
     r_down1 = swap(far, "row", 2)
     gq = gq.reshape(2, hb, tokens)
     att2 = att.reshape(2, hb, tokens)
-    theirs = pair_theirs(after(x, far), gq, go, att2, "pair_theirs")
+    theirs = pair_theirs(after(x, far, gkv1), gq, go, att2, "pair_theirs")
     got3 = swap(theirs, "row", 1)
-    down0 = total(after(down[0][0], theirs), down[0][1], r_down0)
-    z_down0 = Fold(down0)
-    g, sum_kv = key_back(after(gkv0, down0), gkv1, fk, uk, v, omegas, heads, head_width)
+    g, sum_kv = key_back(after(gkv0, theirs), gkv1, fk, uk, v, omegas, heads, head_width)
     g = g.reshape(2, 2 * hb, tokens)
     sums = (sum1, sum2, bd, bu, sum_q, sum_kv)
     far = far_half(after(up[0][0], g), up[0][1])
@@ -748,14 +748,14 @@
     got4 = swap(theirs, "row", 1)
     keep3, send3 = pair_mine(after(x, theirs), gq, go, att2, got3, "pair_mine")
     r_y3 = swap(send3, "col", 1)
-    keep4, send4 = last_parts(after(x, send3), g, sums, got4, "last_mine")
+    far = far_half(after(up[1][0], send3), up[1][1])
+    r_up1 = swap(far, "row", 2)
+    keep4, send4 = last_parts(after(x, far), g, sums, got4, "last_mine")
     r_x4 = swap(send4, "row", 2)
     down1 = total(after(down[1][0], send4), down[1][1], r_down1)
     z_down1 = Fold(down1)
     order = z_down0.middle(down1)
-    far = far_half(after(up[1][0], order), up[1][1])
-    r_up1 = swap(far, "row", 2)
-    gin = input_grad(gq, g, after(go, far), near_a, other_a)
+    gin = input_grad(gq, g, after(go, order), near_a, other_a)
     far = far_half(after(keep4, gin[0]), r_x4)
     r_y4 = swap(far, "col", 1)
     up0 = total(after(up[0][0], far), up[0][1], r_up0)
@@ -765,12 +765,12 @@
     far = far_half(after(keep3, order), r_y3)
     r_x3 = swap(far, "row", 2)
     gin = exchange([after(gin[j], far) for j in (0, 2, 1, 3)])
-    order = z_up0.middle(far)
+    last = total(after(keep4, far), r_x4, r_y4)
+    order = z_up0.middle(last)
     up1 = total(after(up[1][0], order), up[1][1], r_up1)
     z_up1 = Fold(up1)
     order = z_down1.back(up1)
-    last = total(after(keep4, order), r_x4, r_y4)
-    last = jnp.concatenate((last, total(keep3, r_y3, r_x3)), axis=0)
+    last = jnp.concatenate((last, total(after(keep3, order), r_y3, r_x3)), axis=0)
     z_last = Fold(last)
     order = z_up1.middle(last)
     order = z_up0.back(order)

time: 316 us -> 321 us (1.016)
  waiting for transfers between devices: 110 us -> 117 us
    ppermute x66, waiting for transfers between devices: 110 us -> 117 us  [swap(): return lax.ppermute(value, axis, [(s, s ^ mask) for s in range(size)])]
    unnamed x188 -> x180, local copies, waits for them, and re-layouts: 13.6 us -> 13.4 us
  transfers between devices with their start and end apart: 66 -> 66, of which waited for: 25 -> 27; matrix products, arithmetic and copies ran while one was open for 4% -> 4% of each run, Pallas kernels for 22% -> 23%
where the time goes in v1:
time: 321 us; the launch traced here: 319 us
  waiting for transfers between devices  117 us (36%)
  Pallas kernels  108 us (34%)
  starting transfers between devices  57.8 us (18%)
  local copies, waits for them, and re-layouts  19.2 us (6%)
  other arithmetic  11.8 us (4%)
  between operations  4.99 us (2%)
    ppermute x66, waiting for transfers between devices, swap(): return lax.ppermute(value, axis, [(s, s ^ mask) for s in range(size)])  117 us
    pallas_call x22, Pallas kernels, call(): pl.pallas_call(body, out_shape=[make(s, d) for s, d in outs], scratch_sha...  108 us
    ppermute x66, starting transfers between devices, swap(): return lax.ppermute(value, axis, [(s, s ^ mask) for s in range(size)])  57.8 us
    unnamed x180, local copies, waits for them, and re-layouts  13.4 us
  transfers between devices with their start and end apart: 66, of which 27 were waited for; matrix products, arithmetic and copies ran while one was open for 4% of the time, Pallas kernels for 23%

profile of v1, /device:TPU:0, one launch (start us, length us, event | category | flops | bytes accessed | tf_op | source)
XLA Modules:
  0.0 319.1 jit_solution(4058552725998732304)
XLA Ops:
  2.0 2.4 split_positions.2
  4.4 2.1 narrow_a.1.refs_4_.refs_0_
  6.5 3.0 collective-permute-start.6
  16.0 2.6 collective-permute-start.14
  19.1 5.8 %collective-permute-done.7.refs_13_.om1_ref = bf16[6,64,256]{2,1,0:T(8,128)(2,1)S(1)} collective-permute-done((bf16[6,64,256]{2,1,0:T(8,128)(2,1)S(1)}, bf16[6,64,256]{2,1,0:T(8,128)(2,1)S(1)}, u32[]{:S(2)}, u32[]{:S(2)}) %collective-permute-start.7) | collective-permute-done | bytes 196640 | tf_op jit(solution)/shard_map/ppermute | solution.py:598
  28.9 3.6 %narrow_b.1.refs_4_.refs_14_.refs_24_.refs_0_ = bf16[192,3456]{1,0:T(8,128)(2,1)} custom-call(f32[192,384]{1,0:T(8,128)} %refs_0_.1, f32[192,1536]{1,0:T(8,128)} %refs_1_.3, f32[192,1536]{1,0:T(8,128)} %refs_2_.3), custom_call_target="tpu_custom_call" | custom-call | flops 1000 | bytes 1000 | tf_op jit(solution)/shard_map/narrow_b/pallas_call | solution.py:50
  34.7 5.3 %collective-permute-done.8.refs_9_.refs_5_ = bf16[208,1152]{1,0:T(8,128)(2,1)} collective-permute-done((bf16[208,1152]{1,0:T(8,128)(2,1)}, bf16[208,1152]{1,0:T(8,128)(2,1)}, u32[]{:S(2)}, u32[]{:S(2)}) %collective-permute-start.8) | collective-permute-done | bytes 479264 | tf_op jit(solution)/shard_map/ppermute | solution.py:598
  43.5 11.2 %attention_in.1 = (bf16[768,512]{1,0:T(8,128)(2,1)}, bf16[3072,512]{1,0:T(8,128)(2,1)}, bf16[3072,512]{1,0:T(8,128)(2,1)}, bf16[768,512]{1,0:T(8,128)(2,1)}, bf1...) custom-call(bf16[192,512]{1,0:T(8,128)(2,1)} %get-tuple-element.126., ...), custom_call_target="tpu_custom_call" | custom-call | flops 1000 | bytes 1000 | tf_op jit(solution)/shard_map/attention_in/pallas_call | solution.py:50
  54.8 1.8 collective-permute-done.11
  57.8 2.5 split_positions.3
  60.3 3.3 %collective-permute-done.15.refs_5_.refs_15_.refs_25_.refs_1_ = bf16[192,3456]{1,0:T(8,128)(2,1)S(1)} collective-permute-done((bf16[192,3456]{1,0:T(8,128)(2,1)}, bf16[192,3456]{1,0:T(8,128)(2,1)S(1)}, u32[]{:S(2)}, u32[]{:S(2)}) %collective-permute-start.15) | collective-permute-done | bytes 1327136 | tf_op jit(solution)/shard_map/ppermute | solution.py:598
  63.7 1.8 collective-permute-start.20
  65.7 1.8 collective-permute-start.21
  67.6 4.7 %collective-permute-done.18.refs_8_.refs_18_.refs_28_.refs_4_ = bf16[192,3456]{1,0:T(8,128)(2,1)S(1)} collective-permute-done((bf16[192,3456]{1,0:T(8,128)(2,1)}, bf16[192,3456]{1,0:T(8,128)(2,1)S(1)}, u32[]{:S(2)}, u32[]{:S(2)}) %collective-permute-start.18) | collective-permute-done | bytes 1327136 | tf_op jit(solution)/shard_map/ppermute | solution.py:598
  72.3 10.4 %collective-permute-done.21.refs_37_ = bf16[192,512]{1,0:T(8,128)(2,1)S(1)} collective-permute-done((bf16[192,512]{1,0:T(8,128)(2,1)S(1)}, bf16[192,512]{1,0:T(8,128)(2,1)S(1)}, u32[]{:S(2)}, u32[]{:S(2)}) %collective-permute-start.21) | collective-permute-done | bytes 196640 | tf_op jit(solution)/shard_map/ppermute | solution.py:598
  84.7 2.3 collective-permute-start.17
  87.1 5.1 %collective-permute-done.19.refs_9_.refs_19_.refs_29_.refs_5_ = bf16[48,3456]{1,0:T(8,128)(2,1)S(1)} collective-permute-done((bf16[48,3456]{1,0:T(8,128)(2,1)S(1)}, bf16[48,3456]{1,0:T(8,128)(2,1)S(1)}, u32[]{:S(2)}, u32[]{:S(2)}) %collective-permute-start.19) | collective-permute-done | bytes 331808 | tf_op jit(solution)/shard_map/ppermute | solution.py:598
  93.7 2.7 collective-permute-done.26.refs_38_
  98.6 21.2 %middle.1 = (bf16[864,256]{1,0:T(8,128)(2,1)}, bf16[768,512]{1,0:T(8,128)(2,1)}, f32[16,512]{1,0:T(8,128)}, bf16[768,512]{1,0:T(8,128)(2,1)}, f32[8,512]{1,0:T(8...) custom-call(bf16[864,256]{1,0:T(8,128)(2,1)} %copy-done.66, ...), custom_call_target="tpu_custom_call" | custom-call | flops 1000 | bytes 1000 | tf_op jit(solution)/shard_map/middle/pallas_call | solution.py:50
  121.0 1.9 copy-done.24
  122.9 2.8 down_theirs.1
  129.7 7.6 %down_back.1 = (bf16[2,1536,512]{2,1,0:T(8,128)(2,1)}, f32[2,8,1536]{2,1,0:T(8,128)S(1)}, f32[8,768]{1,0:T(8,128)S(1)}) custom-call(bf16[768,512]{1,0:T(8,128)(2,1)S(1)} %copy-done.23, bf16[2,1536,512]{2,1,0:T(8,128)(2,1)} %get-tuple-element.153.slope_ref, bf16[192,3456]{1,0:T(8,128)(2,1)S(1)} %copy-done.1, bf16[192,3456]{1,0:T(8,128)(2,1)S(1)} %copy-done.3, ...), custom_call_target="tpu_custom_call" | custom-call | flops 1000 | bytes 1000 | tf_op jit(solution)/shard_map/down_back/pallas_call | solution.py:50
  137.3 3.9 %down_mine.1 = (bf16[384,768]{1,0:T(8,128)(2,1)S(1)}, bf16[384,768]{1,0:T(8,128)(2,1)S(1)}, bf16[384,768]{1,0:T(8,128)(2,1)S(1)}, bf16[384,768]{1,0:T(8,128)(2,1)}) custom-call(bf16[768,512]{1,0:T(8,128)(2,1)S(1)} %copy-done.23, bf16[2,1536,512]{2,1,0:T(8,128)(2,1)S(1)} %copy-done.24, bf16[2,384,1536]{2,1,0:T(8,128)(2,1)S(1)} %collective-permute-done.27.got_ref), custom_call_target="tpu_custom_call" | custom-call | flops 1000 | bytes 1000 | tf_op jit(solution)/shard_map/down_mine/pallas_call | solution.py:50
  144.6 18.2 %up_back.1 = (bf16[768,512]{1,0:T(8,128)(2,1)S(1)}, f32[24,768]{1,0:T(8,128)S(1)}) custom-call(bf16[2,1536,512]{2,1,0:T(8,128)(2,1)} %get-tuple-element.158.gu_ref.r_ref, bf16[768,512]{1,0:T(8,128)(2,1)S(1)} %copy-done.23, bf16[768,512]{1,0:T(8,128)(2,1)S(1)} %copy-done.44, f32[8,512]{1,0:T(8,128)S(1)} %copy-done.65, f32[8,768]{1,0:T(8,128)S(1)} %copy-done.63, ...), custom_call_target="tpu_custom_call" | custom-call | flops 1000 | bytes 1000 | tf_op jit(solution)/shard_map/up_back/pallas_call | solution.py:50
  162.9 3.7 %attention_mid.1 = (bf16[864,512]{1,0:T(8,128)(2,1)S(1)}, bf16[864,256]{1,0:T(8,128)(2,1)S(1)}) custom-call(bf16[768,512]{1,0:T(8,128)(2,1)S(1)} %get-tuple-element.207.go_ref, bf16[768,512]{1,0:T(8,128)(2,1)S(1)} %copy-done.32, f32[16,512]{1,0:T(8,128)S(1)} %copy-done.64, bf16[3072,512]{1,0:T(8,128)(2,1)} %get-tuple-element.133.refs_2_.fq_ref, ...), custom_call_target="tpu_custom_call" | custom-call | flops 1000 | bytes 1000 | tf_op jit(solution)/shard_map/attention_mid/pallas_call | solution.py:50
  167.9 2.8 up_theirs.1
  172.2 3.8 %collective-permute-done.33 = bf16[864,256]{1,0:T(8,128)(2,1)S(1)} collective-permute-done((bf16[864,256]{1,0:T(8,128)(2,1)S(1)}, bf16[864,256]{1,0:T(8,128)(2,1)S(1)}, u32[]{:S(2)}, u32[]{:S(2)}) %collective-permute-start.33) | collective-permute-done | bytes 442400 | tf_op jit(solution)/shard_map/ppermute | solution.py:598
  176.2 2.8 query_back.1
  181.4 3.9 %up_mine.1 = (bf16[384,768]{1,0:T(8,128)(2,1)S(1)}, bf16[384,768]{1,0:T(8,128)(2,1)S(1)}, bf16[384,768]{1,0:T(8,128)(2,1)S(1)}, bf16[384,768]{1,0:T(8,128)(2,1)}) custom-call(bf16[768,512]{1,0:T(8,128)(2,1)S(1)} %copy-done.36, bf16[2,1536,512]{2,1,0:T(8,128)(2,1)S(1)} %copy-done.20, bf16[2,384,1536]{2,1,0:T(8,128)(2,1)S(1)} %collective-permute-done.34.got_ref), custom_call_target="tpu_custom_call" | custom-call | flops 1000 | bytes 1000 | tf_op jit(solution)/shard_map/up_mine/pallas_call | solution.py:50
  188.2 8.9 %collective-permute-done.36.gkv1_ref = bf16[864,256]{1,0:T(8,128)(2,1)S(1)} collective-permute-done((bf16[864,256]{1,0:T(8,128)(2,1)S(1)}, bf16[864,256]{1,0:T(8,128)(2,1)S(1)}, u32[]{:S(2)}, u32[]{:S(2)}) %collective-permute-start.36) | collective-permute-done | bytes 442400 | tf_op jit(solution)/shard_map/ppermute | solution.py:598
  197.1 2.0 pair_theirs.1
  199.6 3.6 %key_back.1 = (bf16[1536,512]{1,0:T(8,128)(2,1)S(1)}, f32[8,1536]{1,0:T(8,128)S(1)}) custom-call(bf16[864,256]{1,0:T(8,128)(2,1)S(1)} %add.134.gkv0_ref, bf16[864,256]{1,0:T(8,128)(2,1)S(1)} %collective-permute-done.36.gkv1_ref, bf16[3072,512]{1,0:T(8,128)(2,1)S(1)} %copy-done.37, bf16[768,512]{1,0:T(8,128)(2,1)S(1)} %copy-done.45, ...), custom_call_target="tpu_custom_call" | custom-call | flops 1000 | bytes 1000 | tf_op jit(solution)/shard_map/key_back/pallas_call | solution.py:50
  204.1 2.2 last_theirs.1
  211.9 2.3 pair_mine.1
  214.2 8.1 %collective-permute-done.39 = bf16[384,768]{1,0:T(8,128)(2,1)} collective-permute-done((bf16[384,768]{1,0:T(8,128)(2,1)}, bf16[384,768]{1,0:T(8,128)(2,1)}, u32[]{:S(2)}, u32[]{:S(2)}) %collective-permute-start.39) | collective-permute-done | bytes 589856 | tf_op jit(solution)/shard_map/ppermute | solution.py:598
  223.4 2.6 last_mine.1
  226.6 1.8 collective-permute-start.42
  232.1 2.6 collective-permute-start.46
  234.7 3.9 %input_grad.1 = (bf16[192,512]{1,0:T(8,128)(2,1)S(1)}, bf16[192,512]{1,0:T(8,128)(2,1)S(1)}, bf16[192,512]{1,0:T(8,128)(2,1)S(1)}, bf16[192,512]{1,0:T(8,128)(2,1)S(1)}) custom-call(bf16[2,384,512]{2,1,0:T(8,128)(2,1)S(1)} %bitcast.23, bf16[2,768,512]{2,1,0:T(8,128)(2,1)S(1)} %bitcast.20, bf16[768,512]{1,0:T(8,128)(2,1)S(1)} %get-tuple-element.207.go_ref, ...), custom_call_target="tpu_custom_call" | custom-call | flops 1000 | bytes 1000 | tf_op jit(solution)/shard_map/input_grad/pallas_call | solution.py:50
  238.6 4.7 %collective-permute-done.43 = bf16[416,768]{1,0:T(8,128)(2,1)S(1)} collective-permute-done((bf16[416,768]{1,0:T(8,128)(2,1)S(1)}, bf16[416,768]{1,0:T(8,128)(2,1)S(1)}, u32[]{:S(2)}, u32[]{:S(2)}) %collective-permute-start.43) | collective-permute-done | bytes 639008 | tf_op jit(solution)/shard_map/ppermute | solution.py:598
  245.0 4.7 %collective-permute-done.44 = bf16[192,768]{1,0:T(8,128)(2,1)S(1)} collective-permute-done((bf16[192,768]{1,0:T(8,128)(2,1)S(1)}, bf16[192,768]{1,0:T(8,128)(2,1)S(1)}, u32[]{:S(2)}, u32[]{:S(2)}) %collective-permute-start.44) | collective-permute-done | bytes 294944 | tf_op jit(solution)/shard_map/ppermute | solution.py:598
  249.8 2.7 collective-permute-start.51
  256.3 3.1 collective-permute-done.48
  261.1 3.5 %collective-permute-done.49 = bf16[192,384]{1,0:T(8,128)(2,1)S(1)} collective-permute-done((bf16[192,384]{1,0:T(8,128)(2,1)S(1)}, bf16[192,384]{1,0:T(8,128)(2,1)S(1)}, u32[]{:S(2)}, u32[]{:S(2)}) %collective-permute-start.49) | collective-permute-done | bytes 147488 | tf_op jit(solution)/shard_map/ppermute | solution.py:598
  270.2 8.7 %collective-permute-done.53 = bf16[192,384]{1,0:T(8,128)(2,1)S(1)} collective-permute-done((bf16[192,384]{1,0:T(8,128)(2,1)S(1)}, bf16[192,384]{1,0:T(8,128)(2,1)S(1)}, u32[]{:S(2)}, u32[]{:S(2)}) %collective-permute-start.53) | collective-permute-done | bytes 147488 | tf_op jit(solution)/shard_map/ppermute | solution.py:598
  281.5 7.1 %collective-permute-done.55 = bf16[400,384]{1,0:T(8,128)(2,1)S(1)} collective-permute-done((bf16[400,384]{1,0:T(8,128)(2,1)S(1)}, bf16[400,384]{1,0:T(8,128)(2,1)S(1)}, u32[]{:S(2)}, u32[]{:S(2)}) %collective-permute-start.55) | collective-permute-done | bytes 307232 | tf_op jit(solution)/shard_map/ppermute | solution.py:598
  292.3 12.1 %collective-permute-done.57 = bf16[400,384]{1,0:T(8,128)(2,1)S(1)} collective-permute-done((bf16[400,384]{1,0:T(8,128)(2,1)S(1)}, bf16[400,384]{1,0:T(8,128)(2,1)S(1)}, u32[]{:S(2)}, u32[]{:S(2)}) %collective-permute-start.57) | collective-permute-done | bytes 307232 | tf_op jit(solution)/shard_map/ppermute | solution.py:598
  309.3 4.3 %collective-permute-done.58 = bf16[400,384]{1,0:T(8,128)(2,1)S(1)} collective-permute-done((bf16[400,384]{1,0:T(8,128)(2,1)S(1)}, bf16[400,384]{1,0:T(8,128)(2,1)S(1)}, u32[]{:S(2)}, u32[]{:S(2)}) %collective-permute-start.58) | collective-permute-done | bytes 307232 | tf_op jit(solution)/shard_map/ppermute | solution.py:598
  (340 shorter events, 80.3 us)
Async XLA Ops:
  6.5 18.7 %collective-permute-start.6 = (bf16[208,1152]{1,0:T(8,128)(2,1)}, bf16[208,1152]{1,0:T(8,128)(2,1)S(1)}, u32[]{:S(2)}, u32[]{:S(2)}) collective-permute-start(bf16[208,1152]{1,0:T(8,128)(2,1)} %narrow_a.1.refs_4_.refs_0_), channel_id=1, source_target_pairs={{0,1},{1,0},{2,3},{3,2},{4,5},{5,4},{6,7},{7,6},{8,9},{9,8},{10,11... | collective-permute-start | bytes 1437704 | tf_op jit(solution)/shard_map/ppermute | solution.py:598
  9.5 17.2 %collective-permute-start.3 = (bf16[208,1152]{1,0:T(8,128)(2,1)}, bf16[208,1152]{1,0:T(8,128)(2,1)}, u32[]{:S(2)}, u32[]{:S(2)}) collective-permute-start(bf16[208,1152]{1,0:T(8,128)(2,1)} %narrow_a.1.refs_4_.refs_0_), channel_id=1, source_target_pairs={{0,4},{2,6},{4,0},{6,2},{1,5},{3,7},{5,1},{7,3},{8,12},{10,14},{12... | collective-permute-start | bytes 1437704 | tf_op jit(solution)/shard_map/ppermute | solution.py:598
  13.9 10.9 %collective-permute-start.7 = (bf16[6,64,256]{2,1,0:T(8,128)(2,1)S(1)}, bf16[6,64,256]{2,1,0:T(8,128)(2,1)S(1)}, u32[]{:S(2)}, u32[]{:S(2)}) collective-permute-start(bf16[6,64,256]{2,1,0:T(8,128)(2,1)S(1)} %copy-done.40), channel_id=1, source_target_pairs={{0,1},{1,0},{2,3},{3,2},{4,5},{5,4},{6,7},{7,6},{8,9},{9,8},{10,11... | collective-permute-start | bytes 589832 | tf_op jit(solution)/shard_map/ppermute | solution.py:598
  16.0 12.3 %collective-permute-start.14 = (f32[8,128]{1,0:T(8,128)S(1)}, f32[8,128]{1,0:T(8,128)S(1)}, u32[]{:S(2)}, u32[]{:S(2)}) collective-permute-start(f32[8,128]{1,0:T(8,128)S(1)} %broadcast_add_fusion), channel_id=1, source_target_pairs={{0,16},{8,24},{16,0},{24,8},{1,17},{9,25},{17,1},{25,9},{2,18},{10... | collective-permute-start | bytes 12296 | tf_op jit(solution)/shard_map/ppermute | solution.py:598
  18.6 13.9 %collective-permute-start = (bf16[192,512]{1,0:T(8,128)(2,1)S(1)}, bf16[192,512]{1,0:T(8,128)(2,1)S(1)}, u32[]{:S(2)}, u32[]{:S(2)}) collective-permute-start(bf16[192,512]{1,0:T(8,128)(2,1)S(1)} %copy-done.86), channel_id=1, source_target_pairs={{0,4},{2,6},{4,0},{6,2},{1,5},{3,7},{5,1},{7,3},{8,12},{10,14},{12... | collective-permute-start | bytes 589832 | tf_op jit(solution)/shard_map/ppermute | solution.py:598
  25.2 14.8 %collective-permute-start.4 = (bf16[208,1152]{1,0:T(8,128)(2,1)}, bf16[208,1152]{1,0:T(8,128)(2,1)}, u32[]{:S(2)}, u32[]{:S(2)}) collective-permute-start(bf16[208,1152]{1,0:T(8,128)(2,1)} %narrow_a.1.refs_4_.refs_0_), channel_id=1, source_target_pairs={{0,2},{2,0},{4,6},{6,4},{1,3},{3,1},{5,7},{7,5},{8,10},{10,8},{12,... | collective-permute-start | bytes 1437704 | tf_op jit(solution)/shard_map/ppermute | solution.py:598
  26.7 13.3 %collective-permute-start.8 = (bf16[208,1152]{1,0:T(8,128)(2,1)}, bf16[208,1152]{1,0:T(8,128)(2,1)}, u32[]{:S(2)}, u32[]{:S(2)}) collective-permute-start(bf16[208,1152]{1,0:T(8,128)(2,1)} %collective-permute-done.3.refs_5_.refs_1_), channel_id=1, source_target_pairs={{0,1},{1,0},{2,3},{3,2},{4,5},{5,4},{6,7},{7,6},{8,9},{9,8},{10,11... | collective-permute-start | bytes 1437704 | tf_op jit(solution)/shard_map/ppermute | solution.py:598
  32.5 31.1 %collective-permute-start.15 = (bf16[192,3456]{1,0:T(8,128)(2,1)}, bf16[192,3456]{1,0:T(8,128)(2,1)S(1)}, u32[]{:S(2)}, u32[]{:S(2)}) collective-permute-start(bf16[192,3456]{1,0:T(8,128)(2,1)} %narrow_b.1.refs_4_.refs_14_.refs_24_.refs_0_), channel_id=1, source_target_pairs={{0,4},{2,6},{4,0},{6,2},{1,5},{3,7},{5,1},{7,3},{8,12},{10,14},{12... | collective-permute-start | bytes 3981320 | tf_op jit(solution)/shard_map/ppermute | solution.py:598
  33.1 9.7 %collective-permute-start.9 = (bf16[208,1152]{1,0:T(8,128)(2,1)S(1)}, bf16[208,1152]{1,0:T(8,128)(2,1)}, u32[]{:S(2)}, u32[]{:S(2)}) collective-permute-start(bf16[208,1152]{1,0:T(8,128)(2,1)S(1)} %collective-permute-done.6.refs_8_.refs_4_), channel_id=1, source_target_pairs={{0,2},{2,0},{4,6},{6,4},{1,3},{3,1},{5,7},{7,5},{8,10},{10,8},{12,... | collective-permute-start | bytes 1437704 | tf_op jit(solution)/shard_map/ppermute | solution.py:598
  40.0 32.3 %collective-permute-start.18 = (bf16[192,3456]{1,0:T(8,128)(2,1)}, bf16[192,3456]{1,0:T(8,128)(2,1)S(1)}, u32[]{:S(2)}, u32[]{:S(2)}) collective-permute-start(bf16[192,3456]{1,0:T(8,128)(2,1)} %narrow_b.1.refs_4_.refs_14_.refs_24_.refs_0_), channel_id=1, source_target_pairs={{0,1},{1,0},{2,3},{3,2},{4,5},{5,4},{6,7},{7,6},{8,9},{9,8},{10,11... | collective-permute-start | bytes 3981320 | tf_op jit(solution)/shard_map/ppermute | solution.py:598
  63.7 29.4 %collective-permute-start.20 = (bf16[144,3456]{1,0:T(8,128)(2,1)S(1)}, bf16[144,3456]{1,0:T(8,128)(2,1)S(1)}, u32[]{:S(2)}, u32[]{:S(2)}) collective-permute-start(bf16[144,3456]{1,0:T(8,128)(2,1)S(1)} %slice.182), channel_id=1, source_target_pairs={{0,1},{1,0},{2,3},{3,2},{4,5},{5,4},{6,7},{7,6},{8,9},{9,8},{10,11... | collective-permute-start | bytes 2985992 | tf_op jit(solution)/shard_map/ppermute | solution.py:598
  65.5 21.6 %collective-permute-start.12 = (bf16[864,256]{1,0:T(8,128)(2,1)S(1)}, bf16[864,256]{1,0:T(8,128)(2,1)S(1)}, u32[]{:S(2)}, u32[]{:S(2)}) collective-permute-start(bf16[864,256]{1,0:T(8,128)(2,1)S(1)} %add.126.refs_0_), channel_id=1, source_target_pairs={{0,4},{2,6},{4,0},{6,2},{1,5},{3,7},{5,1},{7,3},{8,12},{10,14},{12... | collective-permute-start | bytes 1327112 | tf_op jit(solution)/shard_map/ppermute | solution.py:598
  65.7 27.9 %collective-permute-start.16 = (bf16[192,3456]{1,0:T(8,128)(2,1)S(1)}, bf16[192,3456]{1,0:T(8,128)(2,1)S(1)}, u32[]{:S(2)}, u32[]{:S(2)}) collective-permute-start(bf16[192,3456]{1,0:T(8,128)(2,1)S(1)} %copy-done), channel_id=1, source_target_pairs={{0,2},{2,0},{4,6},{6,4},{1,3},{3,1},{5,7},{7,5},{8,10},{10,8},{12,... | collective-permute-start | bytes 3981320 | tf_op jit(solution)/shard_map/ppermute | solution.py:598
  65.7 17.0 %collective-permute-start.21 = (bf16[192,512]{1,0:T(8,128)(2,1)S(1)}, bf16[192,512]{1,0:T(8,128)(2,1)S(1)}, u32[]{:S(2)}, u32[]{:S(2)}) collective-permute-start(bf16[192,512]{1,0:T(8,128)(2,1)S(1)} %copy-done.88), channel_id=1, source_target_pairs={{0,4},{2,6},{4,0},{6,2},{1,5},{3,7},{5,1},{7,3},{8,12},{10,14},{12... | collective-permute-start | bytes 589832 | tf_op jit(solution)/shard_map/ppermute | solution.py:598
  72.3 12.4 %collective-permute-start.22 = (bf16[192,512]{1,0:T(8,128)(2,1)S(1)}, bf16[192,512]{1,0:T(8,128)(2,1)S(1)}, u32[]{:S(2)}, u32[]{:S(2)}) collective-permute-start(bf16[192,512]{1,0:T(8,128)(2,1)S(1)} %copy-done.87), channel_id=1, source_target_pairs={{0,6},{2,4},{4,2},{6,0},{1,7},{3,5},{5,3},{7,1},{8,14},{10,12},{12... | collective-permute-start | bytes 589832 | tf_op jit(solution)/shard_map/ppermute | solution.py:598
  84.7 11.7 %collective-permute-start.17 = (bf16[192,3456]{1,0:T(8,128)(2,1)S(1)}, bf16[192,3456]{1,0:T(8,128)(2,1)S(1)}, u32[]{:S(2)}, u32[]{:S(2)}) collective-permute-start(bf16[192,3456]{1,0:T(8,128)(2,1)S(1)} %collective-permute-done.15.refs_5_.refs_15_.refs_25_.refs_1_), channel_id=1, source_target_pairs={{0,2},{2,0},{4,6},{6,4},{1,3},{3,1},{5,7},{7,5},{8,10},{10,8},{12,... | collective-permute-start | bytes 3981320 | tf_op jit(solution)/shard_map/ppermute | solution.py:598
  125.7 11.6 %collective-permute-start.27 = (bf16[2,384,1536]{2,1,0:T(8,128)(2,1)S(1)}, bf16[2,384,1536]{2,1,0:T(8,128)(2,1)S(1)}, u32[]{:S(2)}, u32[]{:S(2)}) collective-permute-start(bf16[2,384,1536]{2,1,0:T(8,128)(2,1)S(1)} %down_theirs.1), channel_id=1, source_target_pairs={{0,2},{2,0},{4,6},{6,4},{1,3},{3,1},{5,7},{7,5},{8,10},{10,8},{12,... | collective-permute-start | bytes 7077896 | tf_op jit(solution)/shard_map/ppermute | solution.py:598
  141.2 25.5 %collective-permute-start.31 = (bf16[384,768]{1,0:T(8,128)(2,1)S(1)}, bf16[384,768]{1,0:T(8,128)(2,1)S(1)}, u32[]{:S(2)}, u32[]{:S(2)}) collective-permute-start(bf16[384,768]{1,0:T(8,128)(2,1)S(1)} %get-tuple-element.157), channel_id=1, source_target_pairs={{0,1},{1,0},{2,3},{3,2},{4,5},{5,4},{6,7},{7,6},{8,9},{9,8},{10,11... | collective-permute-start | bytes 1769480 | tf_op jit(solution)/shard_map/ppermute | solution.py:598
  142.7 23.9 %collective-permute-start.28 = (bf16[192,512]{1,0:T(8,128)(2,1)S(1)}, bf16[192,512]{1,0:T(8,128)(2,1)S(1)}, u32[]{:S(2)}, u32[]{:S(2)}) collective-permute-start(bf16[192,512]{1,0:T(8,128)(2,1)S(1)} %copy-done.84), channel_id=1, source_target_pairs={{0,2},{2,0},{4,6},{6,4},{1,3},{3,1},{5,7},{7,5},{8,10},{10,8},{12,... | collective-permute-start | bytes 589832 | tf_op jit(solution)/shard_map/ppermute | solution.py:598
  142.8 23.8 %collective-permute-start.29 = (bf16[192,512]{1,0:T(8,128)(2,1)S(1)}, bf16[192,512]{1,0:T(8,128)(2,1)S(1)}, u32[]{:S(2)}, u32[]{:S(2)}) collective-permute-start(bf16[192,512]{1,0:T(8,128)(2,1)S(1)} %copy-done.82), channel_id=1, source_target_pairs={{0,4},{2,6},{4,0},{6,2},{1,5},{3,7},{5,1},{7,3},{8,12},{10,14},{12... | collective-permute-start | bytes 589832 | tf_op jit(solution)/shard_map/ppermute | solution.py:598
  143.3 23.3 %collective-permute-start.30 = (bf16[192,512]{1,0:T(8,128)(2,1)S(1)}, bf16[192,512]{1,0:T(8,128)(2,1)S(1)}, u32[]{:S(2)}, u32[]{:S(2)}) collective-permute-start(bf16[192,512]{1,0:T(8,128)(2,1)S(1)} %copy-done.81), channel_id=1, source_target_pairs={{0,6},{2,4},{4,2},{6,0},{1,7},{3,5},{5,3},{7,1},{8,14},{10,12},{12... | collective-permute-start | bytes 589832 | tf_op jit(solution)/shard_map/ppermute | solution.py:598
  170.8 10.6 %collective-permute-start.34 = (bf16[2,384,1536]{2,1,0:T(8,128)(2,1)S(1)}, bf16[2,384,1536]{2,1,0:T(8,128)(2,1)S(1)}, u32[]{:S(2)}, u32[]{:S(2)}) collective-permute-start(bf16[2,384,1536]{2,1,0:T(8,128)(2,1)S(1)} %up_theirs.1), channel_id=1, source_target_pairs={{0,2},{2,0},{4,6},{6,4},{1,3},{3,1},{5,7},{7,5},{8,10},{10,8},{12,... | collective-permute-start | bytes 7077896 | tf_op jit(solution)/shard_map/ppermute | solution.py:598
  171.9 15.6 %collective-permute-start.35 = (bf16[384,768]{1,0:T(8,128)(2,1)}, bf16[384,768]{1,0:T(8,128)(2,1)S(1)}, u32[]{:S(2)}, u32[]{:S(2)}) collective-permute-start(bf16[384,768]{1,0:T(8,128)(2,1)} %get-tuple-element.182), channel_id=1, source_target_pairs={{0,1},{1,0},{2,3},{3,2},{4,5},{5,4},{6,7},{7,6},{8,9},{9,8},{10,11... | collective-permute-start | bytes 1769480 | tf_op jit(solution)/shard_map/ppermute | solution.py:598
  185.3 18.0 %collective-permute-start.37 = (bf16[384,768]{1,0:T(8,128)(2,1)S(1)}, bf16[384,768]{1,0:T(8,128)(2,1)S(1)}, u32[]{:S(2)}, u32[]{:S(2)}) collective-permute-start(bf16[384,768]{1,0:T(8,128)(2,1)S(1)} %get-tuple-element.180), channel_id=1, source_target_pairs={{0,1},{1,0},{2,3},{3,2},{4,5},{5,4},{6,7},{7,6},{8,9},{9,8},{10,11... | collective-permute-start | bytes 1769480 | tf_op jit(solution)/shard_map/ppermute | solution.py:598
  185.8 11.3 %collective-permute-start.36 = (bf16[864,256]{1,0:T(8,128)(2,1)S(1)}, bf16[864,256]{1,0:T(8,128)(2,1)S(1)}, u32[]{:S(2)}, u32[]{:S(2)}) collective-permute-start(bf16[864,256]{1,0:T(8,128)(2,1)S(1)} %add.134.gkv0_ref), channel_id=1, source_target_pairs={{0,4},{2,6},{4,0},{6,2},{1,5},{3,7},{5,1},{7,3},{8,12},{10,14},{12... | collective-permute-start | bytes 1327112 | tf_op jit(solution)/shard_map/ppermute | solution.py:598
  199.1 10.5 %collective-permute-start.38 = (bf16[2,384,768]{2,1,0:T(8,128)(2,1)}, bf16[2,384,768]{2,1,0:T(8,128)(2,1)}, u32[]{:S(2)}, u32[]{:S(2)}) collective-permute-start(bf16[2,384,768]{2,1,0:T(8,128)(2,1)} %pair_theirs.1), channel_id=1, source_target_pairs={{0,2},{2,0},{4,6},{6,4},{1,3},{3,1},{5,7},{7,5},{8,10},{10,8},{12,... | collective-permute-start | bytes 3538952 | tf_op jit(solution)/shard_map/ppermute | solution.py:598
  206.3 17.1 %collective-permute-start.40 = (bf16[2,2,208,768]{3,2,1,0:T(8,128)(2,1)}, bf16[2,2,208,768]{3,2,1,0:T(8,128)(2,1)}, u32[]{:S(2)}, u32[]{:S(2)}) collective-permute-start(bf16[2,2,208,768]{3,2,1,0:T(8,128)(2,1)} %last_theirs.1), channel_id=1, source_target_pairs={{0,2},{2,0},{4,6},{6,4},{1,3},{3,1},{5,7},{7,5},{8,10},{10,8},{12,... | collective-permute-start | bytes 3833864 | tf_op jit(solution)/shard_map/ppermute | solution.py:598
  206.4 16.0 %collective-permute-start.39 = (bf16[384,768]{1,0:T(8,128)(2,1)}, bf16[384,768]{1,0:T(8,128)(2,1)}, u32[]{:S(2)}, u32[]{:S(2)}) collective-permute-start(bf16[384,768]{1,0:T(8,128)(2,1)} %get-tuple-element.200), channel_id=1, source_target_pairs={{0,1},{1,0},{2,3},{3,2},{4,5},{5,4},{6,7},{7,6},{8,9},{9,8},{10,11... | collective-permute-start | bytes 1769480 | tf_op jit(solution)/shard_map/ppermute | solution.py:598
  209.0 21.3 %collective-permute-start.41 = (bf16[192,768]{1,0:T(8,128)(2,1)}, bf16[192,768]{1,0:T(8,128)(2,1)S(1)}, u32[]{:S(2)}, u32[]{:S(2)}) collective-permute-start(bf16[192,768]{1,0:T(8,128)(2,1)} %slice_add_fusion.9), channel_id=1, source_target_pairs={{0,4},{2,6},{4,0},{6,2},{1,5},{3,7},{5,1},{7,3},{8,12},{10,14},{12... | collective-permute-start | bytes 884744 | tf_op jit(solution)/shard_map/ppermute | solution.py:598
  226.1 17.3 %collective-permute-start.43 = (bf16[416,768]{1,0:T(8,128)(2,1)S(1)}, bf16[416,768]{1,0:T(8,128)(2,1)S(1)}, u32[]{:S(2)}, u32[]{:S(2)}) collective-permute-start(bf16[416,768]{1,0:T(8,128)(2,1)S(1)} %get-tuple-element.204), channel_id=1, source_target_pairs={{0,4},{2,6},{4,0},{6,2},{1,5},{3,7},{5,1},{7,3},{8,12},{10,14},{12... | collective-permute-start | bytes 1916936 | tf_op jit(solution)/shard_map/ppermute | solution.py:598
  228.3 21.4 %collective-permute-start.44 = (bf16[192,768]{1,0:T(8,128)(2,1)S(1)}, bf16[192,768]{1,0:T(8,128)(2,1)S(1)}, u32[]{:S(2)}, u32[]{:S(2)}) collective-permute-start(bf16[192,768]{1,0:T(8,128)(2,1)S(1)} %copy-done.73), channel_id=1, source_target_pairs={{0,4},{2,6},{4,0},{6,2},{1,5},{3,7},{5,1},{7,3},{8,12},{10,14},{12... | collective-permute-start | bytes 884744 | tf_op jit(solution)/shard_map/ppermute | solution.py:598
  229.8 34.8 %collective-permute-start.50 = (bf16[192,768]{1,0:T(8,128)(2,1)S(1)}, bf16[192,768]{1,0:T(8,128)(2,1)S(1)}, u32[]{:S(2)}, u32[]{:S(2)}) collective-permute-start(bf16[192,768]{1,0:T(8,128)(2,1)S(1)} %slice_add_fusion.7), channel_id=1, source_target_pairs={{0,4},{2,6},{4,0},{6,2},{1,5},{3,7},{5,1},{7,3},{8,12},{10,14},{12... | collective-permute-start | bytes 884744 | tf_op jit(solution)/shard_map/ppermute | solution.py:598
  230.3 25.3 %collective-permute-start.47 = (bf16[384,768]{1,0:T(8,128)(2,1)S(1)}, bf16[384,768]{1,0:T(8,128)(2,1)S(1)}, u32[]{:S(2)}, u32[]{:S(2)}) collective-permute-start(bf16[384,768]{1,0:T(8,128)(2,1)S(1)} %get-tuple-element.198), channel_id=1, source_target_pairs={{0,1},{1,0},{2,3},{3,2},{4,5},{5,4},{6,7},{7,6},{8,9},{9,8},{10,11... | collective-permute-start | bytes 1769480 | tf_op jit(solution)/shard_map/ppermute | solution.py:598
  232.1 21.9 %collective-permute-start.46 = (bf16[192,384]{1,0:T(8,128)(2,1)S(1)}, bf16[192,384]{1,0:T(8,128)(2,1)S(1)}, u32[]{:S(2)}, u32[]{:S(2)}) collective-permute-start(bf16[192,384]{1,0:T(8,128)(2,1)S(1)} %add.140), channel_id=1, source_target_pairs={{0,16},{8,24},{16,0},{24,8},{1,17},{9,25},{17,1},{25,9},{2,18},{10... | collective-permute-start | bytes 442376 | tf_op jit(solution)/shard_map/ppermute | solution.py:598
  249.8 15.9 %collective-permute-start.51 = (bf16[192,384]{1,0:T(8,128)(2,1)S(1)}, bf16[192,384]{1,0:T(8,128)(2,1)S(1)}, u32[]{:S(2)}, u32[]{:S(2)}) collective-permute-start(bf16[192,384]{1,0:T(8,128)(2,1)S(1)} %add.144), channel_id=1, source_target_pairs={{0,16},{8,24},{16,0},{24,8},{1,17},{9,25},{17,1},{25,9},{2,18},{10... | collective-permute-start | bytes 442376 | tf_op jit(solution)/shard_map/ppermute | solution.py:598
  254.0 14.4 %collective-permute-start.64 = (bf16[192,384]{1,0:T(8,128)(2,1)S(1)}, bf16[192,384]{1,0:T(8,128)(2,1)S(1)}, u32[]{:S(2)}, u32[]{:S(2)}) collective-permute-start(bf16[192,384]{1,0:T(8,128)(2,1)S(1)} %add.145), channel_id=1, source_target_pairs={{0,8},{8,0},{16,24},{24,16},{1,9},{9,1},{17,25},{25,17},{2,10},{10... | collective-permute-start | bytes 442376 | tf_op jit(solution)/shard_map/ppermute | solution.py:598
  255.8 12.0 %collective-permute-start.52 = (bf16[192,768]{1,0:T(8,128)(2,1)S(1)}, bf16[192,768]{1,0:T(8,128)(2,1)S(1)}, u32[]{:S(2)}, u32[]{:S(2)}) collective-permute-start(bf16[192,768]{1,0:T(8,128)(2,1)S(1)} %slice_add_fusion.4), channel_id=1, source_target_pairs={{0,4},{2,6},{4,0},{6,2},{1,5},{3,7},{5,1},{7,3},{8,12},{10,14},{12... | collective-permute-start | bytes 884744 | tf_op jit(solution)/shard_map/ppermute | solution.py:598
  264.6 43.5 %collective-permute-start.59 = (bf16[192,512]{1,0:T(8,128)(2,1)S(1)}, bf16[192,512]{1,0:T(8,128)(2,1)S(1)}, u32[]{:S(2)}, u32[]{:S(2)}) collective-permute-start(bf16[192,512]{1,0:T(8,128)(2,1)S(1)} %get-tuple-element.228), channel_id=1, source_target_pairs={{0,2},{2,0},{4,6},{6,4},{1,3},{3,1},{5,7},{7,5},{8,10},{10,8},{12,... | collective-permute-start | bytes 589832 | tf_op jit(solution)/shard_map/ppermute | solution.py:598
  265.7 15.4 %collective-permute-start.65 = (bf16[192,384]{1,0:T(8,128)(2,1)S(1)}, bf16[192,384]{1,0:T(8,128)(2,1)S(1)}, u32[]{:S(2)}, u32[]{:S(2)}) collective-permute-start(bf16[192,384]{1,0:T(8,128)(2,1)S(1)} %add.152), channel_id=1, source_target_pairs={{0,8},{8,0},{16,24},{24,16},{1,9},{9,1},{17,25},{25,17},{2,10},{10... | collective-permute-start | bytes 442376 | tf_op jit(solution)/shard_map/ppermute | solution.py:598
  267.4 12.0 %collective-permute-start.54 = (bf16[192,384]{1,0:T(8,128)(2,1)S(1)}, bf16[192,384]{1,0:T(8,128)(2,1)S(1)}, u32[]{:S(2)}, u32[]{:S(2)}) collective-permute-start(bf16[192,384]{1,0:T(8,128)(2,1)S(1)} %add.149), channel_id=1, source_target_pairs={{0,16},{8,24},{16,0},{24,8},{1,17},{9,25},{17,1},{25,9},{2,18},{10... | collective-permute-start | bytes 442376 | tf_op jit(solution)/shard_map/ppermute | solution.py:598
  267.8 11.1 %collective-permute-start.53 = (bf16[192,384]{1,0:T(8,128)(2,1)S(1)}, bf16[192,384]{1,0:T(8,128)(2,1)S(1)}, u32[]{:S(2)}, u32[]{:S(2)}) collective-permute-start(bf16[192,384]{1,0:T(8,128)(2,1)S(1)} %get-tuple-element.260), channel_id=1, source_target_pairs={{0,8},{8,0},{16,24},{24,16},{1,9},{9,1},{17,25},{25,17},{2,10},{10... | collective-permute-start | bytes 442376 | tf_op jit(solution)/shard_map/ppermute | solution.py:598
  268.5 20.1 %collective-permute-start.55 = (bf16[400,384]{1,0:T(8,128)(2,1)S(1)}, bf16[400,384]{1,0:T(8,128)(2,1)S(1)}, u32[]{:S(2)}, u32[]{:S(2)}) collective-permute-start(bf16[400,384]{1,0:T(8,128)(2,1)S(1)} %get-tuple-element.250), channel_id=1, source_target_pairs={{0,8},{8,0},{16,24},{24,16},{1,9},{9,1},{17,25},{25,17},{2,10},{10... | collective-permute-start | bytes 921608 | tf_op jit(solution)/shard_map/ppermute | solution.py:598
  278.8 29.2 %collective-permute-start.60 = (bf16[192,512]{1,0:T(8,128)(2,1)S(1)}, bf16[192,512]{1,0:T(8,128)(2,1)S(1)}, u32[]{:S(2)}, u32[]{:S(2)}) collective-permute-start(bf16[192,512]{1,0:T(8,128)(2,1)S(1)} %get-tuple-element.230), channel_id=1, source_target_pairs={{0,4},{2,6},{4,0},{6,2},{1,5},{3,7},{5,1},{7,3},{8,12},{10,14},{12... | collective-permute-start | bytes 589832 | tf_op jit(solution)/shard_map/ppermute | solution.py:598
  279.4 11.8 %collective-permute-start.62 = (bf16[192,384]{1,0:T(8,128)(2,1)S(1)}, bf16[192,384]{1,0:T(8,128)(2,1)S(1)}, u32[]{:S(2)}, u32[]{:S(2)}) collective-permute-start(bf16[192,384]{1,0:T(8,128)(2,1)S(1)} %add.156), channel_id=1, source_target_pairs={{0,8},{8,0},{16,24},{24,16},{1,9},{9,1},{17,25},{25,17},{2,10},{10... | collective-permute-start | bytes 442376 | tf_op jit(solution)/shard_map/ppermute | solution.py:598
  281.1 9.8 %collective-permute-start.56 = (bf16[192,384]{1,0:T(8,128)(2,1)S(1)}, bf16[192,384]{1,0:T(8,128)(2,1)S(1)}, u32[]{:S(2)}, u32[]{:S(2)}) collective-permute-start(bf16[192,384]{1,0:T(8,128)(2,1)S(1)} %add.155), channel_id=1, source_target_pairs={{0,16},{8,24},{16,0},{24,8},{1,17},{9,25},{17,1},{25,9},{2,18},{10... | collective-permute-start | bytes 442376 | tf_op jit(solution)/shard_map/ppermute | solution.py:598
  288.7 15.7 %collective-permute-start.57 = (bf16[400,384]{1,0:T(8,128)(2,1)S(1)}, bf16[400,384]{1,0:T(8,128)(2,1)S(1)}, u32[]{:S(2)}, u32[]{:S(2)}) collective-permute-start(bf16[400,384]{1,0:T(8,128)(2,1)S(1)} %add.157), channel_id=1, source_target_pairs={{0,16},{8,24},{16,0},{24,8},{1,17},{9,25},{17,1},{25,9},{2,18},{10... | collective-permute-start | bytes 921608 | tf_op jit(solution)/shard_map/ppermute | solution.py:598
  290.9 17.2 %collective-permute-start.61 = (bf16[192,512]{1,0:T(8,128)(2,1)S(1)}, bf16[192,512]{1,0:T(8,128)(2,1)S(1)}, u32[]{:S(2)}, u32[]{:S(2)}) collective-permute-start(bf16[192,512]{1,0:T(8,128)(2,1)S(1)} %get-tuple-element.232), channel_id=1, source_target_pairs={{0,6},{2,4},{4,2},{6,0},{1,7},{3,5},{5,3},{7,1},{8,14},{10,12},{12... | collective-permute-start | bytes 589832 | tf_op jit(solution)/shard_map/ppermute | solution.py:598
  291.3 13.9 %collective-permute-start.63 = (bf16[192,384]{1,0:T(8,128)(2,1)S(1)}, bf16[192,384]{1,0:T(8,128)(2,1)S(1)}, u32[]{:S(2)}, u32[]{:S(2)}) collective-permute-start(bf16[192,384]{1,0:T(8,128)(2,1)S(1)} %add.158), channel_id=1, source_target_pairs={{0,8},{8,0},{16,24},{24,16},{1,9},{9,1},{17,25},{25,17},{2,10},{10... | collective-permute-start | bytes 442376 | tf_op jit(solution)/shard_map/ppermute | solution.py:598
  (108 other events, 850.4 us)

commit v2 on v1

--- a/solution.py
+++ b/solution.py
@@ -737,43 +737,43 @@
     r_down1 = swap(far, "row", 2)
     gq = gq.reshape(2, hb, tokens)
     att2 = att.reshape(2, hb, tokens)
-    theirs = pair_theirs(after(x, far, gkv1), gq, go, att2, "pair_theirs")
+    theirs = pair_theirs(after(x, far), gq, go, att2, "pair_theirs")
     got3 = swap(theirs, "row", 1)
     g, sum_kv = key_back(after(gkv0, theirs), gkv1, fk, uk, v, omegas, heads, head_width)
     g = g.reshape(2, 2 * hb, tokens)
     sums = (sum1, sum2, bd, bu, sum_q, sum_kv)
     far = far_half(after(up[0][0], g), up[0][1])
     r_up0 = swap(far, "row", 2)
-    theirs = last_parts(after(x, far), g, sums, None, "last_theirs")[0]
+    down1 = total(after(down[1][0], far), down[1][1], r_down1)
+    z_down1 = Fold(down1)
+    order = z_down0.middle(down1)
+    theirs = last_parts(after(x, order), g, sums, None, "last_theirs")[0]
     got4 = swap(theirs, "row", 1)
     keep3, send3 = pair_mine(after(x, theirs), gq, go, att2, got3, "pair_mine")
     r_y3 = swap(send3, "col", 1)
-    far = far_half(after(up[1][0], send3), up[1][1])
+    up0 = total(after(up[0][0], send3), up[0][1], r_up0)
+    z_up0 = Fold(up0)
+    keep4, send4 = last_parts(after(x, up0), g, sums, got4, "last_mine")
+    r_x4 = swap(send4, "row", 2)
+    far = far_half(after(up[1][0], send4), up[1][1])
     r_up1 = swap(far, "row", 2)
-    keep4, send4 = last_parts(after(x, far), g, sums, got4, "last_mine")
-    r_x4 = swap(send4, "row", 2)
-    down1 = total(after(down[1][0], send4), down[1][1], r_down1)
-    z_down1 = Fold(down1)
-    order = z_down0.middle(down1)
+    order = z_down1.middle(far)
+    order = z_down0.back(order)
     gin = input_grad(gq, g, after(go, order), near_a, other_a)
     far = far_half(after(keep4, gin[0]), r_x4)
     r_y4 = swap(far, "col", 1)
-    up0 = total(after(up[0][0], far), up[0][1], r_up0)
-    z_up0 = Fold(up0)
-    order = z_down1.middle(up0)
-    order = z_down0.back(order)
+    up1 = total(after(up[1][0], far), up[1][1], r_up1)
+    z_up1 = Fold(up1)
+    order = z_up0.middle(up1)
     far = far_half(after(keep3, order), r_y3)
     r_x3 = swap(far, "row", 2)
     gin = exchange([after(gin[j], far) for j in (0, 2, 1, 3)])
-    last = total(after(keep4, far), r_x4, r_y4)
-    order = z_up0.middle(last)
-    up1 = total(after(up[1][0], order), up[1][1], r_up1)
-    z_up1 = Fold(up1)
-    order = z_down1.back(up1)
+    order = z_down1.back(far)
+    last = total(after(keep4, order), r_x4, r_y4)
+    order = z_up1.middle(last)
     last = jnp.concatenate((last, total(after(keep3, order), r_y3, r_x3)), axis=0)
     z_last = Fold(last)
-    order = z_up1.middle(last)
-    order = z_up0.back(order)
+    order = z_up0.back(last)
     order = z_last.middle(order)
     order = z_up1.back(order)
     order = z_last.back(order)

time: 321 us -> 301 us (0.938)
  waiting for transfers between devices: 117 us -> 93.2 us
  Pallas kernels: 108 us -> 103 us
  starting transfers between devices: 57.8 us -> 62.6 us
    ppermute x66, waiting for transfers between devices: 117 us -> 93.2 us  [swap(): return lax.ppermute(value, axis, [(s, s ^ mask) for s in range(size)])]
    pallas_call x22, Pallas kernels: 108 us -> 103 us  [call(): pl.pallas_call(body, out_shape=[make(s, d) for s, d in outs], scratch_sha...]
    ppermute x66, starting transfers between devices: 57.8 us -> 62.6 us  [swap(): return lax.ppermute(value, axis, [(s, s ^ mask) for s in range(size)])]
    unnamed x180 -> x182, local copies, waits for them, and re-layouts: 13.4 us -> 14.9 us
  transfers between devices with their start and end apart: 66 -> 66, of which waited for: 27 -> 25; matrix products, arithmetic and copies ran while one was open for 4% -> 5% of each run, Pallas kernels for 23% -> 23%
where the time goes in v2:
time: 301 us; the launch traced here: 299 us
  Pallas kernels  103 us (34%)
  waiting for transfers between devices  93.2 us (31%)
  starting transfers between devices  62.6 us (21%)
  local copies, waits for them, and re-layouts  20.7 us (7%)
  other arithmetic  14.2 us (5%)
  between operations  4.99 us (2%)
    pallas_call x22, Pallas kernels, call(): pl.pallas_call(body, out_shape=[make(s, d) for s, d in outs], scratch_sha...  103 us
    ppermute x66, waiting for transfers between devices, swap(): return lax.ppermute(value, axis, [(s, s ^ mask) for s in range(size)])  93.2 us
    ppermute x66, starting transfers between devices, swap(): return lax.ppermute(value, axis, [(s, s ^ mask) for s in range(size)])  62.6 us
    unnamed x182, local copies, waits for them, and re-layouts  14.9 us
  transfers between devices with their start and end apart: 66, of which 25 were waited for; matrix products, arithmetic and copies ran while one was open for 5% of the time, Pallas kernels for 23%

profile of v2, /device:TPU:0, one launch (start us, length us, event | category | flops | bytes accessed | tf_op | source)
XLA Modules:
  0.0 298.5 jit_solution(5521971633165909061)
XLA Ops:
  2.0 2.4 split_positions.2
  4.4 2.1 narrow_a.1.refs_4_.refs_0_
  6.5 3.0 %collective-permute-start.6 = (bf16[208,1152]{1,0:T(8,128)(2,1)}, bf16[208,1152]{1,0:T(8,128)(2,1)S(1)}, u32[]{:S(2)}, u32[]{:S(2)}) collective-permute-start(bf16[208,1152]{1,0:T(8,128)(2,1)} %narrow_a.1.refs_4_.refs_0_), channel_id=1, source_target_pairs={{0,1},{1,0},{2,3},{3,2},{4,5},{5,4},{6,7},{7,6},{8,9},{9,8},{10,11... | collective-permute-start | bytes 1437704 | tf_op jit(solution)/shard_map/ppermute | solution.py:598
  16.0 2.6 collective-permute-start.14
  19.1 5.8 %collective-permute-done.7.refs_13_.om1_ref = bf16[6,64,256]{2,1,0:T(8,128)(2,1)S(1)} collective-permute-done((bf16[6,64,256]{2,1,0:T(8,128)(2,1)S(1)}, bf16[6,64,256]{2,1,0:T(8,128)(2,1)S(1)}, u32[]{:S(2)}, u32[]{:S(2)}) %collective-permute-start.7) | collective-permute-done | bytes 196640 | tf_op jit(solution)/shard_map/ppermute | solution.py:598
  28.9 3.6 %narrow_b.1.refs_4_.refs_14_.refs_24_.refs_0_ = bf16[192,3456]{1,0:T(8,128)(2,1)} custom-call(f32[192,384]{1,0:T(8,128)} %refs_0_.1, f32[192,1536]{1,0:T(8,128)} %refs_1_.3, f32[192,1536]{1,0:T(8,128)} %refs_2_.3), custom_call_target="tpu_custom_call" | custom-call | flops 1000 | bytes 1000 | tf_op jit(solution)/shard_map/narrow_b/pallas_call | solution.py:50
  34.7 5.3 %collective-permute-done.8.refs_9_.refs_5_ = bf16[208,1152]{1,0:T(8,128)(2,1)} collective-permute-done((bf16[208,1152]{1,0:T(8,128)(2,1)}, bf16[208,1152]{1,0:T(8,128)(2,1)}, u32[]{:S(2)}, u32[]{:S(2)}) %collective-permute-start.8) | collective-permute-done | bytes 479264 | tf_op jit(solution)/shard_map/ppermute | solution.py:598
  43.5 11.2 %attention_in.1 = (bf16[768,512]{1,0:T(8,128)(2,1)}, bf16[3072,512]{1,0:T(8,128)(2,1)}, bf16[3072,512]{1,0:T(8,128)(2,1)}, bf16[768,512]{1,0:T(8,128)(2,1)}, bf1...) custom-call(bf16[192,512]{1,0:T(8,128)(2,1)} %get-tuple-element.126., ...), custom_call_target="tpu_custom_call" | custom-call | flops 1000 | bytes 1000 | tf_op jit(solution)/shard_map/attention_in/pallas_call | solution.py:50
  54.8 1.8 collective-permute-done.11
  57.8 2.5 split_positions.3
  60.3 3.3 %collective-permute-done.15.refs_5_.refs_15_.refs_25_.refs_1_ = bf16[192,3456]{1,0:T(8,128)(2,1)S(1)} collective-permute-done((bf16[192,3456]{1,0:T(8,128)(2,1)}, bf16[192,3456]{1,0:T(8,128)(2,1)S(1)}, u32[]{:S(2)}, u32[]{:S(2)}) %collective-permute-start.15) | collective-permute-done | bytes 1327136 | tf_op jit(solution)/shard_map/ppermute | solution.py:598
  63.7 1.8 collective-permute-start.20
  65.7 1.8 collective-permute-start.21
  67.5 4.7 %collective-permute-done.18.refs_8_.refs_18_.refs_28_.refs_4_ = bf16[192,3456]{1,0:T(8,128)(2,1)S(1)} collective-permute-done((bf16[192,3456]{1,0:T(8,128)(2,1)}, bf16[192,3456]{1,0:T(8,128)(2,1)S(1)}, u32[]{:S(2)}, u32[]{:S(2)}) %collective-permute-start.18) | collective-permute-done | bytes 1327136 | tf_op jit(solution)/shard_map/ppermute | solution.py:598
  72.3 10.4 %collective-permute-done.21.refs_37_ = bf16[192,512]{1,0:T(8,128)(2,1)S(1)} collective-permute-done((bf16[192,512]{1,0:T(8,128)(2,1)S(1)}, bf16[192,512]{1,0:T(8,128)(2,1)S(1)}, u32[]{:S(2)}, u32[]{:S(2)}) %collective-permute-start.21) | collective-permute-done | bytes 196640 | tf_op jit(solution)/shard_map/ppermute | solution.py:598
  83.0 1.7 collective-permute-done.22.refs_39_
  84.7 2.3 collective-permute-start.17
  87.1 5.1 %collective-permute-done.19.refs_9_.refs_19_.refs_29_.refs_5_ = bf16[48,3456]{1,0:T(8,128)(2,1)S(1)} collective-permute-done((bf16[48,3456]{1,0:T(8,128)(2,1)S(1)}, bf16[48,3456]{1,0:T(8,128)(2,1)S(1)}, u32[]{:S(2)}, u32[]{:S(2)}) %collective-permute-start.19) | collective-permute-done | bytes 331808 | tf_op jit(solution)/shard_map/ppermute | solution.py:598
  93.7 2.7 collective-permute-done.26.refs_38_
  98.6 21.2 %middle.1 = (bf16[864,256]{1,0:T(8,128)(2,1)}, bf16[768,512]{1,0:T(8,128)(2,1)}, f32[16,512]{1,0:T(8,128)}, bf16[768,512]{1,0:T(8,128)(2,1)}, f32[8,512]{1,0:T(8...) custom-call(bf16[864,256]{1,0:T(8,128)(2,1)} %copy-done.73, ...), custom_call_target="tpu_custom_call" | custom-call | flops 1000 | bytes 1000 | tf_op jit(solution)/shard_map/middle/pallas_call | solution.py:50
  121.0 1.9 copy-done.24
  122.9 2.8 down_theirs.1
  129.6 7.6 %down_back.1 = (bf16[2,1536,512]{2,1,0:T(8,128)(2,1)}, f32[2,8,1536]{2,1,0:T(8,128)S(1)}, f32[8,768]{1,0:T(8,128)S(1)}) custom-call(bf16[768,512]{1,0:T(8,128)(2,1)S(1)} %copy-done.23, bf16[2,1536,512]{2,1,0:T(8,128)(2,1)} %get-tuple-element.153.slope_ref, bf16[192,3456]{1,0:T(8,128)(2,1)S(1)} %copy-done.1, bf16[192,3456]{1,0:T(8,128)(2,1)S(1)} %copy-done.3, ...), custom_call_target="tpu_custom_call" | custom-call | flops 1000 | bytes 1000 | tf_op jit(solution)/shard_map/down_back/pallas_call | solution.py:50
  137.3 3.9 %down_mine.1 = (bf16[384,768]{1,0:T(8,128)(2,1)S(1)}, bf16[384,768]{1,0:T(8,128)(2,1)S(1)}, bf16[384,768]{1,0:T(8,128)(2,1)S(1)}, bf16[384,768]{1,0:T(8,128)(2,1)}) custom-call(bf16[768,512]{1,0:T(8,128)(2,1)S(1)} %copy-done.23, bf16[2,1536,512]{2,1,0:T(8,128)(2,1)S(1)} %copy-done.24, bf16[2,384,1536]{2,1,0:T(8,128)(2,1)S(1)} %collective-permute-done.27.got_ref), custom_call_target="tpu_custom_call" | custom-call | flops 1000 | bytes 1000 | tf_op jit(solution)/shard_map/down_mine/pallas_call | solution.py:50
  144.7 18.2 %up_back.1 = (bf16[768,512]{1,0:T(8,128)(2,1)S(1)}, f32[24,768]{1,0:T(8,128)S(1)}) custom-call(bf16[2,1536,512]{2,1,0:T(8,128)(2,1)} %get-tuple-element.158.gu_ref.r_ref, bf16[768,512]{1,0:T(8,128)(2,1)S(1)} %copy-done.23, bf16[768,512]{1,0:T(8,128)(2,1)S(1)} %copy-done.41, f32[8,512]{1,0:T(8,128)S(1)} %copy-done.70, f32[8,768]{1,0:T(8,128)S(1)} %copy-done.66, ...), custom_call_target="tpu_custom_call" | custom-call | flops 1000 | bytes 1000 | tf_op jit(solution)/shard_map/up_back/pallas_call | solution.py:50
  163.5 3.7 %attention_mid.1 = (bf16[864,512]{1,0:T(8,128)(2,1)S(1)}, bf16[864,256]{1,0:T(8,128)(2,1)S(1)}) custom-call(bf16[768,512]{1,0:T(8,128)(2,1)S(1)} %get-tuple-element.210.go_ref, bf16[768,512]{1,0:T(8,128)(2,1)S(1)} %copy-done.29, f32[16,512]{1,0:T(8,128)S(1)} %copy-done.69, bf16[3072,512]{1,0:T(8,128)(2,1)} %get-tuple-element.133.refs_2_.fq_ref, ...), custom_call_target="tpu_custom_call" | custom-call | flops 1000 | bytes 1000 | tf_op jit(solution)/shard_map/attention_mid/pallas_call | solution.py:50
  168.6 2.8 up_theirs.1
  172.9 3.8 %collective-permute-done.33 = bf16[864,256]{1,0:T(8,128)(2,1)S(1)} collective-permute-done((bf16[864,256]{1,0:T(8,128)(2,1)S(1)}, bf16[864,256]{1,0:T(8,128)(2,1)S(1)}, u32[]{:S(2)}, u32[]{:S(2)}) %collective-permute-start.33) | collective-permute-done | bytes 442400 | tf_op jit(solution)/shard_map/ppermute | solution.py:598
  177.5 2.8 query_back.1
  182.0 3.8 %up_mine.1 = (bf16[384,768]{1,0:T(8,128)(2,1)S(1)}, bf16[384,768]{1,0:T(8,128)(2,1)S(1)}, bf16[384,768]{1,0:T(8,128)(2,1)}, bf16[384,768]{1,0:T(8,128)(2,1)S(1)}) custom-call(bf16[768,512]{1,0:T(8,128)(2,1)S(1)} %copy-done.32, bf16[2,1536,512]{2,1,0:T(8,128)(2,1)S(1)} %copy-done.20, bf16[2,384,1536]{2,1,0:T(8,128)(2,1)S(1)} %collective-permute-done.34.got_ref), custom_call_target="tpu_custom_call" | custom-call | flops 1000 | bytes 1000 | tf_op jit(solution)/shard_map/up_mine/pallas_call | solution.py:50
  190.3 1.7 collective-permute-start.38
  195.8 6.3 %collective-permute-done.36.gkv1_ref = bf16[864,256]{1,0:T(8,128)(2,1)S(1)} collective-permute-done((bf16[864,256]{1,0:T(8,128)(2,1)}, bf16[864,256]{1,0:T(8,128)(2,1)S(1)}, u32[]{:S(2)}, u32[]{:S(2)}) %collective-permute-start.36) | collective-permute-done | bytes 442400 | tf_op jit(solution)/shard_map/ppermute | solution.py:598
  203.2 3.6 %key_back.1 = (bf16[1536,512]{1,0:T(8,128)(2,1)S(1)}, f32[8,1536]{1,0:T(8,128)S(1)}) custom-call(bf16[864,256]{1,0:T(8,128)(2,1)S(1)} %copy-done.40, bf16[864,256]{1,0:T(8,128)(2,1)S(1)} %collective-permute-done.36.gkv1_ref, bf16[3072,512]{1,0:T(8,128)(2,1)S(1)} %copy-done.33, bf16[768,512]{1,0:T(8,128)(2,1)S(1)} %copy-done.42, ...), custom_call_target="tpu_custom_call" | custom-call | flops 1000 | bytes 1000 | tf_op jit(solution)/shard_map/key_back/pallas_call | solution.py:50
  213.7 2.6 collective-permute-start.45
  217.3 2.5 collective-permute-done.41
  222.5 1.8 collective-permute-start.44
  226.6 1.8 collective-permute-start.47
  228.5 2.0 collective-permute-start.48
  230.7 3.9 %input_grad.1 = (bf16[192,512]{1,0:T(8,128)(2,1)S(1)}, bf16[192,512]{1,0:T(8,128)(2,1)S(1)}, bf16[192,512]{1,0:T(8,128)(2,1)S(1)}, bf16[192,512]{1,0:T(8,128)(2,1)S(1)}) custom-call(bf16[2,384,512]{2,1,0:T(8,128)(2,1)S(1)} %bitcast.23, bf16[2,768,512]{2,1,0:T(8,128)(2,1)S(1)} %bitcast.20, bf16[768,512]{1,0:T(8,128)(2,1)S(1)} %get-tuple-element.210.go_ref, ...), custom_call_target="tpu_custom_call" | custom-call | flops 1000 | bytes 1000 | tf_op jit(solution)/shard_map/input_grad/pallas_call | solution.py:50
  234.7 4.7 %collective-permute-done.46 = bf16[416,768]{1,0:T(8,128)(2,1)S(1)} collective-permute-done((bf16[416,768]{1,0:T(8,128)(2,1)S(1)}, bf16[416,768]{1,0:T(8,128)(2,1)S(1)}, u32[]{:S(2)}, u32[]{:S(2)}) %collective-permute-start.46) | collective-permute-done | bytes 639008 | tf_op jit(solution)/shard_map/ppermute | solution.py:598
  239.3 2.6 collective-permute-start.50
  241.9 2.3 collective-permute-done.47
  245.9 2.7 collective-permute-start.54
  254.0 4.1 %collective-permute-done.52 = bf16[192,384]{1,0:T(8,128)(2,1)S(1)} collective-permute-done((bf16[192,384]{1,0:T(8,128)(2,1)S(1)}, bf16[192,384]{1,0:T(8,128)(2,1)S(1)}, u32[]{:S(2)}, u32[]{:S(2)}) %collective-permute-start.52) | collective-permute-done | bytes 147488 | tf_op jit(solution)/shard_map/ppermute | solution.py:598
  263.4 9.0 %collective-permute-done.55 = bf16[400,384]{1,0:T(8,128)(2,1)S(1)} collective-permute-done((bf16[400,384]{1,0:T(8,128)(2,1)S(1)}, bf16[400,384]{1,0:T(8,128)(2,1)S(1)}, u32[]{:S(2)}, u32[]{:S(2)}) %collective-permute-start.55) | collective-permute-done | bytes 307232 | tf_op jit(solution)/shard_map/ppermute | solution.py:598
  274.0 1.7 collective-permute-start.63
  275.8 9.4 %collective-permute-done.57 = bf16[400,384]{1,0:T(8,128)(2,1)S(1)} collective-permute-done((bf16[400,384]{1,0:T(8,128)(2,1)S(1)}, bf16[400,384]{1,0:T(8,128)(2,1)S(1)}, u32[]{:S(2)}, u32[]{:S(2)}) %collective-permute-start.57) | collective-permute-done | bytes 307232 | tf_op jit(solution)/shard_map/ppermute | solution.py:598
  289.5 3.6 %collective-permute-done.58 = bf16[400,384]{1,0:T(8,128)(2,1)S(1)} collective-permute-done((bf16[400,384]{1,0:T(8,128)(2,1)S(1)}, bf16[400,384]{1,0:T(8,128)(2,1)S(1)}, u32[]{:S(2)}, u32[]{:S(2)}) %collective-permute-start.58) | collective-permute-done | bytes 307232 | tf_op jit(solution)/shard_map/ppermute | solution.py:598
  (342 shorter events, 80.8 us)
Async XLA Ops:
  6.5 18.7 %collective-permute-start.6 = (bf16[208,1152]{1,0:T(8,128)(2,1)}, bf16[208,1152]{1,0:T(8,128)(2,1)S(1)}, u32[]{:S(2)}, u32[]{:S(2)}) collective-permute-start(bf16[208,1152]{1,0:T(8,128)(2,1)} %narrow_a.1.refs_4_.refs_0_), channel_id=1, source_target_pairs={{0,1},{1,0},{2,3},{3,2},{4,5},{5,4},{6,7},{7,6},{8,9},{9,8},{10,11... | collective-permute-start | bytes 1437704 | tf_op jit(solution)/shard_map/ppermute | solution.py:598
  9.5 17.2 %collective-permute-start.3 = (bf16[208,1152]{1,0:T(8,128)(2,1)}, bf16[208,1152]{1,0:T(8,128)(2,1)}, u32[]{:S(2)}, u32[]{:S(2)}) collective-permute-start(bf16[208,1152]{1,0:T(8,128)(2,1)} %narrow_a.1.refs_4_.refs_0_), channel_id=1, source_target_pairs={{0,4},{2,6},{4,0},{6,2},{1,5},{3,7},{5,1},{7,3},{8,12},{10,14},{12... | collective-permute-start | bytes 1437704 | tf_op jit(solution)/shard_map/ppermute | solution.py:598
  13.9 10.9 %collective-permute-start.7 = (bf16[6,64,256]{2,1,0:T(8,128)(2,1)S(1)}, bf16[6,64,256]{2,1,0:T(8,128)(2,1)S(1)}, u32[]{:S(2)}, u32[]{:S(2)}) collective-permute-start(bf16[6,64,256]{2,1,0:T(8,128)(2,1)S(1)} %copy-done.36), channel_id=1, source_target_pairs={{0,1},{1,0},{2,3},{3,2},{4,5},{5,4},{6,7},{7,6},{8,9},{9,8},{10,11... | collective-permute-start | bytes 589832 | tf_op jit(solution)/shard_map/ppermute | solution.py:598
  16.0 12.3 %collective-permute-start.14 = (f32[8,128]{1,0:T(8,128)S(1)}, f32[8,128]{1,0:T(8,128)S(1)}, u32[]{:S(2)}, u32[]{:S(2)}) collective-permute-start(f32[8,128]{1,0:T(8,128)S(1)} %broadcast_add_fusion), channel_id=1, source_target_pairs={{0,16},{8,24},{16,0},{24,8},{1,17},{9,25},{17,1},{25,9},{2,18},{10... | collective-permute-start | bytes 12296 | tf_op jit(solution)/shard_map/ppermute | solution.py:598
  18.6 13.9 %collective-permute-start = (bf16[192,512]{1,0:T(8,128)(2,1)S(1)}, bf16[192,512]{1,0:T(8,128)(2,1)S(1)}, u32[]{:S(2)}, u32[]{:S(2)}) collective-permute-start(bf16[192,512]{1,0:T(8,128)(2,1)S(1)} %copy-done.87), channel_id=1, source_target_pairs={{0,4},{2,6},{4,0},{6,2},{1,5},{3,7},{5,1},{7,3},{8,12},{10,14},{12... | collective-permute-start | bytes 589832 | tf_op jit(solution)/shard_map/ppermute | solution.py:598
  25.2 14.8 %collective-permute-start.4 = (bf16[208,1152]{1,0:T(8,128)(2,1)}, bf16[208,1152]{1,0:T(8,128)(2,1)}, u32[]{:S(2)}, u32[]{:S(2)}) collective-permute-start(bf16[208,1152]{1,0:T(8,128)(2,1)} %narrow_a.1.refs_4_.refs_0_), channel_id=1, source_target_pairs={{0,2},{2,0},{4,6},{6,4},{1,3},{3,1},{5,7},{7,5},{8,10},{10,8},{12,... | collective-permute-start | bytes 1437704 | tf_op jit(solution)/shard_map/ppermute | solution.py:598
  26.7 13.3 %collective-permute-start.8 = (bf16[208,1152]{1,0:T(8,128)(2,1)}, bf16[208,1152]{1,0:T(8,128)(2,1)}, u32[]{:S(2)}, u32[]{:S(2)}) collective-permute-start(bf16[208,1152]{1,0:T(8,128)(2,1)} %collective-permute-done.3.refs_5_.refs_1_), channel_id=1, source_target_pairs={{0,1},{1,0},{2,3},{3,2},{4,5},{5,4},{6,7},{7,6},{8,9},{9,8},{10,11... | collective-permute-start | bytes 1437704 | tf_op jit(solution)/shard_map/ppermute | solution.py:598
  32.5 31.1 %collective-permute-start.15 = (bf16[192,3456]{1,0:T(8,128)(2,1)}, bf16[192,3456]{1,0:T(8,128)(2,1)S(1)}, u32[]{:S(2)}, u32[]{:S(2)}) collective-permute-start(bf16[192,3456]{1,0:T(8,128)(2,1)} %narrow_b.1.refs_4_.refs_14_.refs_24_.refs_0_), channel_id=1, source_target_pairs={{0,4},{2,6},{4,0},{6,2},{1,5},{3,7},{5,1},{7,3},{8,12},{10,14},{12... | collective-permute-start | bytes 3981320 | tf_op jit(solution)/shard_map/ppermute | solution.py:598
  33.1 9.7 %collective-permute-start.9 = (bf16[208,1152]{1,0:T(8,128)(2,1)S(1)}, bf16[208,1152]{1,0:T(8,128)(2,1)}, u32[]{:S(2)}, u32[]{:S(2)}) collective-permute-start(bf16[208,1152]{1,0:T(8,128)(2,1)S(1)} %collective-permute-done.6.refs_8_.refs_4_), channel_id=1, source_target_pairs={{0,2},{2,0},{4,6},{6,4},{1,3},{3,1},{5,7},{7,5},{8,10},{10,8},{12,... | collective-permute-start | bytes 1437704 | tf_op jit(solution)/shard_map/ppermute | solution.py:598
  40.0 32.3 %collective-permute-start.18 = (bf16[192,3456]{1,0:T(8,128)(2,1)}, bf16[192,3456]{1,0:T(8,128)(2,1)S(1)}, u32[]{:S(2)}, u32[]{:S(2)}) collective-permute-start(bf16[192,3456]{1,0:T(8,128)(2,1)} %narrow_b.1.refs_4_.refs_14_.refs_24_.refs_0_), channel_id=1, source_target_pairs={{0,1},{1,0},{2,3},{3,2},{4,5},{5,4},{6,7},{7,6},{8,9},{9,8},{10,11... | collective-permute-start | bytes 3981320 | tf_op jit(solution)/shard_map/ppermute | solution.py:598
  63.7 29.4 %collective-permute-start.20 = (bf16[144,3456]{1,0:T(8,128)(2,1)S(1)}, bf16[144,3456]{1,0:T(8,128)(2,1)S(1)}, u32[]{:S(2)}, u32[]{:S(2)}) collective-permute-start(bf16[144,3456]{1,0:T(8,128)(2,1)S(1)} %slice.182), channel_id=1, source_target_pairs={{0,1},{1,0},{2,3},{3,2},{4,5},{5,4},{6,7},{7,6},{8,9},{9,8},{10,11... | collective-permute-start | bytes 2985992 | tf_op jit(solution)/shard_map/ppermute | solution.py:598
  65.4 21.6 %collective-permute-start.12 = (bf16[864,256]{1,0:T(8,128)(2,1)S(1)}, bf16[864,256]{1,0:T(8,128)(2,1)S(1)}, u32[]{:S(2)}, u32[]{:S(2)}) collective-permute-start(bf16[864,256]{1,0:T(8,128)(2,1)S(1)} %add.126.refs_0_), channel_id=1, source_target_pairs={{0,4},{2,6},{4,0},{6,2},{1,5},{3,7},{5,1},{7,3},{8,12},{10,14},{12... | collective-permute-start | bytes 1327112 | tf_op jit(solution)/shard_map/ppermute | solution.py:598
  65.7 27.9 %collective-permute-start.16 = (bf16[192,3456]{1,0:T(8,128)(2,1)S(1)}, bf16[192,3456]{1,0:T(8,128)(2,1)S(1)}, u32[]{:S(2)}, u32[]{:S(2)}) collective-permute-start(bf16[192,3456]{1,0:T(8,128)(2,1)S(1)} %copy-done), channel_id=1, source_target_pairs={{0,2},{2,0},{4,6},{6,4},{1,3},{3,1},{5,7},{7,5},{8,10},{10,8},{12,... | collective-permute-start | bytes 3981320 | tf_op jit(solution)/shard_map/ppermute | solution.py:598
  65.7 17.0 %collective-permute-start.21 = (bf16[192,512]{1,0:T(8,128)(2,1)S(1)}, bf16[192,512]{1,0:T(8,128)(2,1)S(1)}, u32[]{:S(2)}, u32[]{:S(2)}) collective-permute-start(bf16[192,512]{1,0:T(8,128)(2,1)S(1)} %copy-done.89), channel_id=1, source_target_pairs={{0,4},{2,6},{4,0},{6,2},{1,5},{3,7},{5,1},{7,3},{8,12},{10,14},{12... | collective-permute-start | bytes 589832 | tf_op jit(solution)/shard_map/ppermute | solution.py:598
  72.3 12.4 %collective-permute-start.22 = (bf16[192,512]{1,0:T(8,128)(2,1)S(1)}, bf16[192,512]{1,0:T(8,128)(2,1)S(1)}, u32[]{:S(2)}, u32[]{:S(2)}) collective-permute-start(bf16[192,512]{1,0:T(8,128)(2,1)S(1)} %copy-done.88), channel_id=1, source_target_pairs={{0,6},{2,4},{4,2},{6,0},{1,7},{3,5},{5,3},{7,1},{8,14},{10,12},{12... | collective-permute-start | bytes 589832 | tf_op jit(solution)/shard_map/ppermute | solution.py:598
  84.7 11.7 %collective-permute-start.17 = (bf16[192,3456]{1,0:T(8,128)(2,1)S(1)}, bf16[192,3456]{1,0:T(8,128)(2,1)S(1)}, u32[]{:S(2)}, u32[]{:S(2)}) collective-permute-start(bf16[192,3456]{1,0:T(8,128)(2,1)S(1)} %collective-permute-done.15.refs_5_.refs_15_.refs_25_.refs_1_), channel_id=1, source_target_pairs={{0,2},{2,0},{4,6},{6,4},{1,3},{3,1},{5,7},{7,5},{8,10},{10,8},{12,... | collective-permute-start | bytes 3981320 | tf_op jit(solution)/shard_map/ppermute | solution.py:598
  125.6 11.6 %collective-permute-start.27 = (bf16[2,384,1536]{2,1,0:T(8,128)(2,1)S(1)}, bf16[2,384,1536]{2,1,0:T(8,128)(2,1)S(1)}, u32[]{:S(2)}, u32[]{:S(2)}) collective-permute-start(bf16[2,384,1536]{2,1,0:T(8,128)(2,1)S(1)} %down_theirs.1), channel_id=1, source_target_pairs={{0,2},{2,0},{4,6},{6,4},{1,3},{3,1},{5,7},{7,5},{8,10},{10,8},{12,... | collective-permute-start | bytes 7077896 | tf_op jit(solution)/shard_map/ppermute | solution.py:598
  141.2 26.2 %collective-permute-start.31 = (bf16[384,768]{1,0:T(8,128)(2,1)S(1)}, bf16[384,768]{1,0:T(8,128)(2,1)S(1)}, u32[]{:S(2)}, u32[]{:S(2)}) collective-permute-start(bf16[384,768]{1,0:T(8,128)(2,1)S(1)} %get-tuple-element.157), channel_id=1, source_target_pairs={{0,1},{1,0},{2,3},{3,2},{4,5},{5,4},{6,7},{7,6},{8,9},{9,8},{10,11... | collective-permute-start | bytes 1769480 | tf_op jit(solution)/shard_map/ppermute | solution.py:598
  142.8 24.5 %collective-permute-start.28 = (bf16[192,512]{1,0:T(8,128)(2,1)S(1)}, bf16[192,512]{1,0:T(8,128)(2,1)S(1)}, u32[]{:S(2)}, u32[]{:S(2)}) collective-permute-start(bf16[192,512]{1,0:T(8,128)(2,1)S(1)} %copy-done.85), channel_id=1, source_target_pairs={{0,2},{2,0},{4,6},{6,4},{1,3},{3,1},{5,7},{7,5},{8,10},{10,8},{12,... | collective-permute-start | bytes 589832 | tf_op jit(solution)/shard_map/ppermute | solution.py:598
  142.9 24.4 %collective-permute-start.29 = (bf16[192,512]{1,0:T(8,128)(2,1)S(1)}, bf16[192,512]{1,0:T(8,128)(2,1)S(1)}, u32[]{:S(2)}, u32[]{:S(2)}) collective-permute-start(bf16[192,512]{1,0:T(8,128)(2,1)S(1)} %copy-done.83), channel_id=1, source_target_pairs={{0,4},{2,6},{4,0},{6,2},{1,5},{3,7},{5,1},{7,3},{8,12},{10,14},{12... | collective-permute-start | bytes 589832 | tf_op jit(solution)/shard_map/ppermute | solution.py:598
  143.4 23.9 %collective-permute-start.30 = (bf16[192,512]{1,0:T(8,128)(2,1)S(1)}, bf16[192,512]{1,0:T(8,128)(2,1)S(1)}, u32[]{:S(2)}, u32[]{:S(2)}) collective-permute-start(bf16[192,512]{1,0:T(8,128)(2,1)S(1)} %copy-done.82), channel_id=1, source_target_pairs={{0,6},{2,4},{4,2},{6,0},{1,7},{3,5},{5,3},{7,1},{8,14},{10,12},{12... | collective-permute-start | bytes 589832 | tf_op jit(solution)/shard_map/ppermute | solution.py:598
  171.4 10.6 %collective-permute-start.34 = (bf16[2,384,1536]{2,1,0:T(8,128)(2,1)S(1)}, bf16[2,384,1536]{2,1,0:T(8,128)(2,1)S(1)}, u32[]{:S(2)}, u32[]{:S(2)}) collective-permute-start(bf16[2,384,1536]{2,1,0:T(8,128)(2,1)S(1)} %up_theirs.1), channel_id=1, source_target_pairs={{0,2},{2,0},{4,6},{6,4},{1,3},{3,1},{5,7},{7,5},{8,10},{10,8},{12,... | collective-permute-start | bytes 7077896 | tf_op jit(solution)/shard_map/ppermute | solution.py:598
  172.5 16.7 %collective-permute-start.35 = (bf16[384,768]{1,0:T(8,128)(2,1)}, bf16[384,768]{1,0:T(8,128)(2,1)}, u32[]{:S(2)}, u32[]{:S(2)}) collective-permute-start(bf16[384,768]{1,0:T(8,128)(2,1)} %get-tuple-element.181), channel_id=1, source_target_pairs={{0,1},{1,0},{2,3},{3,2},{4,5},{5,4},{6,7},{7,6},{8,9},{9,8},{10,11... | collective-permute-start | bytes 1769480 | tf_op jit(solution)/shard_map/ppermute | solution.py:598
  188.3 18.6 %collective-permute-start.37 = (bf16[384,768]{1,0:T(8,128)(2,1)}, bf16[384,768]{1,0:T(8,128)(2,1)}, u32[]{:S(2)}, u32[]{:S(2)}) collective-permute-start(bf16[384,768]{1,0:T(8,128)(2,1)} %get-tuple-element.179), channel_id=1, source_target_pairs={{0,1},{1,0},{2,3},{3,2},{4,5},{5,4},{6,7},{7,6},{8,9},{9,8},{10,11... | collective-permute-start | bytes 1769480 | tf_op jit(solution)/shard_map/ppermute | solution.py:598
  188.8 13.3 %collective-permute-start.36 = (bf16[864,256]{1,0:T(8,128)(2,1)}, bf16[864,256]{1,0:T(8,128)(2,1)S(1)}, u32[]{:S(2)}, u32[]{:S(2)}) collective-permute-start(bf16[864,256]{1,0:T(8,128)(2,1)} %add.134.gkv0_ref), channel_id=1, source_target_pairs={{0,4},{2,6},{4,0},{6,2},{1,5},{3,7},{5,1},{7,3},{8,12},{10,14},{12... | collective-permute-start | bytes 1327112 | tf_op jit(solution)/shard_map/ppermute | solution.py:598
  190.3 17.7 %collective-permute-start.38 = (bf16[192,768]{1,0:T(8,128)(2,1)S(1)}, bf16[192,768]{1,0:T(8,128)(2,1)S(1)}, u32[]{:S(2)}, u32[]{:S(2)}) collective-permute-start(bf16[192,768]{1,0:T(8,128)(2,1)S(1)} %slice_add_fusion.9), channel_id=1, source_target_pairs={{0,4},{2,6},{4,0},{6,2},{1,5},{3,7},{5,1},{7,3},{8,12},{10,14},{12... | collective-permute-start | bytes 884744 | tf_op jit(solution)/shard_map/ppermute | solution.py:598
  193.1 15.9 %collective-permute-start.39 = (bf16[192,384]{1,0:T(8,128)(2,1)S(1)}, bf16[192,384]{1,0:T(8,128)(2,1)S(1)}, u32[]{:S(2)}, u32[]{:S(2)}) collective-permute-start(bf16[192,384]{1,0:T(8,128)(2,1)S(1)} %get-tuple-element.266), channel_id=1, source_target_pairs={{0,8},{8,0},{16,24},{24,16},{1,9},{9,1},{17,25},{25,17},{2,10},{10... | collective-permute-start | bytes 442376 | tf_op jit(solution)/shard_map/ppermute | solution.py:598
  195.7 20.6 %collective-permute-start.40 = (bf16[2,384,768]{2,1,0:T(8,128)(2,1)S(1)}, bf16[2,384,768]{2,1,0:T(8,128)(2,1)S(1)}, u32[]{:S(2)}, u32[]{:S(2)}) collective-permute-start(bf16[2,384,768]{2,1,0:T(8,128)(2,1)S(1)} %pair_theirs.1), channel_id=1, source_target_pairs={{0,2},{2,0},{4,6},{6,4},{1,3},{3,1},{5,7},{7,5},{8,10},{10,8},{12,... | collective-permute-start | bytes 3538952 | tf_op jit(solution)/shard_map/ppermute | solution.py:598
  210.3 10.5 %collective-permute-start.42 = (bf16[2,2,208,768]{3,2,1,0:T(8,128)(2,1)S(1)}, bf16[2,2,208,768]{3,2,1,0:T(8,128)(2,1)S(1)}, u32[]{:S(2)}, u32[]{:S(2)}) collective-permute-start(bf16[2,2,208,768]{3,2,1,0:T(8,128)(2,1)S(1)} %last_theirs.1), channel_id=1, source_target_pairs={{0,2},{2,0},{4,6},{6,4},{1,3},{3,1},{5,7},{7,5},{8,10},{10,8},{12,... | collective-permute-start | bytes 3833864 | tf_op jit(solution)/shard_map/ppermute | solution.py:598
  210.8 15.7 %collective-permute-start.43 = (bf16[384,768]{1,0:T(8,128)(2,1)S(1)}, bf16[384,768]{1,0:T(8,128)(2,1)S(1)}, u32[]{:S(2)}, u32[]{:S(2)}) collective-permute-start(bf16[384,768]{1,0:T(8,128)(2,1)S(1)} %copy-done.72), channel_id=1, source_target_pairs={{0,1},{1,0},{2,3},{3,2},{4,5},{5,4},{6,7},{7,6},{8,9},{9,8},{10,11... | collective-permute-start | bytes 1769480 | tf_op jit(solution)/shard_map/ppermute | solution.py:598
  213.7 16.9 %collective-permute-start.45 = (bf16[192,384]{1,0:T(8,128)(2,1)S(1)}, bf16[192,384]{1,0:T(8,128)(2,1)S(1)}, u32[]{:S(2)}, u32[]{:S(2)}) collective-permute-start(bf16[192,384]{1,0:T(8,128)(2,1)S(1)} %add.139), channel_id=1, source_target_pairs={{0,16},{8,24},{16,0},{24,8},{1,17},{9,25},{17,1},{25,9},{2,18},{10... | collective-permute-start | bytes 442376 | tf_op jit(solution)/shard_map/ppermute | solution.py:598
  222.0 17.3 %collective-permute-start.46 = (bf16[416,768]{1,0:T(8,128)(2,1)S(1)}, bf16[416,768]{1,0:T(8,128)(2,1)S(1)}, u32[]{:S(2)}, u32[]{:S(2)}) collective-permute-start(bf16[416,768]{1,0:T(8,128)(2,1)S(1)} %get-tuple-element.204), channel_id=1, source_target_pairs={{0,4},{2,6},{4,0},{6,2},{1,5},{3,7},{5,1},{7,3},{8,12},{10,14},{12... | collective-permute-start | bytes 1916936 | tf_op jit(solution)/shard_map/ppermute | solution.py:598
  224.3 24.2 %collective-permute-start.49 = (bf16[384,768]{1,0:T(8,128)(2,1)S(1)}, bf16[384,768]{1,0:T(8,128)(2,1)S(1)}, u32[]{:S(2)}, u32[]{:S(2)}) collective-permute-start(bf16[384,768]{1,0:T(8,128)(2,1)S(1)} %get-tuple-element.199), channel_id=1, source_target_pairs={{0,1},{1,0},{2,3},{3,2},{4,5},{5,4},{6,7},{7,6},{8,9},{9,8},{10,11... | collective-permute-start | bytes 1769480 | tf_op jit(solution)/shard_map/ppermute | solution.py:598
  226.6 17.6 %collective-permute-start.47 = (bf16[192,768]{1,0:T(8,128)(2,1)S(1)}, bf16[192,768]{1,0:T(8,128)(2,1)S(1)}, u32[]{:S(2)}, u32[]{:S(2)}) collective-permute-start(bf16[192,768]{1,0:T(8,128)(2,1)S(1)} %slice_add_fusion.5), channel_id=1, source_target_pairs={{0,4},{2,6},{4,0},{6,2},{1,5},{3,7},{5,1},{7,3},{8,12},{10,14},{12... | collective-permute-start | bytes 884744 | tf_op jit(solution)/shard_map/ppermute | solution.py:598
  228.5 17.4 %collective-permute-start.48 = (bf16[192,384]{1,0:T(8,128)(2,1)S(1)}, bf16[192,384]{1,0:T(8,128)(2,1)S(1)}, u32[]{:S(2)}, u32[]{:S(2)}) collective-permute-start(bf16[192,384]{1,0:T(8,128)(2,1)S(1)} %get-tuple-element.262), channel_id=1, source_target_pairs={{0,8},{8,0},{16,24},{24,16},{1,9},{9,1},{17,25},{25,17},{2,10},{10... | collective-permute-start | bytes 442376 | tf_op jit(solution)/shard_map/ppermute | solution.py:598
  230.6 29.0 %collective-permute-start.64 = (bf16[192,384]{1,0:T(8,128)(2,1)S(1)}, bf16[192,384]{1,0:T(8,128)(2,1)S(1)}, u32[]{:S(2)}, u32[]{:S(2)}) collective-permute-start(bf16[192,384]{1,0:T(8,128)(2,1)S(1)} %add.144), channel_id=1, source_target_pairs={{0,8},{8,0},{16,24},{24,16},{1,9},{9,1},{17,25},{25,17},{2,10},{10... | collective-permute-start | bytes 442376 | tf_op jit(solution)/shard_map/ppermute | solution.py:598
  239.3 9.9 %collective-permute-start.50 = (bf16[192,384]{1,0:T(8,128)(2,1)S(1)}, bf16[192,384]{1,0:T(8,128)(2,1)S(1)}, u32[]{:S(2)}, u32[]{:S(2)}) collective-permute-start(bf16[192,384]{1,0:T(8,128)(2,1)S(1)} %add.143), channel_id=1, source_target_pairs={{0,16},{8,24},{16,0},{24,8},{1,17},{9,25},{17,1},{25,9},{2,18},{10... | collective-permute-start | bytes 442376 | tf_op jit(solution)/shard_map/ppermute | solution.py:598
  245.9 15.1 %collective-permute-start.54 = (bf16[192,384]{1,0:T(8,128)(2,1)S(1)}, bf16[192,384]{1,0:T(8,128)(2,1)S(1)}, u32[]{:S(2)}, u32[]{:S(2)}) collective-permute-start(bf16[192,384]{1,0:T(8,128)(2,1)S(1)} %add.148), channel_id=1, source_target_pairs={{0,16},{8,24},{16,0},{24,8},{1,17},{9,25},{17,1},{25,9},{2,18},{10... | collective-permute-start | bytes 442376 | tf_op jit(solution)/shard_map/ppermute | solution.py:598
  248.6 9.6 %collective-permute-start.53 = (bf16[192,768]{1,0:T(8,128)(2,1)S(1)}, bf16[192,768]{1,0:T(8,128)(2,1)S(1)}, u32[]{:S(2)}, u32[]{:S(2)}) collective-permute-start(bf16[192,768]{1,0:T(8,128)(2,1)S(1)} %slice_add_fusion.3), channel_id=1, source_target_pairs={{0,4},{2,6},{4,0},{6,2},{1,5},{3,7},{5,1},{7,3},{8,12},{10,14},{12... | collective-permute-start | bytes 884744 | tf_op jit(solution)/shard_map/ppermute | solution.py:598
  249.2 12.8 %collective-permute-start.65 = (bf16[192,384]{1,0:T(8,128)(2,1)S(1)}, bf16[192,384]{1,0:T(8,128)(2,1)S(1)}, u32[]{:S(2)}, u32[]{:S(2)}) collective-permute-start(bf16[192,384]{1,0:T(8,128)(2,1)S(1)} %add.150), channel_id=1, source_target_pairs={{0,8},{8,0},{16,24},{24,16},{1,9},{9,1},{17,25},{25,17},{2,10},{10... | collective-permute-start | bytes 442376 | tf_op jit(solution)/shard_map/ppermute | solution.py:598
  258.4 14.1 %collective-permute-start.55 = (bf16[400,384]{1,0:T(8,128)(2,1)S(1)}, bf16[400,384]{1,0:T(8,128)(2,1)S(1)}, u32[]{:S(2)}, u32[]{:S(2)}) collective-permute-start(bf16[400,384]{1,0:T(8,128)(2,1)S(1)} %get-tuple-element.250), channel_id=1, source_target_pairs={{0,8},{8,0},{16,24},{24,16},{1,9},{9,1},{17,25},{25,17},{2,10},{10... | collective-permute-start | bytes 921608 | tf_op jit(solution)/shard_map/ppermute | solution.py:598
  259.6 28.6 %collective-permute-start.59 = (bf16[192,512]{1,0:T(8,128)(2,1)S(1)}, bf16[192,512]{1,0:T(8,128)(2,1)S(1)}, u32[]{:S(2)}, u32[]{:S(2)}) collective-permute-start(bf16[192,512]{1,0:T(8,128)(2,1)S(1)} %get-tuple-element.228), channel_id=1, source_target_pairs={{0,2},{2,0},{4,6},{6,4},{1,3},{3,1},{5,7},{7,5},{8,10},{10,8},{12,... | collective-permute-start | bytes 589832 | tf_op jit(solution)/shard_map/ppermute | solution.py:598
  259.7 28.6 %collective-permute-start.60 = (bf16[192,512]{1,0:T(8,128)(2,1)S(1)}, bf16[192,512]{1,0:T(8,128)(2,1)S(1)}, u32[]{:S(2)}, u32[]{:S(2)}) collective-permute-start(bf16[192,512]{1,0:T(8,128)(2,1)S(1)} %get-tuple-element.230), channel_id=1, source_target_pairs={{0,4},{2,6},{4,0},{6,2},{1,5},{3,7},{5,1},{7,3},{8,12},{10,14},{12... | collective-permute-start | bytes 589832 | tf_op jit(solution)/shard_map/ppermute | solution.py:598
  261.0 13.0 %collective-permute-start.62 = (bf16[192,384]{1,0:T(8,128)(2,1)S(1)}, bf16[192,384]{1,0:T(8,128)(2,1)S(1)}, u32[]{:S(2)}, u32[]{:S(2)}) collective-permute-start(bf16[192,384]{1,0:T(8,128)(2,1)S(1)} %add.156), channel_id=1, source_target_pairs={{0,8},{8,0},{16,24},{24,16},{1,9},{9,1},{17,25},{25,17},{2,10},{10... | collective-permute-start | bytes 442376 | tf_op jit(solution)/shard_map/ppermute | solution.py:598
  262.1 11.6 %collective-permute-start.56 = (bf16[192,384]{1,0:T(8,128)(2,1)S(1)}, bf16[192,384]{1,0:T(8,128)(2,1)S(1)}, u32[]{:S(2)}, u32[]{:S(2)}) collective-permute-start(bf16[192,384]{1,0:T(8,128)(2,1)S(1)} %add.153), channel_id=1, source_target_pairs={{0,16},{8,24},{16,0},{24,8},{1,17},{9,25},{17,1},{25,9},{2,18},{10... | collective-permute-start | bytes 442376 | tf_op jit(solution)/shard_map/ppermute | solution.py:598
  272.5 12.7 %collective-permute-start.57 = (bf16[400,384]{1,0:T(8,128)(2,1)S(1)}, bf16[400,384]{1,0:T(8,128)(2,1)S(1)}, u32[]{:S(2)}, u32[]{:S(2)}) collective-permute-start(bf16[400,384]{1,0:T(8,128)(2,1)S(1)} %add.157), channel_id=1, source_target_pairs={{0,16},{8,24},{16,0},{24,8},{1,17},{9,25},{17,1},{25,9},{2,18},{10... | collective-permute-start | bytes 921608 | tf_op jit(solution)/shard_map/ppermute | solution.py:598
  273.8 14.5 %collective-permute-start.61 = (bf16[192,512]{1,0:T(8,128)(2,1)S(1)}, bf16[192,512]{1,0:T(8,128)(2,1)S(1)}, u32[]{:S(2)}, u32[]{:S(2)}) collective-permute-start(bf16[192,512]{1,0:T(8,128)(2,1)S(1)} %get-tuple-element.232), channel_id=1, source_target_pairs={{0,6},{2,4},{4,2},{6,0},{1,7},{3,5},{5,3},{7,1},{8,14},{10,12},{12... | collective-permute-start | bytes 589832 | tf_op jit(solution)/shard_map/ppermute | solution.py:598
  274.0 11.3 %collective-permute-start.63 = (bf16[192,384]{1,0:T(8,128)(2,1)S(1)}, bf16[192,384]{1,0:T(8,128)(2,1)S(1)}, u32[]{:S(2)}, u32[]{:S(2)}) collective-permute-start(bf16[192,384]{1,0:T(8,128)(2,1)S(1)} %add.158), channel_id=1, source_target_pairs={{0,8},{8,0},{16,24},{24,16},{1,9},{9,1},{17,25},{25,17},{2,10},{10... | collective-permute-start | bytes 442376 | tf_op jit(solution)/shard_map/ppermute | solution.py:598
  (109 other events, 717.4 us)

commit v3 on v2

--- a/solution.py
+++ b/solution.py
@@ -86,7 +86,11 @@
             at = pl.multiple_of(jnp.bitwise_xor(r, j) * n, n)
             o_ref[...] = in_ref[:, pl.ds(at, n)].astype(bf16)
 
-    return call(body, [((k, n), bf16)] * row_parts, (row, shard), "split_positions", in_specs=[SMEM, single(shard.shape)], pinned=True)
+    rows = k // 3
+    return call(
+        body, [((k, n), bf16)] * row_parts, (row, shard), "split_positions", (3,),
+        [SMEM, pl.BlockSpec((rows, length), lambda s: (s, 0))], [pl.BlockSpec((rows, n), lambda s: (s, 0))] * row_parts, pinned=True,
+    )
 
 
 def join_positions(blocks, row):
@@ -100,7 +104,11 @@
             at = pl.multiple_of(jnp.bitwise_xor(r, j) * n, n)
             o_ref[:, pl.ds(at, n)] = refs[j][...].astype(f32)
 
-    return call(body, [((k, n * parts), f32)], (row, *blocks), "join_positions", in_specs=[SMEM] + [single(b.shape) for b in blocks])[0]
+    rows = k // 3
+    return call(
+        body, [((k, n * parts), f32)], (row, *blocks), "join_positions", (3,),
+        [SMEM] + [pl.BlockSpec((rows, n), lambda s: (s, 0))] * parts, [pl.BlockSpec((rows, n * parts), lambda s: (s, 0))],
+    )[0]
 
 
 def narrow(parts, steps, name):
@@ -336,12 +344,14 @@
     def body(l_ref, r_ref, got_ref, keep0, keep1, send0, send1):
         step = pl.program_id(0)
 
-        def part(keep_ref, send_ref):
-            for i, o_ref in enumerate((keep_ref, send_ref)):
-                o_ref[...] = (nt(l_ref[...], r_ref[i]) + got_ref[i].astype(f32)).astype(bf16)
-
-        pl.when(step < share)(lambda: part(keep0, send0))
-        pl.when(step >= share)(lambda: part(keep1, send1))
+        sums = [(nt(l_ref[...], r_ref[i]) + got_ref[i].astype(f32)).astype(bf16) for i in range(2)]
+
+        def store(*refs):
+            for ref, value in zip(refs, sums):
+                ref[...] = value
+
+        pl.when(step < share)(lambda: store(keep0, send0))
+        pl.when(step >= share)(lambda: store(keep1, send1))
 
     first = pl.BlockSpec((half, block), lambda s: (0, jnp.minimum(s, share - 1)))
     second = pl.BlockSpec((half, block), lambda s: (0, jnp.maximum(s - share, 0)))
@@ -686,12 +696,12 @@
     near_a = (own_a, a_x, swap(own_a, "row", 1), swap(a_x, "row", 1))
     other_a = (a_y, a_far, swap(a_y, "row", 1), swap(a_far, "row", 1))
     count = reduce_small(jnp.sum(lengths).astype(f32).reshape(1, 1) + jnp.zeros((8, 128), f32), "dp")
-    own_b = narrow((after(w_out, own_a, count), w_up, w_down), 3, "narrow_b")
+    own_b = narrow((after(w_out, own_a), w_up, w_down), 3, "narrow_b")
     b_x = swap(after(own_b, a_x, ins_got[2], ins_got[3]), "row", 2)
     b_y = swap(after(own_b, a_far), "col", 1)
     length = lax.dynamic_index_in_dim(lengths, col, 0, False)
     keep = ((row * tokens + jnp.arange(tokens, dtype=jnp.int32)) < length).astype(f32)
-    keep = jnp.broadcast_to(keep[None, :], (8, tokens))
+    keep = after(jnp.broadcast_to(keep[None, :], (8, tokens)), count)
     scale = (2.0 * LOSS_SCALE) / (count * width)
 
     x, fq, fk, uq, uk, v, kv, vecs, up_bias_all = attention_in(
@@ -762,18 +772,18 @@
     gin = input_grad(gq, g, after(go, order), near_a, other_a)
     far = far_half(after(keep4, gin[0]), r_x4)
     r_y4 = swap(far, "col", 1)
+    far = far_half(after(keep3, far), r_y3)
+    r_x3 = swap(far, "row", 2)
     up1 = total(after(up[1][0], far), up[1][1], r_up1)
     z_up1 = Fold(up1)
     order = z_up0.middle(up1)
-    far = far_half(after(keep3, order), r_y3)
-    r_x3 = swap(far, "row", 2)
     gin = exchange([after(gin[j], far) for j in (0, 2, 1, 3)])
-    order = z_down1.back(far)
+    order = z_down1.back(order)
     last = total(after(keep4, order), r_x4, r_y4)
+    last = jnp.concatenate((last, total(keep3, r_y3, r_x3)), axis=0)
+    z_last = Fold(last)
     order = z_up1.middle(last)
-    last = jnp.concatenate((last, total(after(keep3, order), r_y3, r_x3)), axis=0)
-    z_last = Fold(last)
-    order = z_up0.back(last)
+    order = z_up0.back(order)
     order = z_last.middle(order)
     order = z_up1.back(order)
     order = z_last.back(order)

time: 301 us -> 290 us (0.963)
  Pallas kernels: 103 us -> 94 us
  waiting for transfers between devices: 93.2 us -> 98.5 us
  starting transfers between devices: 62.6 us -> 58.1 us
    pallas_call x22, Pallas kernels: 103 us -> 94 us  [call(): pl.pallas_call(body, out_shape=[make(s, d) for s, d in outs], scratch_sha...]
    ppermute x66, waiting for transfers between devices: 93.2 us -> 98.5 us  [swap(): return lax.ppermute(value, axis, [(s, s ^ mask) for s in range(size)])]
    ppermute x66, starting transfers between devices: 62.6 us -> 58.1 us  [swap(): return lax.ppermute(value, axis, [(s, s ^ mask) for s in range(size)])]
  transfers between devices with their start and end apart: 66 -> 66, of which waited for: 25 -> 26; matrix products, arithmetic and copies ran while one was open for 5% -> 5% of each run, Pallas kernels for 23% -> 20%
where the time goes in v3:
time: 290 us; the launch traced here: 289 us
  waiting for transfers between devices  98.5 us (34%)
  Pallas kernels  94 us (32%)
  starting transfers between devices  58.1 us (20%)
  local copies, waits for them, and re-layouts  19.6 us (7%)
  other arithmetic  14.2 us (5%)
  between operations  4.86 us (2%)
    ppermute x66, waiting for transfers between devices, swap(): return lax.ppermute(value, axis, [(s, s ^ mask) for s in range(size)])  98.5 us
    pallas_call x22, Pallas kernels, call(): pl.pallas_call(body, out_shape=[make(s, d) for s, d in outs], scratch_sha...  94 us
    ppermute x66, starting transfers between devices, swap(): return lax.ppermute(value, axis, [(s, s ^ mask) for s in range(size)])  58.1 us
    unnamed x182, local copies, waits for them, and re-layouts  13.8 us
  transfers between devices with their start and end apart: 66, of which 26 were waited for; matrix products, arithmetic and copies ran while one was open for 5% of the time, Pallas kernels for 20%

profile of v3, /device:TPU:0, one launch (start us, length us, event | category | flops | bytes accessed | tf_op | source)
XLA Modules:
  0.0 289.2 jit_solution(7790631597195077729)
XLA Ops:
  2.0 3.1 %split_positions.2 = (bf16[192,512]{1,0:T(8,128)(2,1)}, bf16[192,512]{1,0:T(8,128)(2,1)}, bf16[192,512]{1,0:T(8,128)(2,1)}, bf16[192,512]{1,0:T(8,128)(2,1)}) custom-call(s32[1]{0:T(128)} %bitcast.row_ref, f32[192,2048]{1,0:T(8,128)} %in_ref.1), custom_call_target="tpu_custom_call" | custom-call | flops 1000 | bytes 1000 | tf_op jit(solution)/shard_map/split_positions/pallas_call | solution.py:50
  5.1 2.1 narrow_a.1.refs_4_.refs_0_
  7.2 3.0 %collective-permute-start.6 = (bf16[208,1152]{1,0:T(8,128)(2,1)}, bf16[208,1152]{1,0:T(8,128)(2,1)S(1)}, u32[]{:S(2)}, u32[]{:S(2)}) collective-permute-start(bf16[208,1152]{1,0:T(8,128)(2,1)} %narrow_a.1.refs_4_.refs_0_), channel_id=1, source_target_pairs={{0,1},{1,0},{2,3},{3,2},{4,5},{5,4},{6,7},{7,6},{8,9},{9,8},{10,11... | collective-permute-start | bytes 1437704 | tf_op jit(solution)/shard_map/ppermute | solution.py:608
  12.6 13.0 %collective-permute-done.7.refs_13_.om1_ref = bf16[6,64,256]{2,1,0:T(8,128)(2,1)S(1)} collective-permute-done((bf16[6,64,256]{2,1,0:T(8,128)(2,1)S(1)}, bf16[6,64,256]{2,1,0:T(8,128)(2,1)S(1)}, u32[]{:S(2)}, u32[]{:S(2)}) %collective-permute-start.7) | collective-permute-done | bytes 196640 | tf_op jit(solution)/shard_map/ppermute | solution.py:608
  25.6 1.8 collective-permute-start.8
  27.4 3.5 %narrow_b.1.refs_4_.refs_14_.refs_24_.refs_0_ = bf16[192,3456]{1,0:T(8,128)(2,1)} custom-call(f32[192,384]{1,0:T(8,128)} %refs_0_.1, f32[192,1536]{1,0:T(8,128)} %refs_1_.3, f32[192,1536]{1,0:T(8,128)} %refs_2_.3), custom_call_target="tpu_custom_call" | custom-call | flops 1000 | bytes 1000 | tf_op jit(solution)/shard_map/narrow_b/pallas_call | solution.py:50
  35.5 2.0 collective-permute-done.11
  37.5 2.6 collective-permute-start.12
  40.1 1.9 collective-permute-done.12
  45.7 11.2 %attention_in.1 = (bf16[768,512]{1,0:T(8,128)(2,1)}, bf16[3072,512]{1,0:T(8,128)(2,1)}, bf16[3072,512]{1,0:T(8,128)(2,1)}, bf16[768,512]{1,0:T(8,128)(2,1)}, bf1...) custom-call(bf16[192,512]{1,0:T(8,128)(2,1)} %get-tuple-element.126., ...), custom_call_target="tpu_custom_call" | custom-call | flops 1000 | bytes 1000 | tf_op jit(solution)/shard_map/attention_in/pallas_call | solution.py:50
  57.2 1.8 collective-permute-done.13
  60.1 3.2 %split_positions.3 = (bf16[192,512]{1,0:T(8,128)(2,1)}, bf16[192,512]{1,0:T(8,128)(2,1)}, bf16[192,512]{1,0:T(8,128)(2,1)}, bf16[192,512]{1,0:T(8,128)(2,1)}) custom-call(s32[1]{0:T(128)} %bitcast.row_ref, f32[192,2048]{1,0:T(8,128)} %in_ref.2), custom_call_target="tpu_custom_call" | custom-call | flops 1000 | bytes 1000 | tf_op jit(solution)/shard_map/split_positions/pallas_call | solution.py:50
  67.1 7.8 %collective-permute-done.18.refs_8_.refs_18_.refs_28_.refs_4_ = bf16[192,3456]{1,0:T(8,128)(2,1)S(1)} collective-permute-done((bf16[192,3456]{1,0:T(8,128)(2,1)}, bf16[192,3456]{1,0:T(8,128)(2,1)S(1)}, u32[]{:S(2)}, u32[]{:S(2)}) %collective-permute-start.18) | collective-permute-done | bytes 1327136 | tf_op jit(solution)/shard_map/ppermute | solution.py:608
  75.0 7.3 %collective-permute-done.21.refs_37_ = bf16[192,512]{1,0:T(8,128)(2,1)S(1)} collective-permute-done((bf16[192,512]{1,0:T(8,128)(2,1)S(1)}, bf16[192,512]{1,0:T(8,128)(2,1)S(1)}, u32[]{:S(2)}, u32[]{:S(2)}) %collective-permute-start.21) | collective-permute-done | bytes 196640 | tf_op jit(solution)/shard_map/ppermute | solution.py:608
  82.8 1.7 collective-permute-done.22.refs_39_
  84.6 2.1 collective-permute-start.17
  86.7 5.9 %collective-permute-done.19.refs_9_.refs_19_.refs_29_.refs_5_ = bf16[48,3456]{1,0:T(8,128)(2,1)S(1)} collective-permute-done((bf16[48,3456]{1,0:T(8,128)(2,1)S(1)}, bf16[48,3456]{1,0:T(8,128)(2,1)S(1)}, u32[]{:S(2)}, u32[]{:S(2)}) %collective-permute-start.19) | collective-permute-done | bytes 331808 | tf_op jit(solution)/shard_map/ppermute | solution.py:608
  92.6 3.2 %collective-permute-done.20.refs_10_.refs_20_.refs_30_.refs_6_ = bf16[144,3456]{1,0:T(8,128)(2,1)S(1)} collective-permute-done((bf16[144,3456]{1,0:T(8,128)(2,1)S(1)}, bf16[144,3456]{1,0:T(8,128)(2,1)S(1)}, u32[]{:S(2)}, u32[]{:S(2)}) %collective-permute-start.20) | collective-permute-done | bytes 995360 | tf_op jit(solution)/shard_map/ppermute | solution.py:608
  96.4 2.7 collective-permute-done.26.refs_38_
  101.3 21.2 %middle.1 = (bf16[864,256]{1,0:T(8,128)(2,1)}, bf16[768,512]{1,0:T(8,128)(2,1)}, f32[16,512]{1,0:T(8,128)}, bf16[768,512]{1,0:T(8,128)(2,1)}, f32[8,512]{1,0:T(8...) custom-call(bf16[864,256]{1,0:T(8,128)(2,1)} %copy-done.73, ...), custom_call_target="tpu_custom_call" | custom-call | flops 1000 | bytes 1000 | tf_op jit(solution)/shard_map/middle/pallas_call | solution.py:50
  123.6 1.9 copy-done.24
  125.6 2.8 down_theirs.1
  132.3 7.6 %down_back.1 = (bf16[2,1536,512]{2,1,0:T(8,128)(2,1)}, f32[2,8,1536]{2,1,0:T(8,128)S(1)}, f32[8,768]{1,0:T(8,128)S(1)}) custom-call(bf16[768,512]{1,0:T(8,128)(2,1)S(1)} %copy-done.23, bf16[2,1536,512]{2,1,0:T(8,128)(2,1)} %get-tuple-element.154.slope_ref, bf16[192,3456]{1,0:T(8,128)(2,1)S(1)} %copy-done.1, bf16[192,3456]{1,0:T(8,128)(2,1)S(1)} %copy-done.3, ...), custom_call_target="tpu_custom_call" | custom-call | flops 1000 | bytes 1000 | tf_op jit(solution)/shard_map/down_back/pallas_call | solution.py:50
  140.0 4.1 %down_mine.1 = (bf16[384,768]{1,0:T(8,128)(2,1)S(1)}, bf16[384,768]{1,0:T(8,128)(2,1)S(1)}, bf16[384,768]{1,0:T(8,128)(2,1)S(1)}, bf16[384,768]{1,0:T(8,128)(2,1)}) custom-call(bf16[768,512]{1,0:T(8,128)(2,1)S(1)} %copy-done.23, bf16[2,1536,512]{2,1,0:T(8,128)(2,1)S(1)} %copy-done.24, bf16[2,384,1536]{2,1,0:T(8,128)(2,1)S(1)} %collective-permute-done.27.got_ref), custom_call_target="tpu_custom_call" | custom-call | flops 1000 | bytes 1000 | tf_op jit(solution)/shard_map/down_mine/pallas_call | solution.py:50
  146.5 6.7 %up_back.1 = (bf16[768,512]{1,0:T(8,128)(2,1)S(1)}, f32[24,768]{1,0:T(8,128)S(1)}) custom-call(bf16[2,1536,512]{2,1,0:T(8,128)(2,1)} %get-tuple-element.159.gu_ref.r_ref, bf16[768,512]{1,0:T(8,128)(2,1)S(1)} %copy-done.23, bf16[768,512]{1,0:T(8,128)(2,1)S(1)} %copy-done.41, f32[8,512]{1,0:T(8,128)S(1)} %copy-done.70, f32[8,768]{1,0:T(8,128)S(1)} %copy-done.66, ...), custom_call_target="tpu_custom_call" | custom-call | flops 1000 | bytes 1000 | tf_op jit(solution)/shard_map/up_back/pallas_call | solution.py:50
  153.9 3.7 %attention_mid.1 = (bf16[864,512]{1,0:T(8,128)(2,1)S(1)}, bf16[864,256]{1,0:T(8,128)(2,1)S(1)}) custom-call(bf16[768,512]{1,0:T(8,128)(2,1)S(1)} %get-tuple-element.211.go_ref, bf16[768,512]{1,0:T(8,128)(2,1)S(1)} %copy-done.29, f32[16,512]{1,0:T(8,128)S(1)} %copy-done.69, bf16[3072,512]{1,0:T(8,128)(2,1)} %get-tuple-element.134.refs_2_.fq_ref, ...), custom_call_target="tpu_custom_call" | custom-call | flops 1000 | bytes 1000 | tf_op jit(solution)/shard_map/attention_mid/pallas_call | solution.py:50
  157.7 2.1 collective-permute-done.31
  159.8 2.8 up_theirs.1
  164.4 3.5 %collective-permute-done.33 = bf16[864,256]{1,0:T(8,128)(2,1)S(1)} collective-permute-done((bf16[864,256]{1,0:T(8,128)(2,1)S(1)}, bf16[864,256]{1,0:T(8,128)(2,1)S(1)}, u32[]{:S(2)}, u32[]{:S(2)}) %collective-permute-start.33) | collective-permute-done | bytes 442400 | tf_op jit(solution)/shard_map/ppermute | solution.py:608
  168.8 2.8 query_back.1
  173.0 4.0 %up_mine.1 = (bf16[384,768]{1,0:T(8,128)(2,1)S(1)}, bf16[384,768]{1,0:T(8,128)(2,1)S(1)}, bf16[384,768]{1,0:T(8,128)(2,1)}, bf16[384,768]{1,0:T(8,128)(2,1)S(1)}) custom-call(bf16[768,512]{1,0:T(8,128)(2,1)S(1)} %copy-done.32, bf16[2,1536,512]{2,1,0:T(8,128)(2,1)S(1)} %copy-done.20, bf16[2,384,1536]{2,1,0:T(8,128)(2,1)S(1)} %collective-permute-done.34.got_ref), custom_call_target="tpu_custom_call" | custom-call | flops 1000 | bytes 1000 | tf_op jit(solution)/shard_map/up_mine/pallas_call | solution.py:50
  187.4 6.3 %collective-permute-done.36.gkv1_ref = bf16[864,256]{1,0:T(8,128)(2,1)S(1)} collective-permute-done((bf16[864,256]{1,0:T(8,128)(2,1)}, bf16[864,256]{1,0:T(8,128)(2,1)S(1)}, u32[]{:S(2)}, u32[]{:S(2)}) %collective-permute-start.36) | collective-permute-done | bytes 442400 | tf_op jit(solution)/shard_map/ppermute | solution.py:608
  194.8 3.6 %key_back.1 = (bf16[1536,512]{1,0:T(8,128)(2,1)S(1)}, f32[8,1536]{1,0:T(8,128)S(1)}) custom-call(bf16[864,256]{1,0:T(8,128)(2,1)S(1)} %copy-done.40, bf16[864,256]{1,0:T(8,128)(2,1)S(1)} %collective-permute-done.36.gkv1_ref, bf16[3072,512]{1,0:T(8,128)(2,1)S(1)} %copy-done.33, bf16[768,512]{1,0:T(8,128)(2,1)S(1)} %copy-done.42, ...), custom_call_target="tpu_custom_call" | custom-call | flops 1000 | bytes 1000 | tf_op jit(solution)/shard_map/key_back/pallas_call | solution.py:50
  204.9 2.6 collective-permute-start.45
  208.4 2.9 %collective-permute-done.41 = bf16[192,768]{1,0:T(8,128)(2,1)S(1)} collective-permute-done((bf16[192,768]{1,0:T(8,128)(2,1)S(1)}, bf16[192,768]{1,0:T(8,128)(2,1)S(1)}, u32[]{:S(2)}, u32[]{:S(2)}) %collective-permute-start.41) | collective-permute-done | bytes 294944 | tf_op jit(solution)/shard_map/ppermute | solution.py:608
  217.0 3.0 %collective-permute-done.43 = bf16[384,768]{1,0:T(8,128)(2,1)S(1)} collective-permute-done((bf16[384,768]{1,0:T(8,128)(2,1)S(1)}, bf16[384,768]{1,0:T(8,128)(2,1)S(1)}, u32[]{:S(2)}, u32[]{:S(2)}) %collective-permute-start.43) | collective-permute-done | bytes 589856 | tf_op jit(solution)/shard_map/ppermute | solution.py:608
  222.2 2.6 collective-permute-start.50
  224.8 3.9 %input_grad.1 = (bf16[192,512]{1,0:T(8,128)(2,1)S(1)}, bf16[192,512]{1,0:T(8,128)(2,1)S(1)}, bf16[192,512]{1,0:T(8,128)(2,1)S(1)}, bf16[192,512]{1,0:T(8,128)(2,1)S(1)}) custom-call(bf16[2,384,512]{2,1,0:T(8,128)(2,1)S(1)} %bitcast.23, bf16[2,768,512]{2,1,0:T(8,128)(2,1)S(1)} %bitcast.20, bf16[768,512]{1,0:T(8,128)(2,1)S(1)} %get-tuple-element.211.go_ref, ...), custom_call_target="tpu_custom_call" | custom-call | flops 1000 | bytes 1000 | tf_op jit(solution)/shard_map/input_grad/pallas_call | solution.py:50
  233.4 6.0 %collective-permute-done.48 = bf16[192,768]{1,0:T(8,128)(2,1)S(1)} collective-permute-done((bf16[192,768]{1,0:T(8,128)(2,1)S(1)}, bf16[192,768]{1,0:T(8,128)(2,1)S(1)}, u32[]{:S(2)}, u32[]{:S(2)}) %collective-permute-start.48) | collective-permute-done | bytes 294944 | tf_op jit(solution)/shard_map/ppermute | solution.py:608
  240.6 2.7 collective-permute-start.54
  248.3 6.8 %collective-permute-done.53 = bf16[192,384]{1,0:T(8,128)(2,1)S(1)} collective-permute-done((bf16[192,384]{1,0:T(8,128)(2,1)S(1)}, bf16[192,384]{1,0:T(8,128)(2,1)S(1)}, u32[]{:S(2)}, u32[]{:S(2)}) %collective-permute-start.53) | collective-permute-done | bytes 147488 | tf_op jit(solution)/shard_map/ppermute | solution.py:608
  255.1 1.9 collective-permute-start.56
  257.0 1.8 collective-permute-start.62
  258.9 4.3 %collective-permute-done.55 = bf16[400,384]{1,0:T(8,128)(2,1)S(1)} collective-permute-done((bf16[400,384]{1,0:T(8,128)(2,1)S(1)}, bf16[400,384]{1,0:T(8,128)(2,1)S(1)}, u32[]{:S(2)}, u32[]{:S(2)}) %collective-permute-start.55) | collective-permute-done | bytes 307232 | tf_op jit(solution)/shard_map/ppermute | solution.py:608
  264.5 2.6 collective-permute-done.56
  268.1 7.2 %collective-permute-done.57 = bf16[400,384]{1,0:T(8,128)(2,1)S(1)} collective-permute-done((bf16[400,384]{1,0:T(8,128)(2,1)S(1)}, bf16[400,384]{1,0:T(8,128)(2,1)S(1)}, u32[]{:S(2)}, u32[]{:S(2)}) %collective-permute-start.57) | collective-permute-done | bytes 307232 | tf_op jit(solution)/shard_map/ppermute | solution.py:608
  279.6 1.7 join_positions.3
  281.3 2.6 collective-permute-done.58
  (342 shorter events, 78.9 us)
Async XLA Ops:
  7.2 18.4 %collective-permute-start.6 = (bf16[208,1152]{1,0:T(8,128)(2,1)}, bf16[208,1152]{1,0:T(8,128)(2,1)S(1)}, u32[]{:S(2)}, u32[]{:S(2)}) collective-permute-start(bf16[208,1152]{1,0:T(8,128)(2,1)} %narrow_a.1.refs_4_.refs_0_), channel_id=1, source_target_pairs={{0,1},{1,0},{2,3},{3,2},{4,5},{5,4},{6,7},{7,6},{8,9},{9,8},{10,11... | collective-permute-start | bytes 1437704 | tf_op jit(solution)/shard_map/ppermute | solution.py:608
  10.2 15.4 %collective-permute-start.3 = (bf16[208,1152]{1,0:T(8,128)(2,1)}, bf16[208,1152]{1,0:T(8,128)(2,1)}, u32[]{:S(2)}, u32[]{:S(2)}) collective-permute-start(bf16[208,1152]{1,0:T(8,128)(2,1)} %narrow_a.1.refs_4_.refs_0_), channel_id=1, source_target_pairs={{0,4},{2,6},{4,0},{6,2},{1,5},{3,7},{5,1},{7,3},{8,12},{10,14},{12... | collective-permute-start | bytes 1437704 | tf_op jit(solution)/shard_map/ppermute | solution.py:608
  11.7 13.9 %collective-permute-start.7 = (bf16[6,64,256]{2,1,0:T(8,128)(2,1)S(1)}, bf16[6,64,256]{2,1,0:T(8,128)(2,1)S(1)}, u32[]{:S(2)}, u32[]{:S(2)}) collective-permute-start(bf16[6,64,256]{2,1,0:T(8,128)(2,1)S(1)} %copy-done.36), channel_id=1, source_target_pairs={{0,1},{1,0},{2,3},{3,2},{4,5},{5,4},{6,7},{7,6},{8,9},{9,8},{10,11... | collective-permute-start | bytes 589832 | tf_op jit(solution)/shard_map/ppermute | solution.py:608
  12.2 18.8 %collective-permute-start = (bf16[192,512]{1,0:T(8,128)(2,1)S(1)}, bf16[192,512]{1,0:T(8,128)(2,1)S(1)}, u32[]{:S(2)}, u32[]{:S(2)}) collective-permute-start(bf16[192,512]{1,0:T(8,128)(2,1)S(1)} %copy-done.87), channel_id=1, source_target_pairs={{0,4},{2,6},{4,0},{6,2},{1,5},{3,7},{5,1},{7,3},{8,12},{10,14},{12... | collective-permute-start | bytes 589832 | tf_op jit(solution)/shard_map/ppermute | solution.py:608
  12.3 18.7 %collective-permute-start.2 = (bf16[192,512]{1,0:T(8,128)(2,1)S(1)}, bf16[192,512]{1,0:T(8,128)(2,1)S(1)}, u32[]{:S(2)}, u32[]{:S(2)}) collective-permute-start(bf16[192,512]{1,0:T(8,128)(2,1)S(1)} %copy-done.86), channel_id=1, source_target_pairs={{0,6},{2,4},{4,2},{6,0},{1,7},{3,5},{5,3},{7,1},{8,14},{10,12},{12... | collective-permute-start | bytes 589832 | tf_op jit(solution)/shard_map/ppermute | solution.py:608
  25.6 17.0 %collective-permute-start.8 = (bf16[208,1152]{1,0:T(8,128)(2,1)}, bf16[208,1152]{1,0:T(8,128)(2,1)}, u32[]{:S(2)}, u32[]{:S(2)}) collective-permute-start(bf16[208,1152]{1,0:T(8,128)(2,1)} %collective-permute-done.3.refs_5_.refs_1_), channel_id=1, source_target_pairs={{0,1},{1,0},{2,3},{3,2},{4,5},{5,4},{6,7},{7,6},{8,9},{9,8},{10,11... | collective-permute-start | bytes 1437704 | tf_op jit(solution)/shard_map/ppermute | solution.py:608
  27.4 15.3 %collective-permute-start.4 = (bf16[208,1152]{1,0:T(8,128)(2,1)}, bf16[208,1152]{1,0:T(8,128)(2,1)}, u32[]{:S(2)}, u32[]{:S(2)}) collective-permute-start(bf16[208,1152]{1,0:T(8,128)(2,1)} %narrow_a.1.refs_4_.refs_0_), channel_id=1, source_target_pairs={{0,2},{2,0},{4,6},{6,4},{1,3},{3,1},{5,7},{7,5},{8,10},{10,8},{12,... | collective-permute-start | bytes 1437704 | tf_op jit(solution)/shard_map/ppermute | solution.py:608
  31.0 32.3 %collective-permute-start.15 = (bf16[192,3456]{1,0:T(8,128)(2,1)}, bf16[192,3456]{1,0:T(8,128)(2,1)S(1)}, u32[]{:S(2)}, u32[]{:S(2)}) collective-permute-start(bf16[192,3456]{1,0:T(8,128)(2,1)} %narrow_b.1.refs_4_.refs_14_.refs_24_.refs_0_), channel_id=1, source_target_pairs={{0,4},{2,6},{4,0},{6,2},{1,5},{3,7},{5,1},{7,3},{8,12},{10,14},{12... | collective-permute-start | bytes 3981320 | tf_op jit(solution)/shard_map/ppermute | solution.py:608
  42.7 32.2 %collective-permute-start.18 = (bf16[192,3456]{1,0:T(8,128)(2,1)}, bf16[192,3456]{1,0:T(8,128)(2,1)S(1)}, u32[]{:S(2)}, u32[]{:S(2)}) collective-permute-start(bf16[192,3456]{1,0:T(8,128)(2,1)} %narrow_b.1.refs_4_.refs_14_.refs_24_.refs_0_), channel_id=1, source_target_pairs={{0,1},{1,0},{2,3},{3,2},{4,5},{5,4},{6,7},{7,6},{8,9},{9,8},{10,11... | collective-permute-start | bytes 3981320 | tf_op jit(solution)/shard_map/ppermute | solution.py:608
  63.5 32.4 %collective-permute-start.20 = (bf16[144,3456]{1,0:T(8,128)(2,1)S(1)}, bf16[144,3456]{1,0:T(8,128)(2,1)S(1)}, u32[]{:S(2)}, u32[]{:S(2)}) collective-permute-start(bf16[144,3456]{1,0:T(8,128)(2,1)S(1)} %slice.182), channel_id=1, source_target_pairs={{0,1},{1,0},{2,3},{3,2},{4,5},{5,4},{6,7},{7,6},{8,9},{9,8},{10,11... | collective-permute-start | bytes 2985992 | tf_op jit(solution)/shard_map/ppermute | solution.py:608
  65.0 21.6 %collective-permute-start.14 = (bf16[864,256]{1,0:T(8,128)(2,1)S(1)}, bf16[864,256]{1,0:T(8,128)(2,1)S(1)}, u32[]{:S(2)}, u32[]{:S(2)}) collective-permute-start(bf16[864,256]{1,0:T(8,128)(2,1)S(1)} %add.129.refs_0_), channel_id=1, source_target_pairs={{0,4},{2,6},{4,0},{6,2},{1,5},{3,7},{5,1},{7,3},{8,12},{10,14},{12... | collective-permute-start | bytes 1327112 | tf_op jit(solution)/shard_map/ppermute | solution.py:608
  65.6 30.8 %collective-permute-start.16 = (bf16[192,3456]{1,0:T(8,128)(2,1)S(1)}, bf16[192,3456]{1,0:T(8,128)(2,1)S(1)}, u32[]{:S(2)}, u32[]{:S(2)}) collective-permute-start(bf16[192,3456]{1,0:T(8,128)(2,1)S(1)} %copy-done), channel_id=1, source_target_pairs={{0,2},{2,0},{4,6},{6,4},{1,3},{3,1},{5,7},{7,5},{8,10},{10,8},{12,... | collective-permute-start | bytes 3981320 | tf_op jit(solution)/shard_map/ppermute | solution.py:608
  65.6 16.7 %collective-permute-start.21 = (bf16[192,512]{1,0:T(8,128)(2,1)S(1)}, bf16[192,512]{1,0:T(8,128)(2,1)S(1)}, u32[]{:S(2)}, u32[]{:S(2)}) collective-permute-start(bf16[192,512]{1,0:T(8,128)(2,1)S(1)} %copy-done.89), channel_id=1, source_target_pairs={{0,4},{2,6},{4,0},{6,2},{1,5},{3,7},{5,1},{7,3},{8,12},{10,14},{12... | collective-permute-start | bytes 589832 | tf_op jit(solution)/shard_map/ppermute | solution.py:608
  82.3 10.3 %collective-permute-start.19 = (bf16[48,3456]{1,0:T(8,128)(2,1)S(1)}, bf16[48,3456]{1,0:T(8,128)(2,1)S(1)}, u32[]{:S(2)}, u32[]{:S(2)}) collective-permute-start(bf16[48,3456]{1,0:T(8,128)(2,1)S(1)} %slice.181), channel_id=1, source_target_pairs={{0,4},{2,6},{4,0},{6,2},{1,5},{3,7},{5,1},{7,3},{8,12},{10,14},{12... | collective-permute-start | bytes 995336 | tf_op jit(solution)/shard_map/ppermute | solution.py:608
  84.6 14.6 %collective-permute-start.17 = (bf16[192,3456]{1,0:T(8,128)(2,1)S(1)}, bf16[192,3456]{1,0:T(8,128)(2,1)S(1)}, u32[]{:S(2)}, u32[]{:S(2)}) collective-permute-start(bf16[192,3456]{1,0:T(8,128)(2,1)S(1)} %collective-permute-done.15.refs_5_.refs_15_.refs_25_.refs_1_), channel_id=1, source_target_pairs={{0,2},{2,0},{4,6},{6,4},{1,3},{3,1},{5,7},{7,5},{8,10},{10,8},{12,... | collective-permute-start | bytes 3981320 | tf_op jit(solution)/shard_map/ppermute | solution.py:608
  86.6 12.6 %collective-permute-start.23 = (bf16[192,3456]{1,0:T(8,128)(2,1)S(1)}, bf16[192,3456]{1,0:T(8,128)(2,1)S(1)}, u32[]{:S(2)}, u32[]{:S(2)}) collective-permute-start(bf16[192,3456]{1,0:T(8,128)(2,1)S(1)} %collective-permute-done.18.refs_8_.refs_18_.refs_28_.refs_4_), channel_id=1, source_target_pairs={{0,2},{2,0},{4,6},{6,4},{1,3},{3,1},{5,7},{7,5},{8,10},{10,8},{12,... | collective-permute-start | bytes 3981320 | tf_op jit(solution)/shard_map/ppermute | solution.py:608
  128.3 11.6 %collective-permute-start.27 = (bf16[2,384,1536]{2,1,0:T(8,128)(2,1)S(1)}, bf16[2,384,1536]{2,1,0:T(8,128)(2,1)S(1)}, u32[]{:S(2)}, u32[]{:S(2)}) collective-permute-start(bf16[2,384,1536]{2,1,0:T(8,128)(2,1)S(1)} %down_theirs.1), channel_id=1, source_target_pairs={{0,2},{2,0},{4,6},{6,4},{1,3},{3,1},{5,7},{7,5},{8,10},{10,8},{12,... | collective-permute-start | bytes 7077896 | tf_op jit(solution)/shard_map/ppermute | solution.py:608
  144.1 15.7 %collective-permute-start.31 = (bf16[384,768]{1,0:T(8,128)(2,1)S(1)}, bf16[384,768]{1,0:T(8,128)(2,1)S(1)}, u32[]{:S(2)}, u32[]{:S(2)}) collective-permute-start(bf16[384,768]{1,0:T(8,128)(2,1)S(1)} %get-tuple-element.158), channel_id=1, source_target_pairs={{0,1},{1,0},{2,3},{3,2},{4,5},{5,4},{6,7},{7,6},{8,9},{9,8},{10,11... | collective-permute-start | bytes 1769480 | tf_op jit(solution)/shard_map/ppermute | solution.py:608
  144.6 13.0 %collective-permute-start.28 = (bf16[192,512]{1,0:T(8,128)(2,1)S(1)}, bf16[192,512]{1,0:T(8,128)(2,1)S(1)}, u32[]{:S(2)}, u32[]{:S(2)}) collective-permute-start(bf16[192,512]{1,0:T(8,128)(2,1)S(1)} %copy-done.85), channel_id=1, source_target_pairs={{0,2},{2,0},{4,6},{6,4},{1,3},{3,1},{5,7},{7,5},{8,10},{10,8},{12,... | collective-permute-start | bytes 589832 | tf_op jit(solution)/shard_map/ppermute | solution.py:608
  144.7 12.9 %collective-permute-start.29 = (bf16[192,512]{1,0:T(8,128)(2,1)S(1)}, bf16[192,512]{1,0:T(8,128)(2,1)S(1)}, u32[]{:S(2)}, u32[]{:S(2)}) collective-permute-start(bf16[192,512]{1,0:T(8,128)(2,1)S(1)} %copy-done.83), channel_id=1, source_target_pairs={{0,4},{2,6},{4,0},{6,2},{1,5},{3,7},{5,1},{7,3},{8,12},{10,14},{12... | collective-permute-start | bytes 589832 | tf_op jit(solution)/shard_map/ppermute | solution.py:608
  145.1 12.5 %collective-permute-start.30 = (bf16[192,512]{1,0:T(8,128)(2,1)S(1)}, bf16[192,512]{1,0:T(8,128)(2,1)S(1)}, u32[]{:S(2)}, u32[]{:S(2)}) collective-permute-start(bf16[192,512]{1,0:T(8,128)(2,1)S(1)} %copy-done.82), channel_id=1, source_target_pairs={{0,6},{2,4},{4,2},{6,0},{1,7},{3,5},{5,3},{7,1},{8,14},{10,12},{12... | collective-permute-start | bytes 589832 | tf_op jit(solution)/shard_map/ppermute | solution.py:608
  162.7 10.3 %collective-permute-start.34 = (bf16[2,384,1536]{2,1,0:T(8,128)(2,1)S(1)}, bf16[2,384,1536]{2,1,0:T(8,128)(2,1)S(1)}, u32[]{:S(2)}, u32[]{:S(2)}) collective-permute-start(bf16[2,384,1536]{2,1,0:T(8,128)(2,1)S(1)} %up_theirs.1), channel_id=1, source_target_pairs={{0,2},{2,0},{4,6},{6,4},{1,3},{3,1},{5,7},{7,5},{8,10},{10,8},{12,... | collective-permute-start | bytes 7077896 | tf_op jit(solution)/shard_map/ppermute | solution.py:608
  163.8 17.1 %collective-permute-start.35 = (bf16[384,768]{1,0:T(8,128)(2,1)}, bf16[384,768]{1,0:T(8,128)(2,1)}, u32[]{:S(2)}, u32[]{:S(2)}) collective-permute-start(bf16[384,768]{1,0:T(8,128)(2,1)} %get-tuple-element.182), channel_id=1, source_target_pairs={{0,1},{1,0},{2,3},{3,2},{4,5},{5,4},{6,7},{7,6},{8,9},{9,8},{10,11... | collective-permute-start | bytes 1769480 | tf_op jit(solution)/shard_map/ppermute | solution.py:608
  179.4 19.0 %collective-permute-start.37 = (bf16[384,768]{1,0:T(8,128)(2,1)}, bf16[384,768]{1,0:T(8,128)(2,1)}, u32[]{:S(2)}, u32[]{:S(2)}) collective-permute-start(bf16[384,768]{1,0:T(8,128)(2,1)} %get-tuple-element.180), channel_id=1, source_target_pairs={{0,1},{1,0},{2,3},{3,2},{4,5},{5,4},{6,7},{7,6},{8,9},{9,8},{10,11... | collective-permute-start | bytes 1769480 | tf_op jit(solution)/shard_map/ppermute | solution.py:608
  180.4 13.3 %collective-permute-start.36 = (bf16[864,256]{1,0:T(8,128)(2,1)}, bf16[864,256]{1,0:T(8,128)(2,1)S(1)}, u32[]{:S(2)}, u32[]{:S(2)}) collective-permute-start(bf16[864,256]{1,0:T(8,128)(2,1)} %add.134.gkv0_ref), channel_id=1, source_target_pairs={{0,4},{2,6},{4,0},{6,2},{1,5},{3,7},{5,1},{7,3},{8,12},{10,14},{12... | collective-permute-start | bytes 1327112 | tf_op jit(solution)/shard_map/ppermute | solution.py:608
  182.0 17.5 %collective-permute-start.38 = (bf16[192,768]{1,0:T(8,128)(2,1)S(1)}, bf16[192,768]{1,0:T(8,128)(2,1)S(1)}, u32[]{:S(2)}, u32[]{:S(2)}) collective-permute-start(bf16[192,768]{1,0:T(8,128)(2,1)S(1)} %slice_add_fusion.9), channel_id=1, source_target_pairs={{0,4},{2,6},{4,0},{6,2},{1,5},{3,7},{5,1},{7,3},{8,12},{10,14},{12... | collective-permute-start | bytes 884744 | tf_op jit(solution)/shard_map/ppermute | solution.py:608
  184.7 15.9 %collective-permute-start.39 = (bf16[192,384]{1,0:T(8,128)(2,1)S(1)}, bf16[192,384]{1,0:T(8,128)(2,1)S(1)}, u32[]{:S(2)}, u32[]{:S(2)}) collective-permute-start(bf16[192,384]{1,0:T(8,128)(2,1)S(1)} %get-tuple-element.266), channel_id=1, source_target_pairs={{0,8},{8,0},{16,24},{24,16},{1,9},{9,1},{17,25},{25,17},{2,10},{10... | collective-permute-start | bytes 442376 | tf_op jit(solution)/shard_map/ppermute | solution.py:608
  187.3 20.2 %collective-permute-start.40 = (bf16[2,384,768]{2,1,0:T(8,128)(2,1)S(1)}, bf16[2,384,768]{2,1,0:T(8,128)(2,1)S(1)}, u32[]{:S(2)}, u32[]{:S(2)}) collective-permute-start(bf16[2,384,768]{2,1,0:T(8,128)(2,1)S(1)} %pair_theirs.1), channel_id=1, source_target_pairs={{0,2},{2,0},{4,6},{6,4},{1,3},{3,1},{5,7},{7,5},{8,10},{10,8},{12,... | collective-permute-start | bytes 3538952 | tf_op jit(solution)/shard_map/ppermute | solution.py:608
  201.9 10.5 %collective-permute-start.42 = (bf16[2,2,208,768]{3,2,1,0:T(8,128)(2,1)S(1)}, bf16[2,2,208,768]{3,2,1,0:T(8,128)(2,1)S(1)}, u32[]{:S(2)}, u32[]{:S(2)}) collective-permute-start(bf16[2,2,208,768]{3,2,1,0:T(8,128)(2,1)S(1)} %last_theirs.1), channel_id=1, source_target_pairs={{0,2},{2,0},{4,6},{6,4},{1,3},{3,1},{5,7},{7,5},{8,10},{10,8},{12,... | collective-permute-start | bytes 3833864 | tf_op jit(solution)/shard_map/ppermute | solution.py:608
  203.7 16.3 %collective-permute-start.43 = (bf16[384,768]{1,0:T(8,128)(2,1)S(1)}, bf16[384,768]{1,0:T(8,128)(2,1)S(1)}, u32[]{:S(2)}, u32[]{:S(2)}) collective-permute-start(bf16[384,768]{1,0:T(8,128)(2,1)S(1)} %copy-done.72), channel_id=1, source_target_pairs={{0,1},{1,0},{2,3},{3,2},{4,5},{5,4},{6,7},{7,6},{8,9},{9,8},{10,11... | collective-permute-start | bytes 1769480 | tf_op jit(solution)/shard_map/ppermute | solution.py:608
  204.9 16.8 %collective-permute-start.45 = (bf16[192,384]{1,0:T(8,128)(2,1)S(1)}, bf16[192,384]{1,0:T(8,128)(2,1)S(1)}, u32[]{:S(2)}, u32[]{:S(2)}) collective-permute-start(bf16[192,384]{1,0:T(8,128)(2,1)S(1)} %add.139), channel_id=1, source_target_pairs={{0,16},{8,24},{16,0},{24,8},{1,17},{9,25},{17,1},{25,9},{2,18},{10... | collective-permute-start | bytes 442376 | tf_op jit(solution)/shard_map/ppermute | solution.py:608
  213.6 15.9 %collective-permute-start.46 = (bf16[416,768]{1,0:T(8,128)(2,1)S(1)}, bf16[416,768]{1,0:T(8,128)(2,1)S(1)}, u32[]{:S(2)}, u32[]{:S(2)}) collective-permute-start(bf16[416,768]{1,0:T(8,128)(2,1)S(1)} %get-tuple-element.205), channel_id=1, source_target_pairs={{0,4},{2,6},{4,0},{6,2},{1,5},{3,7},{5,1},{7,3},{8,12},{10,14},{12... | collective-permute-start | bytes 1916936 | tf_op jit(solution)/shard_map/ppermute | solution.py:608
  215.9 15.9 %collective-permute-start.47 = (bf16[384,768]{1,0:T(8,128)(2,1)S(1)}, bf16[384,768]{1,0:T(8,128)(2,1)S(1)}, u32[]{:S(2)}, u32[]{:S(2)}) collective-permute-start(bf16[384,768]{1,0:T(8,128)(2,1)S(1)} %get-tuple-element.200), channel_id=1, source_target_pairs={{0,1},{1,0},{2,3},{3,2},{4,5},{5,4},{6,7},{7,6},{8,9},{9,8},{10,11... | collective-permute-start | bytes 1769480 | tf_op jit(solution)/shard_map/ppermute | solution.py:608
  220.0 20.6 %collective-permute-start.49 = (bf16[192,384]{1,0:T(8,128)(2,1)S(1)}, bf16[192,384]{1,0:T(8,128)(2,1)S(1)}, u32[]{:S(2)}, u32[]{:S(2)}) collective-permute-start(bf16[192,384]{1,0:T(8,128)(2,1)S(1)} %get-tuple-element.262), channel_id=1, source_target_pairs={{0,8},{8,0},{16,24},{24,16},{1,9},{9,1},{17,25},{25,17},{2,10},{10... | collective-permute-start | bytes 442376 | tf_op jit(solution)/shard_map/ppermute | solution.py:608
  221.7 26.5 %collective-permute-start.64 = (bf16[192,384]{1,0:T(8,128)(2,1)S(1)}, bf16[192,384]{1,0:T(8,128)(2,1)S(1)}, u32[]{:S(2)}, u32[]{:S(2)}) collective-permute-start(bf16[192,384]{1,0:T(8,128)(2,1)S(1)} %add.144), channel_id=1, source_target_pairs={{0,8},{8,0},{16,24},{24,16},{1,9},{9,1},{17,25},{25,17},{2,10},{10... | collective-permute-start | bytes 442376 | tf_op jit(solution)/shard_map/ppermute | solution.py:608
  222.2 21.1 %collective-permute-start.50 = (bf16[192,384]{1,0:T(8,128)(2,1)S(1)}, bf16[192,384]{1,0:T(8,128)(2,1)S(1)}, u32[]{:S(2)}, u32[]{:S(2)}) collective-permute-start(bf16[192,384]{1,0:T(8,128)(2,1)S(1)} %add.143), channel_id=1, source_target_pairs={{0,16},{8,24},{16,0},{24,8},{1,17},{9,25},{17,1},{25,9},{2,18},{10... | collective-permute-start | bytes 442376 | tf_op jit(solution)/shard_map/ppermute | solution.py:608
  229.5 9.9 %collective-permute-start.48 = (bf16[192,768]{1,0:T(8,128)(2,1)S(1)}, bf16[192,768]{1,0:T(8,128)(2,1)S(1)}, u32[]{:S(2)}, u32[]{:S(2)}) collective-permute-start(bf16[192,768]{1,0:T(8,128)(2,1)S(1)} %slice_add_fusion.5), channel_id=1, source_target_pairs={{0,4},{2,6},{4,0},{6,2},{1,5},{3,7},{5,1},{7,3},{8,12},{10,14},{12... | collective-permute-start | bytes 884744 | tf_op jit(solution)/shard_map/ppermute | solution.py:608
  231.8 13.1 %collective-permute-start.52 = (bf16[192,768]{1,0:T(8,128)(2,1)S(1)}, bf16[192,768]{1,0:T(8,128)(2,1)S(1)}, u32[]{:S(2)}, u32[]{:S(2)}) collective-permute-start(bf16[192,768]{1,0:T(8,128)(2,1)S(1)} %slice_add_fusion.4), channel_id=1, source_target_pairs={{0,4},{2,6},{4,0},{6,2},{1,5},{3,7},{5,1},{7,3},{8,12},{10,14},{12... | collective-permute-start | bytes 884744 | tf_op jit(solution)/shard_map/ppermute | solution.py:608
  240.6 14.5 %collective-permute-start.54 = (bf16[192,384]{1,0:T(8,128)(2,1)S(1)}, bf16[192,384]{1,0:T(8,128)(2,1)S(1)}, u32[]{:S(2)}, u32[]{:S(2)}) collective-permute-start(bf16[192,384]{1,0:T(8,128)(2,1)S(1)} %add.149), channel_id=1, source_target_pairs={{0,16},{8,24},{16,0},{24,8},{1,17},{9,25},{17,1},{25,9},{2,18},{10... | collective-permute-start | bytes 442376 | tf_op jit(solution)/shard_map/ppermute | solution.py:608
  243.3 13.7 %collective-permute-start.65 = (bf16[192,384]{1,0:T(8,128)(2,1)S(1)}, bf16[192,384]{1,0:T(8,128)(2,1)S(1)}, u32[]{:S(2)}, u32[]{:S(2)}) collective-permute-start(bf16[192,384]{1,0:T(8,128)(2,1)S(1)} %add.150), channel_id=1, source_target_pairs={{0,8},{8,0},{16,24},{24,16},{1,9},{9,1},{17,25},{25,17},{2,10},{10... | collective-permute-start | bytes 442376 | tf_op jit(solution)/shard_map/ppermute | solution.py:608
  245.0 10.1 %collective-permute-start.53 = (bf16[192,384]{1,0:T(8,128)(2,1)S(1)}, bf16[192,384]{1,0:T(8,128)(2,1)S(1)}, u32[]{:S(2)}, u32[]{:S(2)}) collective-permute-start(bf16[192,384]{1,0:T(8,128)(2,1)S(1)} %get-tuple-element.260), channel_id=1, source_target_pairs={{0,8},{8,0},{16,24},{24,16},{1,9},{9,1},{17,25},{25,17},{2,10},{10... | collective-permute-start | bytes 442376 | tf_op jit(solution)/shard_map/ppermute | solution.py:608
  246.5 16.6 %collective-permute-start.55 = (bf16[400,384]{1,0:T(8,128)(2,1)S(1)}, bf16[400,384]{1,0:T(8,128)(2,1)S(1)}, u32[]{:S(2)}, u32[]{:S(2)}) collective-permute-start(bf16[400,384]{1,0:T(8,128)(2,1)S(1)} %get-tuple-element.250), channel_id=1, source_target_pairs={{0,8},{8,0},{16,24},{24,16},{1,9},{9,1},{17,25},{25,17},{2,10},{10... | collective-permute-start | bytes 921608 | tf_op jit(solution)/shard_map/ppermute | solution.py:608
  248.2 31.4 %collective-permute-start.59 = (bf16[192,512]{1,0:T(8,128)(2,1)S(1)}, bf16[192,512]{1,0:T(8,128)(2,1)S(1)}, u32[]{:S(2)}, u32[]{:S(2)}) collective-permute-start(bf16[192,512]{1,0:T(8,128)(2,1)S(1)} %get-tuple-element.228), channel_id=1, source_target_pairs={{0,2},{2,0},{4,6},{6,4},{1,3},{3,1},{5,7},{7,5},{8,10},{10,8},{12,... | collective-permute-start | bytes 589832 | tf_op jit(solution)/shard_map/ppermute | solution.py:608
  255.1 24.5 %collective-permute-start.60 = (bf16[192,512]{1,0:T(8,128)(2,1)S(1)}, bf16[192,512]{1,0:T(8,128)(2,1)S(1)}, u32[]{:S(2)}, u32[]{:S(2)}) collective-permute-start(bf16[192,512]{1,0:T(8,128)(2,1)S(1)} %get-tuple-element.230), channel_id=1, source_target_pairs={{0,4},{2,6},{4,0},{6,2},{1,5},{3,7},{5,1},{7,3},{8,12},{10,14},{12... | collective-permute-start | bytes 589832 | tf_op jit(solution)/shard_map/ppermute | solution.py:608
  255.1 12.0 %collective-permute-start.56 = (bf16[192,384]{1,0:T(8,128)(2,1)S(1)}, bf16[192,384]{1,0:T(8,128)(2,1)S(1)}, u32[]{:S(2)}, u32[]{:S(2)}) collective-permute-start(bf16[192,384]{1,0:T(8,128)(2,1)S(1)} %add.155), channel_id=1, source_target_pairs={{0,16},{8,24},{16,0},{24,8},{1,17},{9,25},{17,1},{25,9},{2,18},{10... | collective-permute-start | bytes 442376 | tf_op jit(solution)/shard_map/ppermute | solution.py:608
  257.0 10.1 %collective-permute-start.62 = (bf16[192,384]{1,0:T(8,128)(2,1)S(1)}, bf16[192,384]{1,0:T(8,128)(2,1)S(1)}, u32[]{:S(2)}, u32[]{:S(2)}) collective-permute-start(bf16[192,384]{1,0:T(8,128)(2,1)S(1)} %add.156), channel_id=1, source_target_pairs={{0,8},{8,0},{16,24},{24,16},{1,9},{9,1},{17,25},{25,17},{2,10},{10... | collective-permute-start | bytes 442376 | tf_op jit(solution)/shard_map/ppermute | solution.py:608
  263.2 12.1 %collective-permute-start.57 = (bf16[400,384]{1,0:T(8,128)(2,1)S(1)}, bf16[400,384]{1,0:T(8,128)(2,1)S(1)}, u32[]{:S(2)}, u32[]{:S(2)}) collective-permute-start(bf16[400,384]{1,0:T(8,128)(2,1)S(1)} %add.157), channel_id=1, source_target_pairs={{0,16},{8,24},{16,0},{24,8},{1,17},{9,25},{17,1},{25,9},{2,18},{10... | collective-permute-start | bytes 921608 | tf_op jit(solution)/shard_map/ppermute | solution.py:608
  267.1 12.5 %collective-permute-start.61 = (bf16[192,512]{1,0:T(8,128)(2,1)S(1)}, bf16[192,512]{1,0:T(8,128)(2,1)S(1)}, u32[]{:S(2)}, u32[]{:S(2)}) collective-permute-start(bf16[192,512]{1,0:T(8,128)(2,1)S(1)} %get-tuple-element.232), channel_id=1, source_target_pairs={{0,6},{2,4},{4,2},{6,0},{1,7},{3,5},{5,3},{7,1},{8,14},{10,12},{12... | collective-permute-start | bytes 589832 | tf_op jit(solution)/shard_map/ppermute | solution.py:608
  (109 other events, 718.4 us)

commit v4 on v3

--- a/solution.py
+++ b/solution.py
@@ -696,12 +696,12 @@
     near_a = (own_a, a_x, swap(own_a, "row", 1), swap(a_x, "row", 1))
     other_a = (a_y, a_far, swap(a_y, "row", 1), swap(a_far, "row", 1))
     count = reduce_small(jnp.sum(lengths).astype(f32).reshape(1, 1) + jnp.zeros((8, 128), f32), "dp")
-    own_b = narrow((after(w_out, own_a), w_up, w_down), 3, "narrow_b")
+    own_b = narrow((after(w_out, own_a, count), w_up, w_down), 3, "narrow_b")
     b_x = swap(after(own_b, a_x, ins_got[2], ins_got[3]), "row", 2)
     b_y = swap(after(own_b, a_far), "col", 1)
     length = lax.dynamic_index_in_dim(lengths, col, 0, False)
     keep = ((row * tokens + jnp.arange(tokens, dtype=jnp.int32)) < length).astype(f32)
-    keep = after(jnp.broadcast_to(keep[None, :], (8, tokens)), count)
+    keep = jnp.broadcast_to(keep[None, :], (8, tokens))
     scale = (2.0 * LOSS_SCALE) / (count * width)
 
     x, fq, fk, uq, uk, v, kv, vecs, up_bias_all = attention_in(

time: 290 us -> 289 us (level)
  waiting for transfers between devices: 98.5 us -> 93.4 us
  starting transfers between devices: 58.1 us -> 61.4 us
    ppermute x66, waiting for transfers between devices: 98.5 us -> 93.4 us  [swap(): return lax.ppermute(value, axis, [(s, s ^ mask) for s in range(size)])]
    ppermute x66, starting transfers between devices: 58.1 us -> 61.4 us  [swap(): return lax.ppermute(value, axis, [(s, s ^ mask) for s in range(size)])]
  transfers between devices with their start and end apart: 66 -> 66, of which waited for: 26 -> 27; matrix products, arithmetic and copies ran while one was open for 5% -> 5% of each run, Pallas kernels for 20% -> 20%
where the time goes in v4:
time: 289 us; the launch traced here: 287 us
  Pallas kernels  94.1 us (33%)
  waiting for transfers between devices  93.4 us (32%)
  starting transfers between devices  61.4 us (21%)
  local copies, waits for them, and re-layouts  19.6 us (7%)
  other arithmetic  14.2 us (5%)
  between operations  4.8 us (2%)
    pallas_call x22, Pallas kernels, call(): pl.pallas_call(body, out_shape=[make(s, d) for s, d in outs], scratch_sha...  94.1 us
    ppermute x66, waiting for transfers between devices, swap(): return lax.ppermute(value, axis, [(s, s ^ mask) for s in range(size)])  93.4 us
    ppermute x66, starting transfers between devices, swap(): return lax.ppermute(value, axis, [(s, s ^ mask) for s in range(size)])  61.4 us
    unnamed x182, local copies, waits for them, and re-layouts  13.9 us
  transfers between devices with their start and end apart: 66, of which 27 were waited for; matrix products, arithmetic and copies ran while one was open for 5% of the time, Pallas kernels for 20%

profile of v4, /device:TPU:0, one launch (start us, length us, event | category | flops | bytes accessed | tf_op | source)
XLA Modules:
  0.0 287.5 jit_solution(8282166153531271410)
XLA Ops:
  2.0 3.2 %split_positions.2 = (bf16[192,512]{1,0:T(8,128)(2,1)}, bf16[192,512]{1,0:T(8,128)(2,1)}, bf16[192,512]{1,0:T(8,128)(2,1)}, bf16[192,512]{1,0:T(8,128)(2,1)}) custom-call(s32[1]{0:T(128)} %bitcast.row_ref, f32[192,2048]{1,0:T(8,128)} %in_ref.1), custom_call_target="tpu_custom_call" | custom-call | flops 1000 | bytes 1000 | tf_op jit(solution)/shard_map/split_positions/pallas_call | solution.py:50
  5.2 2.1 narrow_a.1.refs_4_.refs_0_
  7.3 3.0 %collective-permute-start.6 = (bf16[208,1152]{1,0:T(8,128)(2,1)}, bf16[208,1152]{1,0:T(8,128)(2,1)S(1)}, u32[]{:S(2)}, u32[]{:S(2)}) collective-permute-start(bf16[208,1152]{1,0:T(8,128)(2,1)} %narrow_a.1.refs_4_.refs_0_), channel_id=1, source_target_pairs={{0,1},{1,0},{2,3},{3,2},{4,5},{5,4},{6,7},{7,6},{8,9},{9,8},{10,11... | collective-permute-start | bytes 1437704 | tf_op jit(solution)/shard_map/ppermute | solution.py:608
  16.7 2.6 collective-permute-start.14
  19.9 5.8 %collective-permute-done.7.refs_13_.om1_ref = bf16[6,64,256]{2,1,0:T(8,128)(2,1)S(1)} collective-permute-done((bf16[6,64,256]{2,1,0:T(8,128)(2,1)S(1)}, bf16[6,64,256]{2,1,0:T(8,128)(2,1)S(1)}, u32[]{:S(2)}, u32[]{:S(2)}) %collective-permute-start.7) | collective-permute-done | bytes 196640 | tf_op jit(solution)/shard_map/ppermute | solution.py:608
  29.6 3.6 %narrow_b.1.refs_4_.refs_14_.refs_24_.refs_0_ = bf16[192,3456]{1,0:T(8,128)(2,1)} custom-call(f32[192,384]{1,0:T(8,128)} %refs_0_.1, f32[192,1536]{1,0:T(8,128)} %refs_1_.3, f32[192,1536]{1,0:T(8,128)} %refs_2_.3), custom_call_target="tpu_custom_call" | custom-call | flops 1000 | bytes 1000 | tf_op jit(solution)/shard_map/narrow_b/pallas_call | solution.py:50
  35.4 5.3 %collective-permute-done.8.refs_9_.refs_5_ = bf16[208,1152]{1,0:T(8,128)(2,1)} collective-permute-done((bf16[208,1152]{1,0:T(8,128)(2,1)}, bf16[208,1152]{1,0:T(8,128)(2,1)}, u32[]{:S(2)}, u32[]{:S(2)}) %collective-permute-start.8) | collective-permute-done | bytes 479264 | tf_op jit(solution)/shard_map/ppermute | solution.py:608
  44.2 11.2 %attention_in.1 = (bf16[768,512]{1,0:T(8,128)(2,1)}, bf16[3072,512]{1,0:T(8,128)(2,1)}, bf16[3072,512]{1,0:T(8,128)(2,1)}, bf16[768,512]{1,0:T(8,128)(2,1)}, bf1...) custom-call(bf16[192,512]{1,0:T(8,128)(2,1)} %get-tuple-element.125., ...), custom_call_target="tpu_custom_call" | custom-call | flops 1000 | bytes 1000 | tf_op jit(solution)/shard_map/attention_in/pallas_call | solution.py:50
  55.6 1.8 collective-permute-done.11
  58.6 3.2 %split_positions.3 = (bf16[192,512]{1,0:T(8,128)(2,1)}, bf16[192,512]{1,0:T(8,128)(2,1)}, bf16[192,512]{1,0:T(8,128)(2,1)}, bf16[192,512]{1,0:T(8,128)(2,1)}) custom-call(s32[1]{0:T(128)} %bitcast.row_ref, f32[192,2048]{1,0:T(8,128)} %in_ref.2), custom_call_target="tpu_custom_call" | custom-call | flops 1000 | bytes 1000 | tf_op jit(solution)/shard_map/split_positions/pallas_call | solution.py:50
  61.8 2.5 collective-permute-done.15.refs_5_.refs_15_.refs_25_.refs_1_
  64.4 1.8 collective-permute-start.20
  66.5 1.8 collective-permute-start.21
  68.3 4.7 %collective-permute-done.18.refs_8_.refs_18_.refs_28_.refs_4_ = bf16[192,3456]{1,0:T(8,128)(2,1)S(1)} collective-permute-done((bf16[192,3456]{1,0:T(8,128)(2,1)}, bf16[192,3456]{1,0:T(8,128)(2,1)S(1)}, u32[]{:S(2)}, u32[]{:S(2)}) %collective-permute-start.18) | collective-permute-done | bytes 1327136 | tf_op jit(solution)/shard_map/ppermute | solution.py:608
  73.1 10.4 %collective-permute-done.21.refs_37_ = bf16[192,512]{1,0:T(8,128)(2,1)S(1)} collective-permute-done((bf16[192,512]{1,0:T(8,128)(2,1)S(1)}, bf16[192,512]{1,0:T(8,128)(2,1)S(1)}, u32[]{:S(2)}, u32[]{:S(2)}) %collective-permute-start.21) | collective-permute-done | bytes 196640 | tf_op jit(solution)/shard_map/ppermute | solution.py:608
  83.8 1.7 collective-permute-done.22.refs_39_
  85.5 2.3 collective-permute-start.17
  87.9 5.1 %collective-permute-done.19.refs_9_.refs_19_.refs_29_.refs_5_ = bf16[48,3456]{1,0:T(8,128)(2,1)S(1)} collective-permute-done((bf16[48,3456]{1,0:T(8,128)(2,1)S(1)}, bf16[48,3456]{1,0:T(8,128)(2,1)S(1)}, u32[]{:S(2)}, u32[]{:S(2)}) %collective-permute-start.19) | collective-permute-done | bytes 331808 | tf_op jit(solution)/shard_map/ppermute | solution.py:608
  94.4 2.7 collective-permute-done.26.refs_38_
  99.4 21.2 %middle.1 = (bf16[864,256]{1,0:T(8,128)(2,1)}, bf16[768,512]{1,0:T(8,128)(2,1)}, f32[16,512]{1,0:T(8,128)}, bf16[768,512]{1,0:T(8,128)(2,1)}, f32[8,512]{1,0:T(8...) custom-call(bf16[864,256]{1,0:T(8,128)(2,1)} %copy-done.73, ...), custom_call_target="tpu_custom_call" | custom-call | flops 1000 | bytes 1000 | tf_op jit(solution)/shard_map/middle/pallas_call | solution.py:50
  121.7 1.9 copy-done.24
  123.6 2.8 down_theirs.1
  130.3 7.6 %down_back.1 = (bf16[2,1536,512]{2,1,0:T(8,128)(2,1)}, f32[2,8,1536]{2,1,0:T(8,128)S(1)}, f32[8,768]{1,0:T(8,128)S(1)}) custom-call(bf16[768,512]{1,0:T(8,128)(2,1)S(1)} %copy-done.23, bf16[2,1536,512]{2,1,0:T(8,128)(2,1)} %get-tuple-element.152.slope_ref, bf16[192,3456]{1,0:T(8,128)(2,1)S(1)} %copy-done.1, bf16[192,3456]{1,0:T(8,128)(2,1)S(1)} %copy-done.3, ...), custom_call_target="tpu_custom_call" | custom-call | flops 1000 | bytes 1000 | tf_op jit(solution)/shard_map/down_back/pallas_call | solution.py:50
  138.0 4.1 %down_mine.1 = (bf16[384,768]{1,0:T(8,128)(2,1)S(1)}, bf16[384,768]{1,0:T(8,128)(2,1)S(1)}, bf16[384,768]{1,0:T(8,128)(2,1)S(1)}, bf16[384,768]{1,0:T(8,128)(2,1)}) custom-call(bf16[768,512]{1,0:T(8,128)(2,1)S(1)} %copy-done.23, bf16[2,1536,512]{2,1,0:T(8,128)(2,1)S(1)} %copy-done.24, bf16[2,384,1536]{2,1,0:T(8,128)(2,1)S(1)} %collective-permute-done.27.got_ref), custom_call_target="tpu_custom_call" | custom-call | flops 1000 | bytes 1000 | tf_op jit(solution)/shard_map/down_mine/pallas_call | solution.py:50
  145.6 6.7 %up_back.1 = (bf16[768,512]{1,0:T(8,128)(2,1)S(1)}, f32[24,768]{1,0:T(8,128)S(1)}) custom-call(bf16[2,1536,512]{2,1,0:T(8,128)(2,1)} %get-tuple-element.157.gu_ref.r_ref, bf16[768,512]{1,0:T(8,128)(2,1)S(1)} %copy-done.23, bf16[768,512]{1,0:T(8,128)(2,1)S(1)} %copy-done.41, f32[8,512]{1,0:T(8,128)S(1)} %copy-done.70, f32[8,768]{1,0:T(8,128)S(1)} %copy-done.66, ...), custom_call_target="tpu_custom_call" | custom-call | flops 1000 | bytes 1000 | tf_op jit(solution)/shard_map/up_back/pallas_call | solution.py:50
  152.9 3.7 %attention_mid.1 = (bf16[864,512]{1,0:T(8,128)(2,1)S(1)}, bf16[864,256]{1,0:T(8,128)(2,1)S(1)}) custom-call(bf16[768,512]{1,0:T(8,128)(2,1)S(1)} %get-tuple-element.209.go_ref, bf16[768,512]{1,0:T(8,128)(2,1)S(1)} %copy-done.29, f32[16,512]{1,0:T(8,128)S(1)} %copy-done.69, bf16[3072,512]{1,0:T(8,128)(2,1)} %get-tuple-element.132.refs_2_.fq_ref, ...), custom_call_target="tpu_custom_call" | custom-call | flops 1000 | bytes 1000 | tf_op jit(solution)/shard_map/attention_mid/pallas_call | solution.py:50
  158.0 2.8 up_theirs.1
  163.3 2.7 collective-permute-done.33
  166.9 2.8 query_back.1
  171.4 4.0 %up_mine.1 = (bf16[384,768]{1,0:T(8,128)(2,1)S(1)}, bf16[384,768]{1,0:T(8,128)(2,1)S(1)}, bf16[384,768]{1,0:T(8,128)(2,1)}, bf16[384,768]{1,0:T(8,128)(2,1)S(1)}) custom-call(bf16[768,512]{1,0:T(8,128)(2,1)S(1)} %copy-done.32, bf16[2,1536,512]{2,1,0:T(8,128)(2,1)S(1)} %copy-done.20, bf16[2,384,1536]{2,1,0:T(8,128)(2,1)S(1)} %collective-permute-done.34.got_ref), custom_call_target="tpu_custom_call" | custom-call | flops 1000 | bytes 1000 | tf_op jit(solution)/shard_map/up_mine/pallas_call | solution.py:50
  183.3 1.6 collective-permute-start.39
  186.0 6.3 %collective-permute-done.36.gkv1_ref = bf16[864,256]{1,0:T(8,128)(2,1)S(1)} collective-permute-done((bf16[864,256]{1,0:T(8,128)(2,1)}, bf16[864,256]{1,0:T(8,128)(2,1)S(1)}, u32[]{:S(2)}, u32[]{:S(2)}) %collective-permute-start.36) | collective-permute-done | bytes 442400 | tf_op jit(solution)/shard_map/ppermute | solution.py:608
  193.4 3.6 %key_back.1 = (bf16[1536,512]{1,0:T(8,128)(2,1)S(1)}, f32[8,1536]{1,0:T(8,128)S(1)}) custom-call(bf16[864,256]{1,0:T(8,128)(2,1)S(1)} %copy-done.40, bf16[864,256]{1,0:T(8,128)(2,1)S(1)} %collective-permute-done.36.gkv1_ref, bf16[3072,512]{1,0:T(8,128)(2,1)S(1)} %copy-done.33, bf16[768,512]{1,0:T(8,128)(2,1)S(1)} %copy-done.42, ...), custom_call_target="tpu_custom_call" | custom-call | flops 1000 | bytes 1000 | tf_op jit(solution)/shard_map/key_back/pallas_call | solution.py:50
  203.3 2.6 collective-permute-start.45
  206.9 3.1 %collective-permute-done.41 = bf16[192,768]{1,0:T(8,128)(2,1)S(1)} collective-permute-done((bf16[192,768]{1,0:T(8,128)(2,1)S(1)}, bf16[192,768]{1,0:T(8,128)(2,1)S(1)}, u32[]{:S(2)}, u32[]{:S(2)}) %collective-permute-start.41) | collective-permute-done | bytes 294944 | tf_op jit(solution)/shard_map/ppermute | solution.py:608
  215.4 3.2 %collective-permute-done.43 = bf16[384,768]{1,0:T(8,128)(2,1)S(1)} collective-permute-done((bf16[384,768]{1,0:T(8,128)(2,1)S(1)}, bf16[384,768]{1,0:T(8,128)(2,1)S(1)}, u32[]{:S(2)}, u32[]{:S(2)}) %collective-permute-start.43) | collective-permute-done | bytes 589856 | tf_op jit(solution)/shard_map/ppermute | solution.py:608
  220.9 2.6 collective-permute-start.50
  223.4 3.9 %input_grad.1 = (bf16[192,512]{1,0:T(8,128)(2,1)S(1)}, bf16[192,512]{1,0:T(8,128)(2,1)S(1)}, bf16[192,512]{1,0:T(8,128)(2,1)S(1)}, bf16[192,512]{1,0:T(8,128)(2,1)S(1)}) custom-call(bf16[2,384,512]{2,1,0:T(8,128)(2,1)S(1)} %bitcast.23, bf16[2,768,512]{2,1,0:T(8,128)(2,1)S(1)} %bitcast.20, bf16[768,512]{1,0:T(8,128)(2,1)S(1)} %get-tuple-element.209.go_ref, ...), custom_call_target="tpu_custom_call" | custom-call | flops 1000 | bytes 1000 | tf_op jit(solution)/shard_map/input_grad/pallas_call | solution.py:50
  232.0 6.0 %collective-permute-done.48 = bf16[192,768]{1,0:T(8,128)(2,1)S(1)} collective-permute-done((bf16[192,768]{1,0:T(8,128)(2,1)S(1)}, bf16[192,768]{1,0:T(8,128)(2,1)S(1)}, u32[]{:S(2)}, u32[]{:S(2)}) %collective-permute-start.48) | collective-permute-done | bytes 294944 | tf_op jit(solution)/shard_map/ppermute | solution.py:608
  239.1 2.7 collective-permute-start.54
  246.9 6.6 %collective-permute-done.53 = bf16[192,384]{1,0:T(8,128)(2,1)S(1)} collective-permute-done((bf16[192,384]{1,0:T(8,128)(2,1)S(1)}, bf16[192,384]{1,0:T(8,128)(2,1)S(1)}, u32[]{:S(2)}, u32[]{:S(2)}) %collective-permute-start.53) | collective-permute-done | bytes 147488 | tf_op jit(solution)/shard_map/ppermute | solution.py:608
  253.6 1.8 collective-permute-start.56
  257.1 4.5 %collective-permute-done.55 = bf16[400,384]{1,0:T(8,128)(2,1)S(1)} collective-permute-done((bf16[400,384]{1,0:T(8,128)(2,1)S(1)}, bf16[400,384]{1,0:T(8,128)(2,1)S(1)}, u32[]{:S(2)}, u32[]{:S(2)}) %collective-permute-start.55) | collective-permute-done | bytes 307232 | tf_op jit(solution)/shard_map/ppermute | solution.py:608
  262.9 2.3 collective-permute-done.56
  266.7 7.4 %collective-permute-done.57 = bf16[400,384]{1,0:T(8,128)(2,1)S(1)} collective-permute-done((bf16[400,384]{1,0:T(8,128)(2,1)S(1)}, bf16[400,384]{1,0:T(8,128)(2,1)S(1)}, u32[]{:S(2)}, u32[]{:S(2)}) %collective-permute-start.57) | collective-permute-done | bytes 307232 | tf_op jit(solution)/shard_map/ppermute | solution.py:608
  276.2 1.7 join_positions.2
  277.8 1.7 join_positions.3
  279.5 2.7 collective-permute-done.58
  (342 shorter events, 83.5 us)
Async XLA Ops:
  7.3 18.7 %collective-permute-start.6 = (bf16[208,1152]{1,0:T(8,128)(2,1)}, bf16[208,1152]{1,0:T(8,128)(2,1)S(1)}, u32[]{:S(2)}, u32[]{:S(2)}) collective-permute-start(bf16[208,1152]{1,0:T(8,128)(2,1)} %narrow_a.1.refs_4_.refs_0_), channel_id=1, source_target_pairs={{0,1},{1,0},{2,3},{3,2},{4,5},{5,4},{6,7},{7,6},{8,9},{9,8},{10,11... | collective-permute-start | bytes 1437704 | tf_op jit(solution)/shard_map/ppermute | solution.py:608
  10.3 17.2 %collective-permute-start.3 = (bf16[208,1152]{1,0:T(8,128)(2,1)}, bf16[208,1152]{1,0:T(8,128)(2,1)}, u32[]{:S(2)}, u32[]{:S(2)}) collective-permute-start(bf16[208,1152]{1,0:T(8,128)(2,1)} %narrow_a.1.refs_4_.refs_0_), channel_id=1, source_target_pairs={{0,4},{2,6},{4,0},{6,2},{1,5},{3,7},{5,1},{7,3},{8,12},{10,14},{12... | collective-permute-start | bytes 1437704 | tf_op jit(solution)/shard_map/ppermute | solution.py:608
  14.7 10.9 %collective-permute-start.7 = (bf16[6,64,256]{2,1,0:T(8,128)(2,1)S(1)}, bf16[6,64,256]{2,1,0:T(8,128)(2,1)S(1)}, u32[]{:S(2)}, u32[]{:S(2)}) collective-permute-start(bf16[6,64,256]{2,1,0:T(8,128)(2,1)S(1)} %copy-done.36), channel_id=1, source_target_pairs={{0,1},{1,0},{2,3},{3,2},{4,5},{5,4},{6,7},{7,6},{8,9},{9,8},{10,11... | collective-permute-start | bytes 589832 | tf_op jit(solution)/shard_map/ppermute | solution.py:608
  16.7 12.3 %collective-permute-start.14 = (f32[8,128]{1,0:T(8,128)S(1)}, f32[8,128]{1,0:T(8,128)S(1)}, u32[]{:S(2)}, u32[]{:S(2)}) collective-permute-start(f32[8,128]{1,0:T(8,128)S(1)} %broadcast_add_fusion), channel_id=1, source_target_pairs={{0,16},{8,24},{16,0},{24,8},{1,17},{9,25},{17,1},{25,9},{2,18},{10... | collective-permute-start | bytes 12296 | tf_op jit(solution)/shard_map/ppermute | solution.py:608
  19.3 13.9 %collective-permute-start = (bf16[192,512]{1,0:T(8,128)(2,1)S(1)}, bf16[192,512]{1,0:T(8,128)(2,1)S(1)}, u32[]{:S(2)}, u32[]{:S(2)}) collective-permute-start(bf16[192,512]{1,0:T(8,128)(2,1)S(1)} %copy-done.87), channel_id=1, source_target_pairs={{0,4},{2,6},{4,0},{6,2},{1,5},{3,7},{5,1},{7,3},{8,12},{10,14},{12... | collective-permute-start | bytes 589832 | tf_op jit(solution)/shard_map/ppermute | solution.py:608
  26.0 14.8 %collective-permute-start.4 = (bf16[208,1152]{1,0:T(8,128)(2,1)}, bf16[208,1152]{1,0:T(8,128)(2,1)}, u32[]{:S(2)}, u32[]{:S(2)}) collective-permute-start(bf16[208,1152]{1,0:T(8,128)(2,1)} %narrow_a.1.refs_4_.refs_0_), channel_id=1, source_target_pairs={{0,2},{2,0},{4,6},{6,4},{1,3},{3,1},{5,7},{7,5},{8,10},{10,8},{12,... | collective-permute-start | bytes 1437704 | tf_op jit(solution)/shard_map/ppermute | solution.py:608
  27.5 13.3 %collective-permute-start.8 = (bf16[208,1152]{1,0:T(8,128)(2,1)}, bf16[208,1152]{1,0:T(8,128)(2,1)}, u32[]{:S(2)}, u32[]{:S(2)}) collective-permute-start(bf16[208,1152]{1,0:T(8,128)(2,1)} %collective-permute-done.3.refs_5_.refs_1_), channel_id=1, source_target_pairs={{0,1},{1,0},{2,3},{3,2},{4,5},{5,4},{6,7},{7,6},{8,9},{9,8},{10,11... | collective-permute-start | bytes 1437704 | tf_op jit(solution)/shard_map/ppermute | solution.py:608
  33.3 31.1 %collective-permute-start.15 = (bf16[192,3456]{1,0:T(8,128)(2,1)}, bf16[192,3456]{1,0:T(8,128)(2,1)S(1)}, u32[]{:S(2)}, u32[]{:S(2)}) collective-permute-start(bf16[192,3456]{1,0:T(8,128)(2,1)} %narrow_b.1.refs_4_.refs_14_.refs_24_.refs_0_), channel_id=1, source_target_pairs={{0,4},{2,6},{4,0},{6,2},{1,5},{3,7},{5,1},{7,3},{8,12},{10,14},{12... | collective-permute-start | bytes 3981320 | tf_op jit(solution)/shard_map/ppermute | solution.py:608
  33.9 9.7 %collective-permute-start.9 = (bf16[208,1152]{1,0:T(8,128)(2,1)S(1)}, bf16[208,1152]{1,0:T(8,128)(2,1)}, u32[]{:S(2)}, u32[]{:S(2)}) collective-permute-start(bf16[208,1152]{1,0:T(8,128)(2,1)S(1)} %collective-permute-done.6.refs_8_.refs_4_), channel_id=1, source_target_pairs={{0,2},{2,0},{4,6},{6,4},{1,3},{3,1},{5,7},{7,5},{8,10},{10,8},{12,... | collective-permute-start | bytes 1437704 | tf_op jit(solution)/shard_map/ppermute | solution.py:608
  40.8 32.3 %collective-permute-start.18 = (bf16[192,3456]{1,0:T(8,128)(2,1)}, bf16[192,3456]{1,0:T(8,128)(2,1)S(1)}, u32[]{:S(2)}, u32[]{:S(2)}) collective-permute-start(bf16[192,3456]{1,0:T(8,128)(2,1)} %narrow_b.1.refs_4_.refs_14_.refs_24_.refs_0_), channel_id=1, source_target_pairs={{0,1},{1,0},{2,3},{3,2},{4,5},{5,4},{6,7},{7,6},{8,9},{9,8},{10,11... | collective-permute-start | bytes 3981320 | tf_op jit(solution)/shard_map/ppermute | solution.py:608
  64.4 29.4 %collective-permute-start.20 = (bf16[144,3456]{1,0:T(8,128)(2,1)S(1)}, bf16[144,3456]{1,0:T(8,128)(2,1)S(1)}, u32[]{:S(2)}, u32[]{:S(2)}) collective-permute-start(bf16[144,3456]{1,0:T(8,128)(2,1)S(1)} %slice.182), channel_id=1, source_target_pairs={{0,1},{1,0},{2,3},{3,2},{4,5},{5,4},{6,7},{7,6},{8,9},{9,8},{10,11... | collective-permute-start | bytes 2985992 | tf_op jit(solution)/shard_map/ppermute | solution.py:608
  66.2 21.6 %collective-permute-start.12 = (bf16[864,256]{1,0:T(8,128)(2,1)S(1)}, bf16[864,256]{1,0:T(8,128)(2,1)S(1)}, u32[]{:S(2)}, u32[]{:S(2)}) collective-permute-start(bf16[864,256]{1,0:T(8,128)(2,1)S(1)} %add.126.refs_0_), channel_id=1, source_target_pairs={{0,4},{2,6},{4,0},{6,2},{1,5},{3,7},{5,1},{7,3},{8,12},{10,14},{12... | collective-permute-start | bytes 1327112 | tf_op jit(solution)/shard_map/ppermute | solution.py:608
  66.5 27.9 %collective-permute-start.16 = (bf16[192,3456]{1,0:T(8,128)(2,1)S(1)}, bf16[192,3456]{1,0:T(8,128)(2,1)S(1)}, u32[]{:S(2)}, u32[]{:S(2)}) collective-permute-start(bf16[192,3456]{1,0:T(8,128)(2,1)S(1)} %copy-done), channel_id=1, source_target_pairs={{0,2},{2,0},{4,6},{6,4},{1,3},{3,1},{5,7},{7,5},{8,10},{10,8},{12,... | collective-permute-start | bytes 3981320 | tf_op jit(solution)/shard_map/ppermute | solution.py:608
  66.5 17.0 %collective-permute-start.21 = (bf16[192,512]{1,0:T(8,128)(2,1)S(1)}, bf16[192,512]{1,0:T(8,128)(2,1)S(1)}, u32[]{:S(2)}, u32[]{:S(2)}) collective-permute-start(bf16[192,512]{1,0:T(8,128)(2,1)S(1)} %copy-done.89), channel_id=1, source_target_pairs={{0,4},{2,6},{4,0},{6,2},{1,5},{3,7},{5,1},{7,3},{8,12},{10,14},{12... | collective-permute-start | bytes 589832 | tf_op jit(solution)/shard_map/ppermute | solution.py:608
  73.1 12.4 %collective-permute-start.22 = (bf16[192,512]{1,0:T(8,128)(2,1)S(1)}, bf16[192,512]{1,0:T(8,128)(2,1)S(1)}, u32[]{:S(2)}, u32[]{:S(2)}) collective-permute-start(bf16[192,512]{1,0:T(8,128)(2,1)S(1)} %copy-done.88), channel_id=1, source_target_pairs={{0,6},{2,4},{4,2},{6,0},{1,7},{3,5},{5,3},{7,1},{8,14},{10,12},{12... | collective-permute-start | bytes 589832 | tf_op jit(solution)/shard_map/ppermute | solution.py:608
  85.5 11.7 %collective-permute-start.17 = (bf16[192,3456]{1,0:T(8,128)(2,1)S(1)}, bf16[192,3456]{1,0:T(8,128)(2,1)S(1)}, u32[]{:S(2)}, u32[]{:S(2)}) collective-permute-start(bf16[192,3456]{1,0:T(8,128)(2,1)S(1)} %collective-permute-done.15.refs_5_.refs_15_.refs_25_.refs_1_), channel_id=1, source_target_pairs={{0,2},{2,0},{4,6},{6,4},{1,3},{3,1},{5,7},{7,5},{8,10},{10,8},{12,... | collective-permute-start | bytes 3981320 | tf_op jit(solution)/shard_map/ppermute | solution.py:608
  126.4 11.6 %collective-permute-start.27 = (bf16[2,384,1536]{2,1,0:T(8,128)(2,1)S(1)}, bf16[2,384,1536]{2,1,0:T(8,128)(2,1)S(1)}, u32[]{:S(2)}, u32[]{:S(2)}) collective-permute-start(bf16[2,384,1536]{2,1,0:T(8,128)(2,1)S(1)} %down_theirs.1), channel_id=1, source_target_pairs={{0,2},{2,0},{4,6},{6,4},{1,3},{3,1},{5,7},{7,5},{8,10},{10,8},{12,... | collective-permute-start | bytes 7077896 | tf_op jit(solution)/shard_map/ppermute | solution.py:608
  142.1 15.7 %collective-permute-start.31 = (bf16[384,768]{1,0:T(8,128)(2,1)S(1)}, bf16[384,768]{1,0:T(8,128)(2,1)S(1)}, u32[]{:S(2)}, u32[]{:S(2)}) collective-permute-start(bf16[384,768]{1,0:T(8,128)(2,1)S(1)} %get-tuple-element.156), channel_id=1, source_target_pairs={{0,1},{1,0},{2,3},{3,2},{4,5},{5,4},{6,7},{7,6},{8,9},{9,8},{10,11... | collective-permute-start | bytes 1769480 | tf_op jit(solution)/shard_map/ppermute | solution.py:608
  143.7 13.0 %collective-permute-start.28 = (bf16[192,512]{1,0:T(8,128)(2,1)S(1)}, bf16[192,512]{1,0:T(8,128)(2,1)S(1)}, u32[]{:S(2)}, u32[]{:S(2)}) collective-permute-start(bf16[192,512]{1,0:T(8,128)(2,1)S(1)} %copy-done.85), channel_id=1, source_target_pairs={{0,2},{2,0},{4,6},{6,4},{1,3},{3,1},{5,7},{7,5},{8,10},{10,8},{12,... | collective-permute-start | bytes 589832 | tf_op jit(solution)/shard_map/ppermute | solution.py:608
  143.8 12.9 %collective-permute-start.29 = (bf16[192,512]{1,0:T(8,128)(2,1)S(1)}, bf16[192,512]{1,0:T(8,128)(2,1)S(1)}, u32[]{:S(2)}, u32[]{:S(2)}) collective-permute-start(bf16[192,512]{1,0:T(8,128)(2,1)S(1)} %copy-done.83), channel_id=1, source_target_pairs={{0,4},{2,6},{4,0},{6,2},{1,5},{3,7},{5,1},{7,3},{8,12},{10,14},{12... | collective-permute-start | bytes 589832 | tf_op jit(solution)/shard_map/ppermute | solution.py:608
  144.3 12.4 %collective-permute-start.30 = (bf16[192,512]{1,0:T(8,128)(2,1)S(1)}, bf16[192,512]{1,0:T(8,128)(2,1)S(1)}, u32[]{:S(2)}, u32[]{:S(2)}) collective-permute-start(bf16[192,512]{1,0:T(8,128)(2,1)S(1)} %copy-done.82), channel_id=1, source_target_pairs={{0,6},{2,4},{4,2},{6,0},{1,7},{3,5},{5,3},{7,1},{8,14},{10,12},{12... | collective-permute-start | bytes 589832 | tf_op jit(solution)/shard_map/ppermute | solution.py:608
  160.8 10.6 %collective-permute-start.34 = (bf16[2,384,1536]{2,1,0:T(8,128)(2,1)S(1)}, bf16[2,384,1536]{2,1,0:T(8,128)(2,1)S(1)}, u32[]{:S(2)}, u32[]{:S(2)}) collective-permute-start(bf16[2,384,1536]{2,1,0:T(8,128)(2,1)S(1)} %up_theirs.1), channel_id=1, source_target_pairs={{0,2},{2,0},{4,6},{6,4},{1,3},{3,1},{5,7},{7,5},{8,10},{10,8},{12,... | collective-permute-start | bytes 7077896 | tf_op jit(solution)/shard_map/ppermute | solution.py:608
  161.9 17.6 %collective-permute-start.35 = (bf16[384,768]{1,0:T(8,128)(2,1)}, bf16[384,768]{1,0:T(8,128)(2,1)}, u32[]{:S(2)}, u32[]{:S(2)}) collective-permute-start(bf16[384,768]{1,0:T(8,128)(2,1)} %get-tuple-element.180), channel_id=1, source_target_pairs={{0,1},{1,0},{2,3},{3,2},{4,5},{5,4},{6,7},{7,6},{8,9},{9,8},{10,11... | collective-permute-start | bytes 1769480 | tf_op jit(solution)/shard_map/ppermute | solution.py:608
  177.9 19.2 %collective-permute-start.37 = (bf16[384,768]{1,0:T(8,128)(2,1)}, bf16[384,768]{1,0:T(8,128)(2,1)}, u32[]{:S(2)}, u32[]{:S(2)}) collective-permute-start(bf16[384,768]{1,0:T(8,128)(2,1)} %get-tuple-element.178), channel_id=1, source_target_pairs={{0,1},{1,0},{2,3},{3,2},{4,5},{5,4},{6,7},{7,6},{8,9},{9,8},{10,11... | collective-permute-start | bytes 1769480 | tf_op jit(solution)/shard_map/ppermute | solution.py:608
  179.0 13.3 %collective-permute-start.36 = (bf16[864,256]{1,0:T(8,128)(2,1)}, bf16[864,256]{1,0:T(8,128)(2,1)S(1)}, u32[]{:S(2)}, u32[]{:S(2)}) collective-permute-start(bf16[864,256]{1,0:T(8,128)(2,1)} %add.134.gkv0_ref), channel_id=1, source_target_pairs={{0,4},{2,6},{4,0},{6,2},{1,5},{3,7},{5,1},{7,3},{8,12},{10,14},{12... | collective-permute-start | bytes 1327112 | tf_op jit(solution)/shard_map/ppermute | solution.py:608
  180.6 17.5 %collective-permute-start.38 = (bf16[192,768]{1,0:T(8,128)(2,1)S(1)}, bf16[192,768]{1,0:T(8,128)(2,1)S(1)}, u32[]{:S(2)}, u32[]{:S(2)}) collective-permute-start(bf16[192,768]{1,0:T(8,128)(2,1)S(1)} %slice_add_fusion.9), channel_id=1, source_target_pairs={{0,4},{2,6},{4,0},{6,2},{1,5},{3,7},{5,1},{7,3},{8,12},{10,14},{12... | collective-permute-start | bytes 884744 | tf_op jit(solution)/shard_map/ppermute | solution.py:608
  183.3 15.9 %collective-permute-start.39 = (bf16[192,384]{1,0:T(8,128)(2,1)S(1)}, bf16[192,384]{1,0:T(8,128)(2,1)S(1)}, u32[]{:S(2)}, u32[]{:S(2)}) collective-permute-start(bf16[192,384]{1,0:T(8,128)(2,1)S(1)} %get-tuple-element.264), channel_id=1, source_target_pairs={{0,8},{8,0},{16,24},{24,16},{1,9},{9,1},{17,25},{25,17},{2,10},{10... | collective-permute-start | bytes 442376 | tf_op jit(solution)/shard_map/ppermute | solution.py:608
  185.9 20.0 %collective-permute-start.40 = (bf16[2,384,768]{2,1,0:T(8,128)(2,1)S(1)}, bf16[2,384,768]{2,1,0:T(8,128)(2,1)S(1)}, u32[]{:S(2)}, u32[]{:S(2)}) collective-permute-start(bf16[2,384,768]{2,1,0:T(8,128)(2,1)S(1)} %pair_theirs.1), channel_id=1, source_target_pairs={{0,2},{2,0},{4,6},{6,4},{1,3},{3,1},{5,7},{7,5},{8,10},{10,8},{12,... | collective-permute-start | bytes 3538952 | tf_op jit(solution)/shard_map/ppermute | solution.py:608
  200.5 10.5 %collective-permute-start.42 = (bf16[2,2,208,768]{3,2,1,0:T(8,128)(2,1)S(1)}, bf16[2,2,208,768]{3,2,1,0:T(8,128)(2,1)S(1)}, u32[]{:S(2)}, u32[]{:S(2)}) collective-permute-start(bf16[2,2,208,768]{3,2,1,0:T(8,128)(2,1)S(1)} %last_theirs.1), channel_id=1, source_target_pairs={{0,2},{2,0},{4,6},{6,4},{1,3},{3,1},{5,7},{7,5},{8,10},{10,8},{12,... | collective-permute-start | bytes 3833864 | tf_op jit(solution)/shard_map/ppermute | solution.py:608
  202.3 16.3 %collective-permute-start.43 = (bf16[384,768]{1,0:T(8,128)(2,1)S(1)}, bf16[384,768]{1,0:T(8,128)(2,1)S(1)}, u32[]{:S(2)}, u32[]{:S(2)}) collective-permute-start(bf16[384,768]{1,0:T(8,128)(2,1)S(1)} %copy-done.72), channel_id=1, source_target_pairs={{0,1},{1,0},{2,3},{3,2},{4,5},{5,4},{6,7},{7,6},{8,9},{9,8},{10,11... | collective-permute-start | bytes 1769480 | tf_op jit(solution)/shard_map/ppermute | solution.py:608
  203.3 16.9 %collective-permute-start.45 = (bf16[192,384]{1,0:T(8,128)(2,1)S(1)}, bf16[192,384]{1,0:T(8,128)(2,1)S(1)}, u32[]{:S(2)}, u32[]{:S(2)}) collective-permute-start(bf16[192,384]{1,0:T(8,128)(2,1)S(1)} %add.139), channel_id=1, source_target_pairs={{0,16},{8,24},{16,0},{24,8},{1,17},{9,25},{17,1},{25,9},{2,18},{10... | collective-permute-start | bytes 442376 | tf_op jit(solution)/shard_map/ppermute | solution.py:608
  212.2 15.9 %collective-permute-start.46 = (bf16[416,768]{1,0:T(8,128)(2,1)S(1)}, bf16[416,768]{1,0:T(8,128)(2,1)S(1)}, u32[]{:S(2)}, u32[]{:S(2)}) collective-permute-start(bf16[416,768]{1,0:T(8,128)(2,1)S(1)} %get-tuple-element.203), channel_id=1, source_target_pairs={{0,4},{2,6},{4,0},{6,2},{1,5},{3,7},{5,1},{7,3},{8,12},{10,14},{12... | collective-permute-start | bytes 1916936 | tf_op jit(solution)/shard_map/ppermute | solution.py:608
  214.5 16.0 %collective-permute-start.47 = (bf16[384,768]{1,0:T(8,128)(2,1)S(1)}, bf16[384,768]{1,0:T(8,128)(2,1)S(1)}, u32[]{:S(2)}, u32[]{:S(2)}) collective-permute-start(bf16[384,768]{1,0:T(8,128)(2,1)S(1)} %get-tuple-element.198), channel_id=1, source_target_pairs={{0,1},{1,0},{2,3},{3,2},{4,5},{5,4},{6,7},{7,6},{8,9},{9,8},{10,11... | collective-permute-start | bytes 1769480 | tf_op jit(solution)/shard_map/ppermute | solution.py:608
  218.6 20.4 %collective-permute-start.49 = (bf16[192,384]{1,0:T(8,128)(2,1)S(1)}, bf16[192,384]{1,0:T(8,128)(2,1)S(1)}, u32[]{:S(2)}, u32[]{:S(2)}) collective-permute-start(bf16[192,384]{1,0:T(8,128)(2,1)S(1)} %get-tuple-element.260), channel_id=1, source_target_pairs={{0,8},{8,0},{16,24},{24,16},{1,9},{9,1},{17,25},{25,17},{2,10},{10... | collective-permute-start | bytes 442376 | tf_op jit(solution)/shard_map/ppermute | solution.py:608
  220.3 26.5 %collective-permute-start.64 = (bf16[192,384]{1,0:T(8,128)(2,1)S(1)}, bf16[192,384]{1,0:T(8,128)(2,1)S(1)}, u32[]{:S(2)}, u32[]{:S(2)}) collective-permute-start(bf16[192,384]{1,0:T(8,128)(2,1)S(1)} %add.144), channel_id=1, source_target_pairs={{0,8},{8,0},{16,24},{24,16},{1,9},{9,1},{17,25},{25,17},{2,10},{10... | collective-permute-start | bytes 442376 | tf_op jit(solution)/shard_map/ppermute | solution.py:608
  220.9 20.9 %collective-permute-start.50 = (bf16[192,384]{1,0:T(8,128)(2,1)S(1)}, bf16[192,384]{1,0:T(8,128)(2,1)S(1)}, u32[]{:S(2)}, u32[]{:S(2)}) collective-permute-start(bf16[192,384]{1,0:T(8,128)(2,1)S(1)} %add.143), channel_id=1, source_target_pairs={{0,16},{8,24},{16,0},{24,8},{1,17},{9,25},{17,1},{25,9},{2,18},{10... | collective-permute-start | bytes 442376 | tf_op jit(solution)/shard_map/ppermute | solution.py:608
  228.1 9.9 %collective-permute-start.48 = (bf16[192,768]{1,0:T(8,128)(2,1)S(1)}, bf16[192,768]{1,0:T(8,128)(2,1)S(1)}, u32[]{:S(2)}, u32[]{:S(2)}) collective-permute-start(bf16[192,768]{1,0:T(8,128)(2,1)S(1)} %slice_add_fusion.5), channel_id=1, source_target_pairs={{0,4},{2,6},{4,0},{6,2},{1,5},{3,7},{5,1},{7,3},{8,12},{10,14},{12... | collective-permute-start | bytes 884744 | tf_op jit(solution)/shard_map/ppermute | solution.py:608
  230.5 13.0 %collective-permute-start.52 = (bf16[192,768]{1,0:T(8,128)(2,1)S(1)}, bf16[192,768]{1,0:T(8,128)(2,1)S(1)}, u32[]{:S(2)}, u32[]{:S(2)}) collective-permute-start(bf16[192,768]{1,0:T(8,128)(2,1)S(1)} %slice_add_fusion.4), channel_id=1, source_target_pairs={{0,4},{2,6},{4,0},{6,2},{1,5},{3,7},{5,1},{7,3},{8,12},{10,14},{12... | collective-permute-start | bytes 884744 | tf_op jit(solution)/shard_map/ppermute | solution.py:608
  239.1 14.5 %collective-permute-start.54 = (bf16[192,384]{1,0:T(8,128)(2,1)S(1)}, bf16[192,384]{1,0:T(8,128)(2,1)S(1)}, u32[]{:S(2)}, u32[]{:S(2)}) collective-permute-start(bf16[192,384]{1,0:T(8,128)(2,1)S(1)} %add.149), channel_id=1, source_target_pairs={{0,16},{8,24},{16,0},{24,8},{1,17},{9,25},{17,1},{25,9},{2,18},{10... | collective-permute-start | bytes 442376 | tf_op jit(solution)/shard_map/ppermute | solution.py:608
  241.8 13.7 %collective-permute-start.65 = (bf16[192,384]{1,0:T(8,128)(2,1)S(1)}, bf16[192,384]{1,0:T(8,128)(2,1)S(1)}, u32[]{:S(2)}, u32[]{:S(2)}) collective-permute-start(bf16[192,384]{1,0:T(8,128)(2,1)S(1)} %add.150), channel_id=1, source_target_pairs={{0,8},{8,0},{16,24},{24,16},{1,9},{9,1},{17,25},{25,17},{2,10},{10... | collective-permute-start | bytes 442376 | tf_op jit(solution)/shard_map/ppermute | solution.py:608
  243.4 10.1 %collective-permute-start.53 = (bf16[192,384]{1,0:T(8,128)(2,1)S(1)}, bf16[192,384]{1,0:T(8,128)(2,1)S(1)}, u32[]{:S(2)}, u32[]{:S(2)}) collective-permute-start(bf16[192,384]{1,0:T(8,128)(2,1)S(1)} %get-tuple-element.258), channel_id=1, source_target_pairs={{0,8},{8,0},{16,24},{24,16},{1,9},{9,1},{17,25},{25,17},{2,10},{10... | collective-permute-start | bytes 442376 | tf_op jit(solution)/shard_map/ppermute | solution.py:608
  245.2 16.4 %collective-permute-start.55 = (bf16[400,384]{1,0:T(8,128)(2,1)S(1)}, bf16[400,384]{1,0:T(8,128)(2,1)S(1)}, u32[]{:S(2)}, u32[]{:S(2)}) collective-permute-start(bf16[400,384]{1,0:T(8,128)(2,1)S(1)} %get-tuple-element.248), channel_id=1, source_target_pairs={{0,8},{8,0},{16,24},{24,16},{1,9},{9,1},{17,25},{25,17},{2,10},{10... | collective-permute-start | bytes 921608 | tf_op jit(solution)/shard_map/ppermute | solution.py:608
  246.9 31.0 %collective-permute-start.59 = (bf16[192,512]{1,0:T(8,128)(2,1)S(1)}, bf16[192,512]{1,0:T(8,128)(2,1)S(1)}, u32[]{:S(2)}, u32[]{:S(2)}) collective-permute-start(bf16[192,512]{1,0:T(8,128)(2,1)S(1)} %get-tuple-element.226), channel_id=1, source_target_pairs={{0,2},{2,0},{4,6},{6,4},{1,3},{3,1},{5,7},{7,5},{8,10},{10,8},{12,... | collective-permute-start | bytes 589832 | tf_op jit(solution)/shard_map/ppermute | solution.py:608
  253.5 24.3 %collective-permute-start.60 = (bf16[192,512]{1,0:T(8,128)(2,1)S(1)}, bf16[192,512]{1,0:T(8,128)(2,1)S(1)}, u32[]{:S(2)}, u32[]{:S(2)}) collective-permute-start(bf16[192,512]{1,0:T(8,128)(2,1)S(1)} %get-tuple-element.228), channel_id=1, source_target_pairs={{0,4},{2,6},{4,0},{6,2},{1,5},{3,7},{5,1},{7,3},{8,12},{10,14},{12... | collective-permute-start | bytes 589832 | tf_op jit(solution)/shard_map/ppermute | solution.py:608
  253.6 11.6 %collective-permute-start.56 = (bf16[192,384]{1,0:T(8,128)(2,1)S(1)}, bf16[192,384]{1,0:T(8,128)(2,1)S(1)}, u32[]{:S(2)}, u32[]{:S(2)}) collective-permute-start(bf16[192,384]{1,0:T(8,128)(2,1)S(1)} %add.155), channel_id=1, source_target_pairs={{0,16},{8,24},{16,0},{24,8},{1,17},{9,25},{17,1},{25,9},{2,18},{10... | collective-permute-start | bytes 442376 | tf_op jit(solution)/shard_map/ppermute | solution.py:608
  255.5 9.8 %collective-permute-start.62 = (bf16[192,384]{1,0:T(8,128)(2,1)S(1)}, bf16[192,384]{1,0:T(8,128)(2,1)S(1)}, u32[]{:S(2)}, u32[]{:S(2)}) collective-permute-start(bf16[192,384]{1,0:T(8,128)(2,1)S(1)} %add.156), channel_id=1, source_target_pairs={{0,8},{8,0},{16,24},{24,16},{1,9},{9,1},{17,25},{25,17},{2,10},{10... | collective-permute-start | bytes 442376 | tf_op jit(solution)/shard_map/ppermute | solution.py:608
  261.7 12.4 %collective-permute-start.57 = (bf16[400,384]{1,0:T(8,128)(2,1)S(1)}, bf16[400,384]{1,0:T(8,128)(2,1)S(1)}, u32[]{:S(2)}, u32[]{:S(2)}) collective-permute-start(bf16[400,384]{1,0:T(8,128)(2,1)S(1)} %add.157), channel_id=1, source_target_pairs={{0,16},{8,24},{16,0},{24,8},{1,17},{9,25},{17,1},{25,9},{2,18},{10... | collective-permute-start | bytes 921608 | tf_op jit(solution)/shard_map/ppermute | solution.py:608
  265.2 12.6 %collective-permute-start.61 = (bf16[192,512]{1,0:T(8,128)(2,1)S(1)}, bf16[192,512]{1,0:T(8,128)(2,1)S(1)}, u32[]{:S(2)}, u32[]{:S(2)}) collective-permute-start(bf16[192,512]{1,0:T(8,128)(2,1)S(1)} %get-tuple-element.230), channel_id=1, source_target_pairs={{0,6},{2,4},{4,2},{6,0},{1,7},{3,5},{5,3},{7,1},{8,14},{10,12},{12... | collective-permute-start | bytes 589832 | tf_op jit(solution)/shard_map/ppermute | solution.py:608
  (109 other events, 699.5 us)
